TPU v7x, 256 devices: a whole 4x4x8 slice. The times are simulated.
256 devices in a mesh: blk: 256 (over z, x, y, core).
Axes of the slice: x: 4, y: 4, z: 8, core: 2. Of those that a mesh axis runs over, the one named last changes fastest.
Arguments:
- features: float32 [65536, 128], P('blk'), may hold values from -6 to 6
- weight_one: float32 [128, 128], replicated, may hold values from -0.5 to 0.5
- weight_two: float32 [128, 128], replicated, may hold values from -0.5 to 0.5
- dense_tiles: bfloat16 [65536, 128, 128], P('blk'), may hold values from -0.0390625 to 0.0390625
- dense_row: int32 [65536], P('blk'), may hold values from 0 to 1
- hub_block: int32 [256], replicated, may hold values from 0 to 1
- sparse_tiles: bfloat16 [28672, 128, 128], P('blk'), may hold values from -0.0390625 to 0.0390625
- sparse_row: int32 [28672], P('blk'), may hold values from 0 to 1
- sparse_src: int32 [28672], P('blk'), may hold values from 0 to 5
- sparse_count: int32 [256], P('blk'), may hold values from 1 to 112, as said below
- fetch_list: int32 [256, 4], P('blk'), may hold values from 0 to 1
Outputs:
- embedded: float32 [65536, 128], P('blk')
Inputs may be any that keep to these rules, and one draw needn't show every extreme that they name: `sparse_count`: one device has exactly 112 live slots.
All inputs are finite; a program needn't handle non-finite values.
Results may differ from a plain program's by a relative error of at most 0.0041.
Values may be sent and summed in bfloat16 or wider, within the bound.
No kernel may reach another device: no remote copies, remote signals or barrier semaphores. Data moves between devices by JAX's collectives and lax.ppermute only.
A program may use at most 128 MiB of HBM per device.

v0:
```python
import jax
import jax.numpy as jnp
from jax import lax
from jax.sharding import PartitionSpec as P

F = 128
TILE = 128
NB = 2
KS = 112
HOPS = 2
FETCH = 1


def from_behind(shard, axis, by):
    size = lax.axis_size(axis)
    return lax.ppermute(shard, axis, [(i, (i + by) % size) for i in range(size)])


def neighbour_offsets():
    return list(range(-HOPS, 0)) + list(range(1, HOPS + 1))


def accumulate(running, tile_set, row_ids, inputs, slot_mask):
    products = jnp.einsum("sij,sjf->sif", tile_set, inputs, preferred_element_type=jnp.float32)
    block_ids = jnp.arange(running.shape[0], dtype=jnp.int32)
    onehot = (row_ids[:, None] == block_ids[None, :]).astype(jnp.float32) * slot_mask[:, None]
    return running + jnp.einsum("sn,sif->nif", onehot, products, precision=lax.Precision.HIGHEST)


def shards(
    features,
    weight_one,
    weight_two,
    dense_tiles,
    dense_row,
    hub_block,
    sparse_tiles,
    sparse_row,
    sparse_src,
    sparse_count,
    fetch_list,
):
    own_index = lax.axis_index("blk")
    offsets = neighbour_offsets()
    wanted_lists = [fetch_list[0, entry * FETCH : (entry + 1) * FETCH] for entry in range(2 * HOPS)]

    def propagate(hidden_rows, weight):
        blocks = hidden_rows.reshape(NB, TILE, F)
        zero_sums = jnp.zeros((NB, TILE, F), jnp.float32)
        hub_here = lax.dynamic_index_in_dim(hub_block, own_index, 0, keepdims=False)
        hub_rows = lax.dynamic_index_in_dim(blocks, hub_here, 0, keepdims=False)
        stripe = lax.all_gather(hub_rows, "blk", axis=0, tiled=True)
        shard_total = stripe.shape[0] // TILE
        summed = accumulate(
            zero_sums,
            dense_tiles,
            dense_row,
            stripe.reshape(shard_total, TILE, F),
            jnp.ones((shard_total,), jnp.float32),
        )
        fetched = [
            from_behind(blocks, "blk", -offsets[entry])[wanted_lists[entry]]
            for entry in range(2 * HOPS)
        ]
        gathered_blocks = jnp.concatenate([blocks] + fetched, axis=0)
        live_total = sparse_count[0]
        live_mask = (jnp.arange(KS, dtype=jnp.int32) < live_total).astype(jnp.float32)
        summed = accumulate(
            summed, sparse_tiles, sparse_row, gathered_blocks[sparse_src], live_mask
        )
        projected = jnp.dot(
            summed.reshape(NB * TILE, F),
            weight,
            precision=lax.Precision.HIGHEST,
            preferred_element_type=jnp.float32,
        )
        return jax.nn.relu(projected)

    hidden = propagate(features.astype(jnp.bfloat16), weight_one).astype(jnp.bfloat16)
    return propagate(hidden, weight_two)


def solution(mesh):
    placed = (
        P("blk", None),
        P(),
        P(),
        P("blk", None, None),
        P("blk"),
        P(),
        P("blk", None, None),
        P("blk"),
        P("blk"),
        P("blk"),
        P("blk", None),
    )
    return jax.shard_map(
        shards, mesh=mesh, in_specs=placed, out_specs=P("blk", None), check_vma=False
    )
```

profile of v0, /device:TPU:1, one launch (start us, length us, event | category | flops | bytes accessed | tf_op | source)
XLA Modules:
  0.0 343.1 jit_solution(18267663183371844)
XLA Ops:
  7.5 1.3 dynamic_slice.12
  11.4 2.2 collective-permute-start
  13.6 2.1 collective-permute-start.1
  15.7 7.6 %collective-permute-start.3 = (bf16[2,128,128]{2,1,0:T(8,128)(2,1)S(1)}, bf16[2,128,128]{2,1,0:T(8,128)(2,1)S(1)}, u32[]{:S(2)}, u32[]{:S(2)}) collective-permute-start(bf16[2,128,128]{2,1,0:T(8,128)(2,1)S(1)} %bitcast.62), channel_id=1, source_target_pairs={{0,254},{1,255},{2,0},{3,1},{4,2},{5,3},{6,4},{7,5},{8,6},{9,7},{1... | collective-permute-start | bytes 196616 | tf_op jit(solution)/shard_map/ppermute | solution.py:16
  23.4 1.5 fusion.30
  33.6 2.9 gather_fusion
  36.5 8.9 %fusion.32 = f32[112,128,128]{2,1,0:T(8,128)} fusion(bf16[112,128,128]{2,1,0:T(8,128)(2,1)} %gather_fusion, bf16[112,128,128]{2,1,0:T(8,128)(2,1)} %param.17), kind=kOutput, calls=%fused_computation.47 | convolution fusion | flops 469762048 | bytes 14680064 | tf_op jit(solution)/shard_map/sij,sjf->sif/dot_general | solution.py:24
  45.3 8.4 %copy.15 = f32[112,128,128]{1,0,2:T(8,128)} copy(f32[112,128,128]{2,1,0:T(8,128)} %fusion.32) | data formatting | bytes 14680064 | tf_op jit(solution)/shard_map/sij,sjf->sif/dot_general | solution.py:24
  53.7 79.8 %all-gather.5.cloned.1.call-done = bf16[1,32768,128]{2,1,0:T(8,128)(2,1)} async-done(((bf16[1,128,128]{2,1,0:T(8,128)(2,1)}), bf16[1,32768,128]{2,1,0:T(8,128)(2,1)}) %all-gather.5.cloned.1.call-update) | async-done | bytes 8388624 | tf_op jit(solution)/shard_map/all_gather | solution.py:52
  133.5 12.8 %fusion.31 = f32[256,128,128]{2,1,0:T(8,128)} fusion(bf16[256,128,128]{2,1,0:T(8,128)(2,1)} %bitcast.54, bf16[256,128,128]{2,1,0:T(8,128)(2,1)} %param.14), kind=kOutput, calls=%fused_computation.46 | convolution fusion | flops 1073741824 | bytes 33554432 | tf_op jit(solution)/shard_map/sij,sjf->sif/dot_general | solution.py:24
  146.4 17.5 %copy.14 = f32[256,128,128]{1,0,2:T(8,128)} copy(f32[256,128,128]{2,1,0:T(8,128)} %fusion.31) | data formatting | bytes 33554432 | tf_op jit(solution)/shard_map/sij,sjf->sif/dot_general | solution.py:24
  163.9 9.0 %fusion.2 = f32[2,128,128]{2,0,1:T(2,128)S(1)} fusion(f32[256,128,128]{1,0,2:T(8,128)} %copy.14, s32[256]{0:T(256)S(1)} %copy-done.5), kind=kOutput, calls=%fused_computation.4 | convolution fusion | flops 100663808 | bytes 16909312 | tf_op jit(solution)/shard_map/sn,sif->nif/dot_general | solution.py:27
  172.9 3.5 %fusion.8 = f32[2,128,128]{2,0,1:T(2,128)S(1)} fusion(f32[2,128,128]{2,0,1:T(2,128)S(1)} %fusion.2, f32[112,128,128]{1,0,2:T(8,128)S(1)} %copy-done.3, f32[112]{0:T(128)S(1)} %compare_convert_fusion, s32[112]{0:T(128)S(1)} %copy-done.6), kind=kOutput, calls=%fused_computation.10 | convolution fusion | flops 44073408 | bytes 7603072 | tf_op jit(solution)/shard_map/sn,sif->nif/dot_general | solution.py:27
  177.4 1.3 collective-permute-start.4
  178.7 1.7 collective-permute-start.5
  180.4 5.7 %collective-permute-start.7 = (bf16[2,128,128]{2,1,0:T(8,128)(2,1)S(1)}, bf16[2,128,128]{2,1,0:T(8,128)(2,1)S(1)}, u32[]{:S(2)}, u32[]{:S(2)}) collective-permute-start(bf16[2,128,128]{2,1,0:T(8,128)(2,1)S(1)} %bitcast.68), channel_id=1, source_target_pairs={{0,254},{1,255},{2,0},{3,1},{4,2},{5,3},{6,4},{7,5},{8,6},{9,7},{1... | collective-permute-start | bytes 196616 | tf_op jit(solution)/shard_map/ppermute | solution.py:16
  187.4 2.8 gather_fusion.1
  190.2 8.9 %fusion.34 = f32[112,128,128]{2,1,0:T(8,128)} fusion(bf16[112,128,128]{2,1,0:T(8,128)(2,1)} %gather_fusion.1, bf16[112,128,128]{2,1,0:T(8,128)(2,1)} %param.17), kind=kOutput, calls=%fused_computation.49 | convolution fusion | flops 469762048 | bytes 14680064 | tf_op jit(solution)/shard_map/sij,sjf->sif/dot_general | solution.py:24
  199.1 8.4 %copy.17 = f32[112,128,128]{1,0,2:T(8,128)} copy(f32[112,128,128]{2,1,0:T(8,128)} %fusion.34) | data formatting | bytes 14680064 | tf_op jit(solution)/shard_map/sij,sjf->sif/dot_general | solution.py:24
  207.5 84.9 %all-gather.7.cloned.1.call-done = bf16[1,32768,128]{2,1,0:T(8,128)(2,1)} async-done(((bf16[1,128,128]{2,1,0:T(8,128)(2,1)}), bf16[1,32768,128]{2,1,0:T(8,128)(2,1)}) %all-gather.7.cloned.1.call-update) | async-done | bytes 8388624 | tf_op jit(solution)/shard_map/all_gather | solution.py:52
  292.4 12.8 %fusion.33 = f32[256,128,128]{2,1,0:T(8,128)} fusion(bf16[256,128,128]{2,1,0:T(8,128)(2,1)} %bitcast.55, bf16[256,128,128]{2,1,0:T(8,128)(2,1)} %param.14), kind=kOutput, calls=%fused_computation.48 | convolution fusion | flops 1073741824 | bytes 33554432 | tf_op jit(solution)/shard_map/sij,sjf->sif/dot_general | solution.py:24
  305.3 17.5 %copy.16 = f32[256,128,128]{1,0,2:T(8,128)} copy(f32[256,128,128]{2,1,0:T(8,128)} %fusion.33) | data formatting | bytes 33554432 | tf_op jit(solution)/shard_map/sij,sjf->sif/dot_general | solution.py:24
  322.8 9.0 %fusion = f32[2,128,128]{2,0,1:T(2,128)S(1)} fusion(f32[256,128,128]{1,0,2:T(8,128)} %copy.16, s32[256]{0:T(256)S(1)} %copy-done.5), kind=kOutput, calls=%fused_computation.2 | convolution fusion | flops 100663808 | bytes 16909312 | tf_op jit(solution)/shard_map/sn,sif->nif/dot_general | solution.py:27
  331.8 3.5 %fusion.11 = f32[2,128,128]{2,0,1:T(2,128)S(1)} fusion(f32[2,128,128]{2,0,1:T(2,128)S(1)} %fusion, f32[112,128,128]{1,0,2:T(8,128)S(1)} %copy-done.2, f32[112]{0:T(128)S(1)} %compare_convert_fusion, s32[112]{0:T(128)S(1)} %copy-done.6), kind=kOutput, calls=%fused_computation.11 | convolution fusion | flops 44073408 | bytes 7603072 | tf_op jit(solution)/shard_map/sn,sif->nif/dot_general | solution.py:27
  (48 shorter events, 5.6 us)
Async XLA Ops:
  6.5 170.0 %copy-start = (f32[128,128]{1,0:T(8,128)S(1)}, f32[128,128]{1,0:T(8,128)}, u32[]{:S(2)}) copy-start(f32[128,128]{1,0:T(8,128)} %param.12) | copy-start | bytes 196612
  6.5 127.0 %all-gather.5.cloned.1.call-start = ((), (), s32[]{:S(2)}) async-start(), calls=%async_computation | async-start | bytes 8421376 | tf_op jit(solution)/shard_map/all_gather | solution.py:52
  11.3 281.1 %all-gather.7.cloned.1.call-start = ((), (), s32[]{:S(2)}) async-start(), calls=%async_computation.1 | async-start | bytes 8421376 | tf_op jit(solution)/shard_map/all_gather | solution.py:52
  11.4 22.1 %collective-permute-start = (bf16[2,128,128]{2,1,0:T(8,128)(2,1)S(1)}, bf16[2,128,128]{2,1,0:T(8,128)(2,1)S(1)}, u32[]{:S(2)}, u32[]{:S(2)}) collective-permute-start(bf16[2,128,128]{2,1,0:T(8,128)(2,1)S(1)} %bitcast.59), channel_id=1, source_target_pairs={{0,2},{1,3},{2,4},{3,5},{4,6},{5,7},{6,8},{7,9},{8,10},{9,11},{10,... | collective-permute-start | bytes 196616 | tf_op jit(solution)/shard_map/ppermute | solution.py:16
  13.6 19.9 %collective-permute-start.1 = (bf16[2,128,128]{2,1,0:T(8,128)(2,1)S(1)}, bf16[2,128,128]{2,1,0:T(8,128)(2,1)S(1)}, u32[]{:S(2)}, u32[]{:S(2)}) collective-permute-start(bf16[2,128,128]{2,1,0:T(8,128)(2,1)S(1)} %bitcast.60), channel_id=1, source_target_pairs={{0,1},{1,2},{2,3},{3,4},{4,5},{5,6},{6,7},{7,8},{8,9},{9,10},{10,1... | collective-permute-start | bytes 196616 | tf_op jit(solution)/shard_map/ppermute | solution.py:16
  15.7 17.8 %collective-permute-start.2 = (bf16[2,128,128]{2,1,0:T(8,128)(2,1)S(1)}, bf16[2,128,128]{2,1,0:T(8,128)(2,1)S(1)}, u32[]{:S(2)}, u32[]{:S(2)}) collective-permute-start(bf16[2,128,128]{2,1,0:T(8,128)(2,1)S(1)} %bitcast.61), channel_id=1, source_target_pairs={{0,255},{1,0},{2,1},{3,2},{4,3},{5,4},{6,5},{7,6},{8,7},{9,8},{10,... | collective-permute-start | bytes 196616 | tf_op jit(solution)/shard_map/ppermute | solution.py:16
  15.7 17.9 %collective-permute-start.3 = (bf16[2,128,128]{2,1,0:T(8,128)(2,1)S(1)}, bf16[2,128,128]{2,1,0:T(8,128)(2,1)S(1)}, u32[]{:S(2)}, u32[]{:S(2)}) collective-permute-start(bf16[2,128,128]{2,1,0:T(8,128)(2,1)S(1)} %bitcast.62), channel_id=1, source_target_pairs={{0,254},{1,255},{2,0},{3,1},{4,2},{5,3},{6,4},{7,5},{8,6},{9,7},{1... | collective-permute-start | bytes 196616 | tf_op jit(solution)/shard_map/ppermute | solution.py:16
  146.4 17.5 %copy-start.5 = (s32[256]{0:T(256)S(1)}, s32[256]{0:T(256)}, u32[]{:S(2)}) copy-start(s32[256]{0:T(256)} %param.15) | copy-start | bytes 3076
  163.9 9.0 %copy-start.3 = (f32[112,128,128]{1,0,2:T(8,128)S(1)}, f32[112,128,128]{1,0,2:T(8,128)}, u32[]{:S(2)}) copy-start(f32[112,128,128]{1,0,2:T(8,128)} %copy.15) | copy-start | bytes 22020100
  163.9 9.0 %copy-start.6 = (s32[112]{0:T(128)S(1)}, s32[112]{0:T(128)}, u32[]{:S(2)}) copy-start(s32[112]{0:T(128)} %param.18) | copy-start | bytes 1348
  177.4 8.6 %collective-permute-start.4 = (bf16[2,128,128]{2,1,0:T(8,128)(2,1)S(1)}, bf16[2,128,128]{2,1,0:T(8,128)(2,1)S(1)}, u32[]{:S(2)}, u32[]{:S(2)}) collective-permute-start(bf16[2,128,128]{2,1,0:T(8,128)(2,1)S(1)} %bitcast.65), channel_id=1, source_target_pairs={{0,2},{1,3},{2,4},{3,5},{4,6},{5,7},{6,8},{7,9},{8,10},{9,11},{10,... | collective-permute-start | bytes 196616 | tf_op jit(solution)/shard_map/ppermute | solution.py:16
  178.7 7.4 %collective-permute-start.5 = (bf16[2,128,128]{2,1,0:T(8,128)(2,1)S(1)}, bf16[2,128,128]{2,1,0:T(8,128)(2,1)S(1)}, u32[]{:S(2)}, u32[]{:S(2)}) collective-permute-start(bf16[2,128,128]{2,1,0:T(8,128)(2,1)S(1)} %bitcast.66), channel_id=1, source_target_pairs={{0,1},{1,2},{2,3},{3,4},{4,5},{5,6},{6,7},{7,8},{8,9},{9,10},{10,1... | collective-permute-start | bytes 196616 | tf_op jit(solution)/shard_map/ppermute | solution.py:16
  180.4 5.7 %collective-permute-start.6 = (bf16[2,128,128]{2,1,0:T(8,128)(2,1)S(1)}, bf16[2,128,128]{2,1,0:T(8,128)(2,1)S(1)}, u32[]{:S(2)}, u32[]{:S(2)}) collective-permute-start(bf16[2,128,128]{2,1,0:T(8,128)(2,1)S(1)} %bitcast.67), channel_id=1, source_target_pairs={{0,255},{1,0},{2,1},{3,2},{4,3},{5,4},{6,5},{7,6},{8,7},{9,8},{10,... | collective-permute-start | bytes 196616 | tf_op jit(solution)/shard_map/ppermute | solution.py:16
  180.4 7.0 %collective-permute-start.7 = (bf16[2,128,128]{2,1,0:T(8,128)(2,1)S(1)}, bf16[2,128,128]{2,1,0:T(8,128)(2,1)S(1)}, u32[]{:S(2)}, u32[]{:S(2)}) collective-permute-start(bf16[2,128,128]{2,1,0:T(8,128)(2,1)S(1)} %bitcast.68), channel_id=1, source_target_pairs={{0,254},{1,255},{2,0},{3,1},{4,2},{5,3},{6,4},{7,5},{8,6},{9,7},{1... | collective-permute-start | bytes 196616 | tf_op jit(solution)/shard_map/ppermute | solution.py:16
  322.7 9.0 %copy-start.2 = (f32[112,128,128]{1,0,2:T(8,128)S(1)}, f32[112,128,128]{1,0,2:T(8,128)}, u32[]{:S(2)}) copy-start(f32[112,128,128]{1,0,2:T(8,128)} %copy.17) | copy-start | bytes 22020100
  322.8 13.5 %copy-start.1 = (f32[128,128]{1,0:T(8,128)S(1)}, f32[128,128]{1,0:T(8,128)}, u32[]{:S(2)}) copy-start(f32[128,128]{1,0:T(8,128)} %param.12) | copy-start | bytes 196612
  331.8 3.6 %copy-start.4 = (f32[128,128]{1,0:T(8,128)S(1)}, f32[128,128]{1,0:T(8,128)}, u32[]{:S(2)}) copy-start(f32[128,128]{1,0:T(8,128)} %param.13) | copy-start | bytes 196612
Sparse Core Ops, SparseCore 0:
  11.5 122.0 all-gather.4
  177.6 114.8 all-gather.6
where the time goes:
time: 344 us; the launch traced here: 343 us
  waiting for transfers between devices  166 us (48%)
  matrix products  69.7 us (20%)
  local copies, waits for them, and re-layouts  61.7 us (18%)
  between operations  23.5 us (7%)
  starting transfers between devices  20.6 us (6%)
    all_gather x2, waiting for transfers between devices, propagate(): stripe = lax.all_gather(hub_rows, 'blk', axis=0, tiled=True)  165 us
    dot_general x4, local copies, waits for them, and re-layouts, accumulate(): jnp.einsum('sij,sjf->sif', tile_set, inputs, preferred_element_type=jnp.f...  51.8 us
    dot_general x4, matrix products, accumulate(): jnp.einsum('sij,sjf->sif', tile_set, inputs, preferred_element_type=jnp.f...  43.4 us
    dot_general x4, matrix products, accumulate(): jnp.einsum('sn,sif->nif', onehot, products, precision=lax.Precision.HIGHEST)  25.1 us
    ppermute x8, starting transfers between devices, from_behind(): lax.ppermute(shard, axis, [(i, (i + by) % size) for i in range(size)])  20.6 us
  transfers between devices with their start and end apart: 10, of which 3 were waited for; matrix products, arithmetic and copies ran while one was open for 12% of the time, Pallas kernels for 0%

commit v1 on v0

v1 whole, which is shorter than its diff:
```python
import functools

import jax
import jax.numpy as jnp
from jax import lax
from jax.experimental import pallas as pl
from jax.experimental.pallas import tpu as pltpu
from jax.sharding import PartitionSpec as P

F = 128
TILE = 128
NB = 2
KS = 112
HOPS = 2
FETCH = 1
SOURCES = NB + 2 * HOPS * FETCH


def from_behind(shard, axis, by):
    size = lax.axis_size(axis)
    return lax.ppermute(shard, axis, [(i, (i + by) % size) for i in range(size)])


def neighbour_offsets():
    return list(range(-HOPS, 0)) + list(range(1, HOPS + 1))


def placed_pair(block, row):
    zeros = jnp.zeros_like(block)
    return jnp.concatenate([jnp.where(row == 0, block, zeros), jnp.where(row == 0, zeros, block)], axis=1)


def sparse_kernel(row_ref, src_ref, count_ref, fetch_ref, blocks_ref, *refs):
    fetched_refs, (tiles_ref, out_ref, placed_ref) = refs[: 2 * HOPS], refs[2 * HOPS :]
    zeros = jnp.zeros((TILE, F), jnp.bfloat16)
    for source in range(SOURCES):
        if source < NB:
            block = blocks_ref[source]
        else:
            block = fetched_refs[source - NB][fetch_ref[source - NB]]
        placed_ref[2 * source] = jnp.concatenate([block, zeros], axis=1)
        placed_ref[2 * source + 1] = jnp.concatenate([zeros, block], axis=1)
    placed_ref[2 * SOURCES] = jnp.zeros((TILE, NB * F), jnp.bfloat16)
    out_ref[...] = jnp.zeros_like(out_ref)
    live = count_ref[0]

    def which(slot):
        return jnp.where(slot < live, 2 * src_ref[slot] + row_ref[slot], 2 * SOURCES)

    group = 8

    def step(at, _):
        first = at * group
        left = jnp.concatenate([tiles_ref[first + k] for k in range(group)], axis=1)
        right = jnp.concatenate([placed_ref[which(first + k)] for k in range(group)], axis=0)
        out_ref[...] += jnp.dot(left, right, preferred_element_type=jnp.float32)
        return 0

    lax.fori_loop(0, (live + group - 1) // group, step, 0)


def sparse_sums(row, src, count, wanted, blocks, fetched, tiles):
    smem = pl.BlockSpec(memory_space=pltpu.SMEM)
    vmem = pl.BlockSpec(memory_space=pltpu.VMEM)
    return pl.pallas_call(
        sparse_kernel,
        out_shape=jax.ShapeDtypeStruct((TILE, NB * F), jnp.float32),
        in_specs=[smem] * 4 + [vmem] * (2 + 2 * HOPS),
        out_specs=vmem,
        scratch_shapes=[pltpu.VMEM((2 * SOURCES + 1, TILE, NB * F), jnp.bfloat16)],
        name="sparse_sums",
    )(row, src, count, wanted, blocks, *fetched, tiles)


def dense_kernel(group, row_ref, stripe_ref, tiles_ref, start_ref, weight_ref, out_ref, total):
    at = pl.program_id(0)

    @pl.when(at == 0)
    def _():
        total[...] = start_ref[...]

    first = at * group
    left = jnp.concatenate([tiles_ref[k] for k in range(group)], axis=1)
    right = jnp.concatenate([placed_pair(stripe_ref[k], row_ref[first + k]) for k in range(group)], axis=0)
    total[...] += jnp.dot(left, right, preferred_element_type=jnp.float32)

    @pl.when(at == pl.num_programs(0) - 1)
    def _():
        for block in range(NB):
            projected = jnp.dot(
                total[:, block * F : (block + 1) * F],
                weight_ref[...],
                precision=lax.Precision.HIGHEST,
                preferred_element_type=jnp.float32,
            )
            out_ref[block] = jnp.maximum(projected, 0.0).astype(out_ref.dtype)


def dense_layer(row, stripe, tiles, start, weight, dtype, group=16):
    shards = stripe.shape[0]
    whole = lambda shape: pl.BlockSpec(shape, lambda at, *_: (0,) * len(shape))
    return pl.pallas_call(
        functools.partial(dense_kernel, group),
        out_shape=jax.ShapeDtypeStruct((NB, TILE, F), dtype),
        grid_spec=pltpu.PrefetchScalarGridSpec(
            num_scalar_prefetch=1,
            grid=(shards // group,),
            in_specs=[
                pl.BlockSpec((group, TILE, F), lambda at, *_: (at, 0, 0)),
                pl.BlockSpec((group, TILE, TILE), lambda at, *_: (at, 0, 0)),
                whole((TILE, NB * F)),
                whole((F, F)),
            ],
            out_specs=whole((NB, TILE, F)),
            scratch_shapes=[pltpu.VMEM((TILE, NB * F), jnp.float32)],
        ),
        name="dense_layer",
    )(row, stripe, tiles, start, weight)


def shards(
    features,
    weight_one,
    weight_two,
    dense_tiles,
    dense_row,
    hub_block,
    sparse_tiles,
    sparse_row,
    sparse_src,
    sparse_count,
    fetch_list,
):
    own_index = lax.axis_index("blk")
    offsets = neighbour_offsets()
    wanted = fetch_list.reshape(2 * HOPS)
    hub_here = lax.dynamic_index_in_dim(hub_block, own_index, 0, keepdims=False)

    def propagate(blocks, weight, dtype):
        hub_rows = jnp.where(hub_here == 0, blocks[0], blocks[1])[None]
        stripe = lax.all_gather(hub_rows, "blk", axis=0, tiled=True)
        fetched = [from_behind(blocks, "blk", -offsets[entry]) for entry in range(2 * HOPS)]
        start = sparse_sums(sparse_row, sparse_src, sparse_count, wanted, blocks, fetched, sparse_tiles)
        return dense_layer(dense_row, stripe, dense_tiles, start, weight, dtype)

    hidden = propagate(features.astype(jnp.bfloat16).reshape(NB, TILE, F), weight_one, jnp.bfloat16)
    return propagate(hidden, weight_two, jnp.float32).reshape(NB * TILE, F)


def solution(mesh):
    placed = (
        P("blk", None),
        P(),
        P(),
        P("blk", None, None),
        P("blk"),
        P(),
        P("blk", None, None),
        P("blk"),
        P("blk"),
        P("blk"),
        P("blk", None),
    )
    return jax.shard_map(
        shards, mesh=mesh, in_specs=placed, out_specs=P("blk", None), check_vma=False
    )
```

time: 344 us -> 287 us (0.83)
  matrix products: 69.7 us -> 0 us
  local copies, waits for them, and re-layouts: 61.7 us -> 2.55 us
  waiting for transfers between devices: 166 us -> 209 us
  Pallas kernels: 0 us -> 35.9 us
  between operations: 23.5 us -> 14.8 us
    dot_general x10 -> x0, matrix products: 69.7 us -> none  [the longest x4 43.4 us: accumulate(): jnp.einsum('sij,sjf->sif', tile_set, inputs, preferred_element_type=jnp.f...]
    dot_general x4 -> x0, local copies, waits for them, and re-layouts: 51.8 us -> none  [accumulate(): jnp.einsum('sij,sjf->sif', tile_set, inputs, preferred_element_type=jnp.f...]
    all_gather x2, waiting for transfers between devices: 165 us -> 206 us  [propagate(): stripe = lax.all_gather(hub_rows, 'blk', axis=0, tiled=True)]
    pallas_call x0 -> x4, Pallas kernels: none -> 35.9 us  [the longest x2 29.5 us: dense_layer(): pl.pallas_call(functools.partial(dense_kernel, group), out_shape=jax.Shap...]
    gather x2 -> x0, local copies, waits for them, and re-layouts: 5.7 us -> none  [propagate(): gathered_blocks[sparse_src]]
  transfers between devices with their start and end apart: 10 -> 10, of which waited for: 3 -> 6; matrix products, arithmetic and copies ran while one was open for 12% -> 0% of each run, Pallas kernels for 0% -> 2%
where the time goes in v1:
time: 287 us; the launch traced here: 286 us
  waiting for transfers between devices  209 us (73%)
  Pallas kernels  35.9 us (13%)
  starting transfers between devices  20.6 us (7%)
  between operations  14.8 us (5%)
  other arithmetic  2.93 us (1%)
    all_gather x2, waiting for transfers between devices, propagate(): stripe = lax.all_gather(hub_rows, 'blk', axis=0, tiled=True)  206 us
    pallas_call x2, Pallas kernels, dense_layer(): pl.pallas_call(functools.partial(dense_kernel, group), out_shape=jax.Shap...  29.5 us
    ppermute x8, starting transfers between devices, from_behind(): lax.ppermute(shard, axis, [(i, (i + by) % size) for i in range(size)])  20.6 us
    pallas_call x2, Pallas kernels, sparse_sums(): pl.pallas_call(sparse_kernel, out_shape=jax.ShapeDtypeStruct((TILE, NB *...  6.39 us
  transfers between devices with their start and end apart: 10, of which 6 were waited for; matrix products, arithmetic and copies ran while one was open for 0% of the time, Pallas kernels for 2%

profile of v1, /device:TPU:1, one launch (start us, length us, event | category | flops | bytes accessed | tf_op | source)
XLA Modules:
  0.0 285.9 jit_solution(15488140424714863359)
XLA Ops:
  6.5 0.9 convert_element_type.3
  7.5 1.3 dynamic_slice.4
  9.4 0.6 slice_select_fusion.1
  10.0 0.0 all-gather.6.cloned.1.call-update
  10.1 0.0 all-gather.4.cloned.1.call-start
  10.1 2.2 collective-permute-start
  12.3 2.1 collective-permute-start.1
  14.4 7.6 %collective-permute-start.3 = (bf16[2,128,128]{2,1,0:T(8,128)(2,1)S(1)}, bf16[2,128,128]{2,1,0:T(8,128)(2,1)S(1)}, u32[]{:S(2)}, u32[]{:S(2)}) collective-permute-start(bf16[2,128,128]{2,1,0:T(8,128)(2,1)S(1)} %bitcast.9), channel_id=1, source_target_pairs={{0,254},{1,255},{2,0},{3,1},{4,2},{5,3},{6,4},{7,5},{8,6},{9,7},{1... | collective-permute-start | bytes 196616 | tf_op jit(solution)/shard_map/ppermute | solution.py:21
  22.7 0.1 collective-permute-done.refs_0_
  22.9 1.1 collective-permute-done.3.refs_3_
  24.0 0.6 copy-done.7
  24.6 3.2 %sparse_sums.2.start_ref = f32[128,256]{1,0:T(8,128)} custom-call(s32[112]{0:T(128)} %row_ref.6, s32[112]{0:T(128)} %src_ref.3, s32[1]{0:T(128)S(6)} %copy.12.count_ref, s32[4]{0:T(128)} %bitcast.11, bf16[2,128,128]{2,1,0:T(8,128)(2,1)} %bitcast.10, bf16[2,128,128]{2,1,0:T(8,128)(2,1)} %copy-done.1, bf16[2,128,128]{2,1,0:T(8,128)(2,1)} %copy-done.3, ...), custom_call_target="tpu_custom_call" | custom-call | tf_op jit(solution)/shard_map/sparse_sums/pallas_call | solution.py:65
  27.8 105.3 %all-gather.6.cloned.1.call-done = bf16[32768,128]{1,0:T(8,128)(2,1)} async-done(((bf16[128,128]{1,0:T(8,128)(2,1)}), bf16[32768,128]{1,0:T(8,128)(2,1)}) %all-gather.6.cloned.1.call-update) | async-done | bytes 8388624 | tf_op jit(solution)/shard_map/all_gather | solution.py:141
  133.1 14.8 %dense_layer.2.blocks_ref = bf16[2,128,128]{2,1,0:T(8,128)(2,1)} custom-call(s32[256]{0:T(256)} %row_ref.7, bf16[256,128,128]{2,1,0:T(8,128)(2,1)} %bitcast.5, bf16[256,128,128]{2,1,0:T(8,128)(2,1)} %tiles_ref.3, f32[128,256]{1,0:T(8,128)} %sparse_sums.2.start_ref, f32[128,128]{1,0:T(8,128)} %weight_ref.2), custom_call_target="tpu_custom_call" | custom-call | tf_op jit(solution)/shard_map/dense_layer/pallas_call | solution.py:102
  147.9 1.4 slice_select_fusion
  149.3 1.3 collective-permute-start.4
  150.6 1.7 collective-permute-start.5
  152.2 5.7 %collective-permute-start.7 = (bf16[2,128,128]{2,1,0:T(8,128)(2,1)}, bf16[2,128,128]{2,1,0:T(8,128)(2,1)S(1)}, u32[]{:S(2)}, u32[]{:S(2)}) collective-permute-start(bf16[2,128,128]{2,1,0:T(8,128)(2,1)} %dense_layer.2.blocks_ref), channel_id=1, source_target_pairs={{0,254},{1,255},{2,0},{3,1},{4,2},{5,3},{6,4},{7,5},{8,6},{9,7},{1... | collective-permute-start | bytes 196616 | tf_op jit(solution)/shard_map/ppermute | solution.py:21
  157.9 0.2 collective-permute-done.4.refs_0_
  158.1 1.4 collective-permute-done.7.refs_3_
  159.6 0.6 copy-done.8
  160.2 3.2 %sparse_sums.3.start_ref = f32[128,256]{1,0:T(8,128)} custom-call(s32[112]{0:T(128)} %row_ref.6, s32[112]{0:T(128)} %src_ref.3, s32[1]{0:T(128)S(6)} %copy.12.count_ref, s32[4]{0:T(128)} %bitcast.12, bf16[2,128,128]{2,1,0:T(8,128)(2,1)} %dense_layer.2.blocks_ref, bf16[2,128,128]{2,1,0:T(8,128)(2,1)} %copy-done.2, bf16[2,128,128]{2,1,0:T(8,128)(2,1)} %copy-done.4, ...), custom_call_target="tpu_custom_call" | custom-call | tf_op jit(solution)/shard_map/sparse_sums/pallas_call | solution.py:65
  163.4 100.9 %all-gather.4.cloned.1.call-done.stripe_ref = bf16[256,128,128]{2,1,0:T(8,128)(2,1)} async-done(((bf16[1,128,128]{2,1,0:T(8,128)(2,1)}), bf16[256,128,128]{2,1,0:T(8,128)(2,1)}) %all-gather.4.cloned.1.call-update) | async-done | bytes 8388624 | tf_op jit(solution)/shard_map/all_gather | solution.py:141
  264.2 14.8 %dense_layer.3 = f32[2,128,128]{2,1,0:T(8,128)} custom-call(s32[256]{0:T(256)} %row_ref.7, bf16[256,128,128]{2,1,0:T(8,128)(2,1)} %all-gather.4.cloned.1.call-done.stripe_ref, bf16[256,128,128]{2,1,0:T(8,128)(2,1)} %tiles_ref.3, f32[128,256]{1,0:T(8,128)} %sparse_sums.3.start_ref, f32[128,128]{1,0:T(8,128)} %weight_ref.3), custom_call_target="tpu_custom_call" | custom-call | tf_op jit(solution)/shard_map/dense_layer/pallas_call | solution.py:102
  (24 shorter events, 0.1 us)
Async XLA Ops:
  6.5 126.6 %all-gather.6.cloned.1.call-start = ((), (), s32[]{:S(2)}) async-start(), calls=%async_computation.1 | async-start | bytes 8421376 | tf_op jit(solution)/shard_map/all_gather | solution.py:141
  7.4 16.5 %copy-start = (bf16[256,128]{1,0:T(8,128)(2,1)}, bf16[256,128]{1,0:T(8,128)(2,1)S(1)}, u32[]{:S(2)}) copy-start(bf16[256,128]{1,0:T(8,128)(2,1)S(1)} %convert_element_type.3) | copy-start | bytes 196612
  10.1 254.2 %all-gather.4.cloned.1.call-start = ((), (), s32[]{:S(2)}) async-start(), calls=%async_computation | async-start | bytes 8421376 | tf_op jit(solution)/shard_map/all_gather | solution.py:141
  10.1 12.8 %collective-permute-start = (bf16[2,128,128]{2,1,0:T(8,128)(2,1)S(1)}, bf16[2,128,128]{2,1,0:T(8,128)(2,1)S(1)}, u32[]{:S(2)}, u32[]{:S(2)}) collective-permute-start(bf16[2,128,128]{2,1,0:T(8,128)(2,1)S(1)} %bitcast.6), channel_id=1, source_target_pairs={{0,2},{1,3},{2,4},{3,5},{4,6},{5,7},{6,8},{7,9},{8,10},{9,11},{10,... | collective-permute-start | bytes 196616 | tf_op jit(solution)/shard_map/ppermute | solution.py:21
  12.3 10.6 %collective-permute-start.1 = (bf16[2,128,128]{2,1,0:T(8,128)(2,1)S(1)}, bf16[2,128,128]{2,1,0:T(8,128)(2,1)S(1)}, u32[]{:S(2)}, u32[]{:S(2)}) collective-permute-start(bf16[2,128,128]{2,1,0:T(8,128)(2,1)S(1)} %bitcast.7), channel_id=1, source_target_pairs={{0,1},{1,2},{2,3},{3,4},{4,5},{5,6},{6,7},{7,8},{8,9},{9,10},{10,1... | collective-permute-start | bytes 196616 | tf_op jit(solution)/shard_map/ppermute | solution.py:21
  14.4 8.5 %collective-permute-start.2 = (bf16[2,128,128]{2,1,0:T(8,128)(2,1)S(1)}, bf16[2,128,128]{2,1,0:T(8,128)(2,1)S(1)}, u32[]{:S(2)}, u32[]{:S(2)}) collective-permute-start(bf16[2,128,128]{2,1,0:T(8,128)(2,1)S(1)} %bitcast.8), channel_id=1, source_target_pairs={{0,255},{1,0},{2,1},{3,2},{4,3},{5,4},{6,5},{7,6},{8,7},{9,8},{10,... | collective-permute-start | bytes 196616 | tf_op jit(solution)/shard_map/ppermute | solution.py:21
  14.4 9.5 %collective-permute-start.3 = (bf16[2,128,128]{2,1,0:T(8,128)(2,1)S(1)}, bf16[2,128,128]{2,1,0:T(8,128)(2,1)S(1)}, u32[]{:S(2)}, u32[]{:S(2)}) collective-permute-start(bf16[2,128,128]{2,1,0:T(8,128)(2,1)S(1)} %bitcast.9), channel_id=1, source_target_pairs={{0,254},{1,255},{2,0},{3,1},{4,2},{5,3},{6,4},{7,5},{8,6},{9,7},{1... | collective-permute-start | bytes 196616 | tf_op jit(solution)/shard_map/ppermute | solution.py:21
  22.9 1.1 copy-start.1
  22.9 1.1 copy-start.3
  22.9 1.1 copy-start.5
  24.0 0.6 copy-start.7
  149.3 8.8 %collective-permute-start.4 = (bf16[2,128,128]{2,1,0:T(8,128)(2,1)}, bf16[2,128,128]{2,1,0:T(8,128)(2,1)S(1)}, u32[]{:S(2)}, u32[]{:S(2)}) collective-permute-start(bf16[2,128,128]{2,1,0:T(8,128)(2,1)} %dense_layer.2.blocks_ref), channel_id=1, source_target_pairs={{0,2},{1,3},{2,4},{3,5},{4,6},{5,7},{6,8},{7,9},{8,10},{9,11},{10,... | collective-permute-start | bytes 196616 | tf_op jit(solution)/shard_map/ppermute | solution.py:21
  150.6 7.6 %collective-permute-start.5 = (bf16[2,128,128]{2,1,0:T(8,128)(2,1)}, bf16[2,128,128]{2,1,0:T(8,128)(2,1)S(1)}, u32[]{:S(2)}, u32[]{:S(2)}) collective-permute-start(bf16[2,128,128]{2,1,0:T(8,128)(2,1)} %dense_layer.2.blocks_ref), channel_id=1, source_target_pairs={{0,1},{1,2},{2,3},{3,4},{4,5},{5,6},{6,7},{7,8},{8,9},{9,10},{10,1... | collective-permute-start | bytes 196616 | tf_op jit(solution)/shard_map/ppermute | solution.py:21
  152.2 5.9 %collective-permute-start.6 = (bf16[2,128,128]{2,1,0:T(8,128)(2,1)}, bf16[2,128,128]{2,1,0:T(8,128)(2,1)S(1)}, u32[]{:S(2)}, u32[]{:S(2)}) collective-permute-start(bf16[2,128,128]{2,1,0:T(8,128)(2,1)} %dense_layer.2.blocks_ref), channel_id=1, source_target_pairs={{0,255},{1,0},{2,1},{3,2},{4,3},{5,4},{6,5},{7,6},{8,7},{9,8},{10,... | collective-permute-start | bytes 196616 | tf_op jit(solution)/shard_map/ppermute | solution.py:21
  152.2 7.3 %collective-permute-start.7 = (bf16[2,128,128]{2,1,0:T(8,128)(2,1)}, bf16[2,128,128]{2,1,0:T(8,128)(2,1)S(1)}, u32[]{:S(2)}, u32[]{:S(2)}) collective-permute-start(bf16[2,128,128]{2,1,0:T(8,128)(2,1)} %dense_layer.2.blocks_ref), channel_id=1, source_target_pairs={{0,254},{1,255},{2,0},{3,1},{4,2},{5,3},{6,4},{7,5},{8,6},{9,7},{1... | collective-permute-start | bytes 196616 | tf_op jit(solution)/shard_map/ppermute | solution.py:21
  158.1 1.4 copy-start.2
  158.1 1.4 copy-start.4
  158.1 1.4 copy-start.6
  159.6 0.6 copy-start.8
Sparse Core Ops, SparseCore 0:
  11.0 121.9 all-gather.5
  149.4 114.8 all-gather.3

commit v2 on v1

v2 whole, which is shorter than its diff:
```python
import functools

import jax
import jax.numpy as jnp
from jax import lax
from jax.experimental import pallas as pl
from jax.experimental.pallas import tpu as pltpu
from jax.sharding import PartitionSpec as P

F = 128
TILE = 128
NB = 2
KS = 112
HOPS = 2
FETCH = 1
SOURCES = NB + 2 * HOPS * FETCH
NZ, NX, NY, NC = 8, 4, 4, 2
SHARDS = NZ * NX * NY * NC
SIDE = 4

SMEM = pl.BlockSpec(memory_space=pltpu.SMEM)
VMEM = pl.BlockSpec(memory_space=pltpu.VMEM)
ANY = pl.BlockSpec(memory_space=pl.ANY)


def place(index):
    return index // (NX * NY * NC), index // (NY * NC) % NX, index // NC % NY, index % NC


def index_of(z, x, y, core):
    return ((z % NZ * NX + x % NX) * NY + y % NY) * NC + core % NC


def groups_along_z():
    return [[index_of(z, x, y, core) for z in range(NZ)] for x in range(NX) for y in range(NY) for core in range(NC)]


def groups_crossways():
    return [[index_of(z, x, y, 0) for y in range(NY)] for z in range(NZ) for x in range(NX)] + [
        [index_of(z, x, y, 1) for x in range(NX)] for z in range(NZ) for y in range(NY)
    ]


def ring_step(array, by):
    pairs = []
    for index in range(SHARDS):
        z, x, y, core = place(index)
        pairs.append((index, index_of(z, x + (by if core == 0 else 0), y + (by if core == 1 else 0), core)))
    return lax.ppermute(array, "blk", pairs)


def swap_cores(array):
    return lax.ppermute(array, "blk", [(i, i ^ 1) for i in range(SHARDS)])


def swap_across(array):
    return lax.ppermute(array, "blk", [(i, (i + (1 if i % 2 else -1)) % SHARDS) for i in range(SHARDS)])


def from_behind(array, by):
    return lax.ppermute(array, "blk", [(i, (i + by) % SHARDS) for i in range(SHARDS)])


def placed_pair(block, row):
    zeros = jnp.zeros_like(block)
    return jnp.concatenate([jnp.where(row == 0, block, zeros), jnp.where(row == 0, zeros, block)], axis=1)


def enter_kernel(me_ref, hub_ref, features_ref, blocks_ref, copies_ref):
    blocks = [features_ref[b * TILE : (b + 1) * TILE].astype(jnp.bfloat16) for b in range(NB)]
    hub = jnp.where(hub_ref[me_ref[0]] == 0, blocks[0], blocks[1])
    for b in range(NB):
        blocks_ref[b] = blocks[b]
    for z in range(NZ):
        copies_ref[z] = hub


def enter(me, hub_block, features):
    return pl.pallas_call(
        enter_kernel,
        out_shape=(
            jax.ShapeDtypeStruct((NB, TILE, F), jnp.bfloat16),
            jax.ShapeDtypeStruct((NZ, TILE, F), jnp.bfloat16),
        ),
        in_specs=[SMEM, SMEM, VMEM],
        out_specs=(VMEM, VMEM),
        compiler_params=pltpu.CompilerParams(vmem_limit_bytes=8 << 20),
        name="enter",
    )(me, hub_block, features)


def sparse_kernel(me_ref, row_ref, src_ref, count_ref, fetch_ref, blocks_ref, behind_ref, swap_ref, across_ref, ahead_ref, tiles_ref, out_ref, placed_ref):
    zeros = jnp.zeros((TILE, F), jnp.bfloat16)
    even = me_ref[0] % 2 == 0
    before, after = fetch_ref[0, 1], fetch_ref[0, 2]
    blocks = [
        blocks_ref[0],
        blocks_ref[1],
        behind_ref[fetch_ref[0, 0]],
        jnp.where(even, across_ref[before], swap_ref[before]),
        jnp.where(even, swap_ref[after], across_ref[after]),
        ahead_ref[fetch_ref[0, 3]],
    ]
    for source in range(SOURCES):
        placed_ref[2 * source] = jnp.concatenate([blocks[source], zeros], axis=1)
        placed_ref[2 * source + 1] = jnp.concatenate([zeros, blocks[source]], axis=1)
    placed_ref[2 * SOURCES] = jnp.zeros((TILE, NB * F), jnp.bfloat16)
    out_ref[...] = jnp.zeros_like(out_ref)
    live = count_ref[0]

    def which(slot):
        return jnp.where(slot < live, 2 * src_ref[slot] + row_ref[slot], 2 * SOURCES)

    group = 8

    def step(at, _):
        first = at * group
        left = jnp.concatenate([tiles_ref[first + k] for k in range(group)], axis=1)
        right = jnp.concatenate([placed_ref[which(first + k)] for k in range(group)], axis=0)
        out_ref[...] += jnp.dot(left, right, preferred_element_type=jnp.float32)
        return 0

    lax.fori_loop(0, (live + group - 1) // group, step, 0)


def sparse_sums(me, row, src, count, wanted, blocks, fetched, tiles):
    return pl.pallas_call(
        sparse_kernel,
        out_shape=jax.ShapeDtypeStruct((TILE, NB * F), jnp.float32),
        in_specs=[SMEM] * 5 + [VMEM] * (2 + 2 * HOPS),
        out_specs=VMEM,
        scratch_shapes=[pltpu.VMEM((2 * SOURCES + 1, TILE, NB * F), jnp.bfloat16)],
        cost_estimate=pl.CostEstimate(flops=2 * KS * TILE**3, bytes_accessed=2 * KS * TILE**2, transcendentals=0),
        compiler_params=pltpu.CompilerParams(vmem_limit_bytes=16 << 20),
        name="sparse_sums",
    )(me, row, src, count, wanted, blocks, *fetched, tiles)


def dense_kernel(counts, me_ref, shift_ref, own_row_ref, other_row_ref, *refs):
    chunk_refs, (own_ref, other_ref, start_ref, out_ref, held, sems) = refs[: len(counts)], refs[len(counts) :]
    me = me_ref[0]
    x, y, core = me // (NY * NC) % NX, me // NC % NY, me % NC
    fixed = (jnp.where(core == 0, x, y) + shift_ref[0]) % SIDE
    origins = []
    copies = []
    for step in range(sum(counts)):
        at_x = jnp.where(core == 0, fixed, step)
        at_y = jnp.where(core == 0, step, fixed)
        origins.append((at_x * NY + at_y) * NC + core)
        for side, tiles_ref in enumerate((own_ref, other_ref)):
            copies.append(
                pltpu.make_async_copy(tiles_ref.at[:, at_x, at_y, core], held.at[step, side], sems.at[step, side])
            )
            copies[-1].start()
    out_ref[...] = start_ref[...]
    step = 0
    for chunk_ref, count in zip(chunk_refs, counts):
        for k in range(count):
            for side, row_ref in enumerate((own_row_ref, other_row_ref)):
                copies[2 * step + side].wait()
                left = jnp.concatenate([held[step, side, z] for z in range(NZ)], axis=1)
                right = jnp.concatenate(
                    [
                        placed_pair(chunk_ref[k, z], row_ref[z * (NX * NY * NC) + origins[step]])
                        for z in range(NZ)
                    ],
                    axis=0,
                )
                out_ref[side] += jnp.dot(left, right, preferred_element_type=jnp.float32)
            step += 1


def dense_part(me, shift, rows, chunks, tiles, start):
    counts = tuple(chunk.shape[0] for chunk in chunks)
    steps = sum(counts)
    return pl.pallas_call(
        functools.partial(dense_kernel, counts),
        out_shape=jax.ShapeDtypeStruct((NC, TILE, NB * F), jnp.float32),
        in_specs=[SMEM] * 4 + [VMEM] * len(chunks) + [ANY, ANY, VMEM],
        out_specs=VMEM,
        scratch_shapes=[
            pltpu.VMEM((steps, NC, NZ, TILE, TILE), jnp.bfloat16),
            pltpu.SemaphoreType.DMA((steps, NC)),
        ],
        compiler_params=pltpu.CompilerParams(vmem_limit_bytes=16 << 20),
        cost_estimate=pl.CostEstimate(
            flops=8 * steps * NZ * TILE**3, bytes_accessed=6 * steps * NZ * TILE**2, transcendentals=0
        ),
        name="dense_part",
    )(me, jnp.array([shift], jnp.int32), *rows, *chunks, *tiles, start)


def finish_kernel(wide, me_ref, hub_ref, dense_ref, other_ref, sparse_ref, weight_ref, out_ref, *copies):
    blocks = []
    for block in range(NB):
        columns = slice(block * F, (block + 1) * F)
        summed = dense_ref[0, :, columns] + other_ref[:, columns] + sparse_ref[:, columns]
        projected = jnp.dot(
            summed, weight_ref[...], precision=lax.Precision.HIGHEST, preferred_element_type=jnp.float32
        )
        blocks.append(jnp.maximum(projected, 0.0).astype(out_ref.dtype))
        out_ref[block] = blocks[block]
    if wide:
        hub = jnp.where(hub_ref[me_ref[0]] == 0, blocks[0], blocks[1])
        for z in range(NZ):
            copies[0][z] = hub


def finish(me, hub_block, dense, other, sparse, weight, dtype, wide):
    shape = jax.ShapeDtypeStruct((NB, TILE, F), dtype)
    copies = [jax.ShapeDtypeStruct((NZ, TILE, F), dtype)] if wide else []
    return pl.pallas_call(
        functools.partial(finish_kernel, wide),
        out_shape=(shape, *copies),
        in_specs=[SMEM, SMEM] + [VMEM] * 4,
        out_specs=(VMEM,) * (1 + len(copies)),
        compiler_params=pltpu.CompilerParams(vmem_limit_bytes=8 << 20),
        name="finish",
    )(me, hub_block, dense, other, sparse, weight)


def shards(
    features,
    weight_one,
    weight_two,
    dense_tiles,
    dense_row,
    hub_block,
    sparse_tiles,
    sparse_row,
    sparse_src,
    sparse_count,
    fetch_list,
):
    me = lax.axis_index("blk").astype(jnp.int32).reshape(1)
    tiles = [array.reshape(NZ, NX, NY, NC, TILE, TILE) for array in (dense_tiles, swap_cores(dense_tiles))]
    rows = [dense_row, swap_cores(dense_row)]
    zeros = jnp.zeros((NC, TILE, NB * F), jnp.float32)

    def propagate(blocks, copies, weight, dtype, wide):
        column = lax.all_to_all(copies, "blk", 0, 0, axis_index_groups=groups_along_z(), tiled=True)
        plane = lax.all_to_all(
            jnp.broadcast_to(column[None], (SIDE, NZ, TILE, F)),
            "blk",
            0,
            0,
            axis_index_groups=groups_crossways(),
            tiled=True,
        )
        blocks, plane = lax.optimization_barrier((blocks, plane))
        behind = ring_step(plane, 1)
        ahead = ring_step(plane, -1)
        fetched = [from_behind(blocks, 2), swap_cores(blocks), swap_across(blocks), from_behind(blocks, -2)]
        total = dense_part(me, 0, rows, [plane], tiles, zeros)
        behind, ahead, total = lax.optimization_barrier((behind, ahead, total))
        far = (ring_step(behind[: SIDE // 2], 1), ring_step(ahead[SIDE // 2 :], -1))
        total = dense_part(me, SIDE - 1, rows, [behind], tiles, total)
        total = dense_part(me, 1, rows, [ahead], tiles, total)
        sparse = sparse_sums(me, sparse_row, sparse_src, sparse_count, fetch_list, blocks, fetched, sparse_tiles)
        far, total, sparse = lax.optimization_barrier((far, total, sparse))
        total = dense_part(me, 2, rows, far, tiles, total)
        returned = swap_cores(total[1])
        return finish(me, hub_block, total, returned, sparse, weight, dtype, wide)

    blocks, copies = enter(me, hub_block, features)
    hidden, copies = propagate(blocks, copies, weight_one, jnp.bfloat16, True)
    (embedded,) = propagate(hidden, copies, weight_two, jnp.float32, False)
    return embedded.reshape(NB * TILE, F)


def solution(mesh):
    placed = (
        P("blk", None),
        P(),
        P(),
        P("blk", None, None),
        P("blk"),
        P(),
        P("blk", None, None),
        P("blk"),
        P("blk"),
        P("blk"),
        P("blk", None),
    )
    return jax.shard_map(
        shards, mesh=mesh, in_specs=placed, out_specs=P("blk", None), check_vma=False
    )
```

time: 287 us -> 169 us (0.59)
  waiting for transfers between devices: 209 us -> 25.9 us
  blocking collectives: 0 us -> 59.7 us
  starting transfers between devices: 20.6 us -> 45.8 us
  between operations: 14.8 us -> 0.96 us
  Pallas kernels: 35.9 us -> 30 us
  local copies, waits for them, and re-layouts: 2.55 us -> 6.33 us
  other arithmetic: 2.93 us -> 0 us
    all_gather x2 -> x0, waiting for transfers between devices: 206 us -> none  [propagate(): stripe = lax.all_gather(hub_rows, 'blk', axis=0, tiled=True)]
    all_to_all x0 -> x4, blocking collectives: none -> 59.7 us  [the longest x2 33.4 us: propagate(): lax.all_to_all(copies, 'blk', 0, 0, axis_index_groups=groups_along_z(), t...]
    ppermute x8 -> x20, starting transfers between devices: 20.6 us -> 45.8 us  [the longest x6 30.7 us: swap_cores(): return lax.ppermute(array, 'blk', [(i, i ^ 1) for i in range(SHARDS)])]
    ppermute x8 -> x20, waiting for transfers between devices: 2.87 us -> 25.9 us  [the longest x4 11.9 us: from_behind(): lax.ppermute(array, 'blk', [(i, (i + by) % SHARDS) for i in range(SHARDS)])]
    unnamed x18 -> x26, local copies, waits for them, and re-layouts: 1.26 us -> 5.68 us
    pallas_call x2, Pallas kernels: 6.39 us -> 2.11 us  [sparse_sums(): pl.pallas_call(sparse_kernel, out_shape=jax.ShapeDtypeStruct((TILE, NB *...]
    pallas_call x2 -> x11, Pallas kernels: 29.5 us -> 27.9 us  [the longest x8 25 us: dense_part(): pl.pallas_call(functools.partial(dense_kernel, counts), out_shape=jax.Sha...]
  transfers between devices with their start and end apart: 10 -> 20, of which waited for: 6 -> 9; matrix products, arithmetic and copies ran while one was open for 0% -> 0% of each run, Pallas kernels for 2% -> 13%
where the time goes in v2:
time: 169 us
  blocking collectives  59.7 us (35%)
  starting transfers between devices  45.8 us (27%)
  Pallas kernels  30 us (18%)
  waiting for transfers between devices  25.9 us (15%)
  local copies, waits for them, and re-layouts  6.33 us (4%)
    all_to_all x2, blocking collectives, propagate(): lax.all_to_all(copies, 'blk', 0, 0, axis_index_groups=groups_along_z(), t...  33.4 us
    ppermute x6, starting transfers between devices, swap_cores(): return lax.ppermute(array, 'blk', [(i, i ^ 1) for i in range(SHARDS)])  30.7 us
    all_to_all x2, blocking collectives, propagate(): lax.all_to_all(jnp.broadcast_to(column[None], (SIDE, NZ, TILE, F)), 'blk'...  26.3 us
    pallas_call x8, Pallas kernels, dense_part(): pl.pallas_call(functools.partial(dense_kernel, counts), out_shape=jax.Sha...  25 us
    ppermute x4, waiting for transfers between devices, from_behind(): lax.ppermute(array, 'blk', [(i, (i + by) % SHARDS) for i in range(SHARDS)])  11.9 us
    ppermute x8, starting transfers between devices, ring_step(): return lax.ppermute(array, 'blk', pairs)  11 us
    ppermute x8, waiting for transfers between devices, ring_step(): return lax.ppermute(array, 'blk', pairs)  11 us
    unnamed x26, local copies, waits for them, and re-layouts  5.68 us
  transfers between devices with their start and end apart: 20, of which 9 were waited for; matrix products, arithmetic and copies ran while one was open for 0% of the time, Pallas kernels for 13%

profile of v2, /device:TPU:1, one launch (start us, length us, event | category | flops | bytes accessed | tf_op | source)
XLA Modules:
  0.0 168.6 jit_solution(11568606873694071326)
XLA Ops:
  0.0 3.2 %collective-permute-start.3 = (bf16[256,128,128]{2,1,0:T(8,128)(2,1)}, bf16[256,128,128]{2,1,0:T(8,128)(2,1)}, u32[]{:S(2)}, u32[]{:S(2)}) collective-permute-start(bf16[256,128,128]{2,1,0:T(8,128)(2,1)} %param.22), channel_id=1, source_target_pairs={{0,1},{1,0},{2,3},{3,2},{4,5},{5,4},{6,7},{7,6},{8,9},{9,8},{10,11... | collective-permute-start | bytes 25165832 | tf_op jit(solution)/shard_map/ppermute | solution.py:53
  5.4 18.6 %all_to_all.20 = bf16[8,128,128]{2,1,0:T(8,128)(2,1)S(1)} all-to-all(bf16[8,128,128]{2,1,0:T(8,128)(2,1)S(1)} %get-tuple-element.28), channel_id=1, replica_groups={{0,32,64,96,128,160,192,224},{1,33,65,97,129,161,193,225},{2,34,66,98,1..., dimensions={0} | all-to-all | bytes 524288 | tf_op jit(solution)/shard_map/all_to_all | solution.py:241
  24.3 13.8 %all_to_all.21.refs_0_ = bf16[4,8,128,128]{3,2,1,0:T(8,128)(2,1)S(1)} all-to-all(bf16[4,8,128,128]{3,2,1,0:T(8,128)(2,1)S(1)} %broadcast_in_dim.6), channel_id=1, replica_groups={{0,2,4,6},{8,10,12,14},{16,18,20,22},{24,26,28,30},{32,34,36,38},{40,42..., dimensions={0} | all-to-all | bytes 2097152 | tf_op jit(solution)/shard_map/all_to_all | solution.py:242
  40.8 2.4 %collective-permute-start = (s32[256]{0:T(256)}, s32[256]{0:T(256)S(1)}, u32[]{:S(2)}, u32[]{:S(2)}) collective-permute-start(s32[256]{0:T(256)} %own_row_ref.15), channel_id=1, source_target_pairs={{0,1},{1,0},{2,3},{3,2},{4,5},{5,4},{6,7},{7,6},{8,9},{9,8},{10,11... | collective-permute-start | bytes 3080 | tf_op jit(solution)/shard_map/ppermute | solution.py:53
  44.2 3.4 %copy-done = bf16[256,128,128]{2,1,0:T(8,128)(2,1)S(1)} copy-done((bf16[256,128,128]{2,1,0:T(8,128)(2,1)S(1)}, bf16[256,128,128]{2,1,0:T(8,128)(2,1)}, u32[]{:S(2)}) %copy-start) | copy-done | bytes 8388632
  48.3 3.4 %dense_part.8.refs_3_ = f32[2,128,256]{2,1,0:T(8,128)S(1)} custom-call(s32[1]{0:T(128)} %bitcast.me_ref, s32[1]{0:T(128)} %constant.14.clone.shift_ref, s32[256]{0:T(256)S(1)} %copy-done.4, s32[256]{0:T(256)S(1)} %collective-permute-done.other_row_ref, bf16[4,8,128,128]{3,2,1,0:T(8,128)(2,1)S(1)} %all_to_all.21.refs_0_, ...), custom_call_target="tpu_custom_call" | custom-call | flops 536870912 | bytes 3145728 | tf_op jit(solution)/shard_map/dense_part/pallas_call | solution.py:176
  56.2 4.0 %collective-permute-start.7 = (bf16[2,128,128]{2,1,0:T(8,128)(2,1)S(1)}, bf16[2,128,128]{2,1,0:T(8,128)(2,1)S(1)}, u32[]{:S(2)}, u32[]{:S(2)}) collective-permute-start(bf16[2,128,128]{2,1,0:T(8,128)(2,1)S(1)} %get-tuple-element.33.blocks_ref), channel_id=1, source_target_pairs={{0,1},{1,0},{2,3},{3,2},{4,5},{5,4},{6,7},{7,6},{8,9},{9,8},{10,11... | collective-permute-start | bytes 196616 | tf_op jit(solution)/shard_map/ppermute | solution.py:53
  60.2 4.6 %collective-permute-done.6.behind_ref = bf16[2,128,128]{2,1,0:T(8,128)(2,1)S(1)} collective-permute-done((bf16[2,128,128]{2,1,0:T(8,128)(2,1)S(1)}, bf16[2,128,128]{2,1,0:T(8,128)(2,1)S(1)}, u32[]{:S(2)}, u32[]{:S(2)}) %collective-permute-start.6) | collective-permute-done | bytes 65568 | tf_op jit(solution)/shard_map/ppermute | solution.py:61
  69.6 3.1 %dense_part.9.refs_3_ = f32[2,128,256]{2,1,0:T(8,128)S(1)} custom-call(s32[1]{0:T(128)} %bitcast.me_ref, s32[1]{0:T(128)} %constant.15.clone.shift_ref, s32[256]{0:T(256)S(1)} %copy-done.5, s32[256]{0:T(256)S(1)} %collective-permute-done.other_row_ref, bf16[4,8,128,128]{3,2,1,0:T(8,128)(2,1)S(1)} %collective-permute-done.1.refs_0_, ...), custom_call_target="tpu_custom_call" | custom-call | flops 536870912 | bytes 3145728 | tf_op jit(solution)/shard_map/dense_part/pallas_call | solution.py:176
  72.7 3.1 %dense_part.10.refs_4_ = f32[2,128,256]{2,1,0:T(8,128)S(1)} custom-call(s32[1]{0:T(128)} %bitcast.me_ref, s32[1]{0:T(128)} %constant.16.clone.shift_ref, s32[256]{0:T(256)S(1)} %copy-done.5, s32[256]{0:T(256)S(1)} %collective-permute-done.other_row_ref, bf16[4,8,128,128]{3,2,1,0:T(8,128)(2,1)S(1)} %collective-permute-done.2.refs_0_, ...), custom_call_target="tpu_custom_call" | custom-call | flops 536870912 | bytes 3145728 | tf_op jit(solution)/shard_map/dense_part/pallas_call | solution.py:176
  75.8 3.1 %dense_part.11.dense_ref = f32[2,128,256]{2,1,0:T(8,128)S(1)} custom-call(s32[1]{0:T(128)} %bitcast.me_ref, s32[1]{0:T(128)} %constant.17.clone.shift_ref, s32[256]{0:T(256)S(1)} %copy-done.5, s32[256]{0:T(256)S(1)} %collective-permute-done.other_row_ref, bf16[2,8,128,128]{3,2,1,0:T(8,128)(2,1)S(1)} %collective-permute-done.4.refs_0_, ...), custom_call_target="tpu_custom_call" | custom-call | flops 536870912 | bytes 3145728 | tf_op jit(solution)/shard_map/dense_part/pallas_call | solution.py:176
  78.9 8.7 %collective-permute-start.10 = (f32[128,256]{1,0:T(8,128)S(1)}, f32[128,256]{1,0:T(8,128)S(1)}, u32[]{:S(2)}, u32[]{:S(2)}) collective-permute-start(f32[128,256]{1,0:T(8,128)S(1)} %slice_bitcast_fusion.1), channel_id=1, source_target_pairs={{0,1},{1,0},{2,3},{3,2},{4,5},{5,4},{6,7},{7,6},{8,9},{9,8},{10,11... | collective-permute-start | bytes 393224 | tf_op jit(solution)/shard_map/ppermute | solution.py:53
  89.5 14.7 %all_to_all.22 = bf16[8,128,128]{2,1,0:T(8,128)(2,1)S(1)} all-to-all(bf16[8,128,128]{2,1,0:T(8,128)(2,1)S(1)} %get-tuple-element.39), channel_id=1, replica_groups={{0,32,64,96,128,160,192,224},{1,33,65,97,129,161,193,225},{2,34,66,98,1..., dimensions={0} | all-to-all | bytes 524288 | tf_op jit(solution)/shard_map/all_to_all | solution.py:241
  104.5 12.5 %all_to_all.23.refs_0_ = bf16[4,8,128,128]{3,2,1,0:T(8,128)(2,1)S(1)} all-to-all(bf16[4,8,128,128]{3,2,1,0:T(8,128)(2,1)S(1)} %broadcast_in_dim.8), channel_id=1, replica_groups={{0,2,4,6},{8,10,12,14},{16,18,20,22},{24,26,28,30},{32,34,36,38},{40,42..., dimensions={0} | all-to-all | bytes 2097152 | tf_op jit(solution)/shard_map/all_to_all | solution.py:242
  116.9 2.7 %collective-permute-start.12 = (bf16[4,8,128,128]{3,2,1,0:T(8,128)(2,1)S(1)}, bf16[4,8,128,128]{3,2,1,0:T(8,128)(2,1)S(1)}, u32[]{:S(2)}, u32[]{:S(2)}) collective-permute-start(bf16[4,8,128,128]{3,2,1,0:T(8,128)(2,1)S(1)} %all_to_all.23.refs_0_), channel_id=1, source_target_pairs={{0,24},{1,7},{2,26},{3,1},{4,28},{5,3},{6,30},{7,5},{8,0},{9,15},{... | collective-permute-start | bytes 3145736 | tf_op jit(solution)/shard_map/ppermute | solution.py:49
  119.6 3.1 %dense_part.12.refs_3_ = f32[2,128,256]{2,1,0:T(8,128)S(1)} custom-call(s32[1]{0:T(128)} %bitcast.me_ref, s32[1]{0:T(128)} %constant.14.clone.shift_ref, s32[256]{0:T(256)S(1)} %copy-done.5, s32[256]{0:T(256)S(1)} %collective-permute-done.other_row_ref, bf16[4,8,128,128]{3,2,1,0:T(8,128)(2,1)S(1)} %all_to_all.23.refs_0_, ...), custom_call_target="tpu_custom_call" | custom-call | flops 536870912 | bytes 3145728 | tf_op jit(solution)/shard_map/dense_part/pallas_call | solution.py:176
  122.7 9.4 %collective-permute-done.11.refs_0_ = bf16[4,8,128,128]{3,2,1,0:T(8,128)(2,1)S(1)} collective-permute-done((bf16[4,8,128,128]{3,2,1,0:T(8,128)(2,1)S(1)}, bf16[4,8,128,128]{3,2,1,0:T(8,128)(2,1)S(1)}, u32[]{:S(2)}, u32[]{:S(2)}) %collective-permute-start.11) | collective-permute-done | bytes 1048608 | tf_op jit(solution)/shard_map/ppermute | solution.py:49
  132.3 2.7 %collective-permute-start.14 = (bf16[2,8,128,128]{3,2,1,0:T(8,128)(2,1)S(1)}, bf16[2,8,128,128]{3,2,1,0:T(8,128)(2,1)S(1)}, u32[]{:S(2)}, u32[]{:S(2)}) collective-permute-start(bf16[2,8,128,128]{3,2,1,0:T(8,128)(2,1)S(1)} %slice.22), channel_id=1, source_target_pairs={{0,24},{1,7},{2,26},{3,1},{4,28},{5,3},{6,30},{7,5},{8,0},{9,15},{... | collective-permute-start | bytes 1572872 | tf_op jit(solution)/shard_map/ppermute | solution.py:49
  135.0 3.7 %collective-permute-start.16 = (bf16[2,128,128]{2,1,0:T(8,128)(2,1)S(1)}, bf16[2,128,128]{2,1,0:T(8,128)(2,1)S(1)}, u32[]{:S(2)}, u32[]{:S(2)}) collective-permute-start(bf16[2,128,128]{2,1,0:T(8,128)(2,1)S(1)} %get-tuple-element.44.blocks_ref), channel_id=1, source_target_pairs={{0,1},{1,0},{2,3},{3,2},{4,5},{5,4},{6,7},{7,6},{8,9},{9,8},{10,11... | collective-permute-start | bytes 196616 | tf_op jit(solution)/shard_map/ppermute | solution.py:53
  138.8 4.9 %collective-permute-done.15.behind_ref = bf16[2,128,128]{2,1,0:T(8,128)(2,1)S(1)} collective-permute-done((bf16[2,128,128]{2,1,0:T(8,128)(2,1)S(1)}, bf16[2,128,128]{2,1,0:T(8,128)(2,1)S(1)}, u32[]{:S(2)}, u32[]{:S(2)}) %collective-permute-start.15) | collective-permute-done | bytes 65568 | tf_op jit(solution)/shard_map/ppermute | solution.py:61
  148.2 3.1 %dense_part.13.refs_3_ = f32[2,128,256]{2,1,0:T(8,128)S(1)} custom-call(s32[1]{0:T(128)} %bitcast.me_ref, s32[1]{0:T(128)} %constant.15.clone.shift_ref, s32[256]{0:T(256)S(1)} %copy-done.5, s32[256]{0:T(256)S(1)} %collective-permute-done.other_row_ref, bf16[4,8,128,128]{3,2,1,0:T(8,128)(2,1)S(1)} %collective-permute-done.11.refs_0_, ...), custom_call_target="tpu_custom_call" | custom-call | flops 536870912 | bytes 3145728 | tf_op jit(solution)/shard_map/dense_part/pallas_call | solution.py:176
  151.3 3.1 %dense_part.14.refs_4_ = f32[2,128,256]{2,1,0:T(8,128)S(1)} custom-call(s32[1]{0:T(128)} %bitcast.me_ref, s32[1]{0:T(128)} %constant.16.clone.shift_ref, s32[256]{0:T(256)S(1)} %copy-done.5, s32[256]{0:T(256)S(1)} %collective-permute-done.other_row_ref, bf16[4,8,128,128]{3,2,1,0:T(8,128)(2,1)S(1)} %collective-permute-done.12.refs_0_, ...), custom_call_target="tpu_custom_call" | custom-call | flops 536870912 | bytes 3145728 | tf_op jit(solution)/shard_map/dense_part/pallas_call | solution.py:176
  154.4 3.1 %dense_part.15.dense_ref = f32[2,128,256]{2,1,0:T(8,128)S(1)} custom-call(s32[1]{0:T(128)} %bitcast.me_ref, s32[1]{0:T(128)} %constant.17.clone.shift_ref, s32[256]{0:T(256)S(1)} %copy-done.5, s32[256]{0:T(256)S(1)} %collective-permute-done.other_row_ref, bf16[2,8,128,128]{3,2,1,0:T(8,128)(2,1)S(1)} %collective-permute-done.13.refs_0_, ...), custom_call_target="tpu_custom_call" | custom-call | flops 536870912 | bytes 3145728 | tf_op jit(solution)/shard_map/dense_part/pallas_call | solution.py:176
  157.5 8.6 %collective-permute-start.19 = (f32[128,256]{1,0:T(8,128)S(1)}, f32[128,256]{1,0:T(8,128)S(1)}, u32[]{:S(2)}, u32[]{:S(2)}) collective-permute-start(f32[128,256]{1,0:T(8,128)S(1)} %slice_bitcast_fusion), channel_id=1, source_target_pairs={{0,1},{1,0},{2,3},{3,2},{4,5},{5,4},{6,7},{7,6},{8,9},{9,8},{10,11... | collective-permute-start | bytes 393224 | tf_op jit(solution)/shard_map/ppermute | solution.py:53
  (68 shorter events, 24.7 us)
Async XLA Ops:
  0.0 44.2 %collective-permute-start.3 = (bf16[256,128,128]{2,1,0:T(8,128)(2,1)}, bf16[256,128,128]{2,1,0:T(8,128)(2,1)}, u32[]{:S(2)}, u32[]{:S(2)}) collective-permute-start(bf16[256,128,128]{2,1,0:T(8,128)(2,1)} %param.22), channel_id=1, source_target_pairs={{0,1},{1,0},{2,3},{3,2},{4,5},{5,4},{6,7},{7,6},{8,9},{9,8},{10,11... | collective-permute-start | bytes 25165832 | tf_op jit(solution)/shard_map/ppermute | solution.py:53
  38.1 15.2 %collective-permute-start.1 = (bf16[4,8,128,128]{3,2,1,0:T(8,128)(2,1)S(1)}, bf16[4,8,128,128]{3,2,1,0:T(8,128)(2,1)S(1)}, u32[]{:S(2)}, u32[]{:S(2)}) collective-permute-start(bf16[4,8,128,128]{3,2,1,0:T(8,128)(2,1)S(1)} %all_to_all.21.refs_0_), channel_id=1, source_target_pairs={{0,8},{1,3},{2,10},{3,5},{4,12},{5,7},{6,14},{7,1},{8,16},{9,11},{... | collective-permute-start | bytes 3145736 | tf_op jit(solution)/shard_map/ppermute | solution.py:49
  39.1 14.1 %collective-permute-start.2 = (bf16[4,8,128,128]{3,2,1,0:T(8,128)(2,1)S(1)}, bf16[4,8,128,128]{3,2,1,0:T(8,128)(2,1)S(1)}, u32[]{:S(2)}, u32[]{:S(2)}) collective-permute-start(bf16[4,8,128,128]{3,2,1,0:T(8,128)(2,1)S(1)} %all_to_all.21.refs_0_), channel_id=1, source_target_pairs={{0,24},{1,7},{2,26},{3,1},{4,28},{5,3},{6,30},{7,5},{8,0},{9,15},{... | collective-permute-start | bytes 3145736 | tf_op jit(solution)/shard_map/ppermute | solution.py:49
  40.8 3.4 %collective-permute-start = (s32[256]{0:T(256)}, s32[256]{0:T(256)S(1)}, u32[]{:S(2)}, u32[]{:S(2)}) collective-permute-start(s32[256]{0:T(256)} %own_row_ref.15), channel_id=1, source_target_pairs={{0,1},{1,0},{2,3},{3,2},{4,5},{5,4},{6,7},{7,6},{8,9},{9,8},{10,11... | collective-permute-start | bytes 3080 | tf_op jit(solution)/shard_map/ppermute | solution.py:53
  48.2 20.3 %copy-start.11 = (s32[112]{0:T(128)S(1)}, s32[112]{0:T(128)}, u32[]{:S(2)}) copy-start(s32[112]{0:T(128)} %src_ref.3) | copy-start | bytes 1348
  48.2 20.3 %copy-start.12 = (s32[1,4]{1,0:T(1,128)S(1)}, s32[1,4]{1,0:T(1,128)}, u32[]{:S(2)}) copy-start(s32[1,4]{1,0:T(1,128)} %fetch_ref.3) | copy-start | bytes 52
  48.3 21.3 %copy-start.1 = (bf16[256,128,128]{2,1,0:T(8,128)(2,1)S(1)}, bf16[256,128,128]{2,1,0:T(8,128)(2,1)}, u32[]{:S(2)}) copy-start(bf16[256,128,128]{2,1,0:T(8,128)(2,1)} %param.22) | copy-start | bytes 25165828
  48.3 21.3 %copy-start.5 = (s32[256]{0:T(256)S(1)}, s32[256]{0:T(256)}, u32[]{:S(2)}) copy-start(s32[256]{0:T(256)} %own_row_ref.15) | copy-start | bytes 3076
  53.3 22.5 %collective-permute-start.4 = (bf16[2,8,128,128]{3,2,1,0:T(8,128)(2,1)S(1)}, bf16[2,8,128,128]{3,2,1,0:T(8,128)(2,1)S(1)}, u32[]{:S(2)}, u32[]{:S(2)}) collective-permute-start(bf16[2,8,128,128]{3,2,1,0:T(8,128)(2,1)S(1)} %slice.18), channel_id=1, source_target_pairs={{0,8},{1,3},{2,10},{3,5},{4,12},{5,7},{6,14},{7,1},{8,16},{9,11},{... | collective-permute-start | bytes 1572872 | tf_op jit(solution)/shard_map/ppermute | solution.py:49
  54.5 21.3 %collective-permute-start.5 = (bf16[2,8,128,128]{3,2,1,0:T(8,128)(2,1)S(1)}, bf16[2,8,128,128]{3,2,1,0:T(8,128)(2,1)S(1)}, u32[]{:S(2)}, u32[]{:S(2)}) collective-permute-start(bf16[2,8,128,128]{3,2,1,0:T(8,128)(2,1)S(1)} %slice.19), channel_id=1, source_target_pairs={{0,24},{1,7},{2,26},{3,1},{4,28},{5,3},{6,30},{7,5},{8,0},{9,15},{... | collective-permute-start | bytes 1572872 | tf_op jit(solution)/shard_map/ppermute | solution.py:49
  56.2 8.6 %collective-permute-start.6 = (bf16[2,128,128]{2,1,0:T(8,128)(2,1)S(1)}, bf16[2,128,128]{2,1,0:T(8,128)(2,1)S(1)}, u32[]{:S(2)}, u32[]{:S(2)}) collective-permute-start(bf16[2,128,128]{2,1,0:T(8,128)(2,1)S(1)} %get-tuple-element.33.blocks_ref), channel_id=1, source_target_pairs={{0,2},{1,3},{2,4},{3,5},{4,6},{5,7},{6,8},{7,9},{8,10},{9,11},{10,... | collective-permute-start | bytes 196616 | tf_op jit(solution)/shard_map/ppermute | solution.py:61
  56.2 11.5 %collective-permute-start.7 = (bf16[2,128,128]{2,1,0:T(8,128)(2,1)S(1)}, bf16[2,128,128]{2,1,0:T(8,128)(2,1)S(1)}, u32[]{:S(2)}, u32[]{:S(2)}) collective-permute-start(bf16[2,128,128]{2,1,0:T(8,128)(2,1)S(1)} %get-tuple-element.33.blocks_ref), channel_id=1, source_target_pairs={{0,1},{1,0},{2,3},{3,2},{4,5},{5,4},{6,7},{7,6},{8,9},{9,8},{10,11... | collective-permute-start | bytes 196616 | tf_op jit(solution)/shard_map/ppermute | solution.py:53
  60.2 7.5 %collective-permute-start.8 = (bf16[2,128,128]{2,1,0:T(8,128)(2,1)S(1)}, bf16[2,128,128]{2,1,0:T(8,128)(2,1)S(1)}, u32[]{:S(2)}, u32[]{:S(2)}) collective-permute-start(bf16[2,128,128]{2,1,0:T(8,128)(2,1)S(1)} %get-tuple-element.33.blocks_ref), channel_id=1, source_target_pairs={{0,255},{1,2},{2,1},{3,4},{4,3},{5,6},{6,5},{7,8},{8,7},{9,10},{10... | collective-permute-start | bytes 196616 | tf_op jit(solution)/shard_map/ppermute | solution.py:57
  64.8 3.7 %collective-permute-start.9 = (bf16[2,128,128]{2,1,0:T(8,128)(2,1)S(1)}, bf16[2,128,128]{2,1,0:T(8,128)(2,1)S(1)}, u32[]{:S(2)}, u32[]{:S(2)}) collective-permute-start(bf16[2,128,128]{2,1,0:T(8,128)(2,1)S(1)} %get-tuple-element.33.blocks_ref), channel_id=1, source_target_pairs={{0,254},{1,255},{2,0},{3,1},{4,2},{5,3},{6,4},{7,5},{8,6},{9,7},{1... | collective-permute-start | bytes 196616 | tf_op jit(solution)/shard_map/ppermute | solution.py:61
  78.9 9.7 %collective-permute-start.10 = (f32[128,256]{1,0:T(8,128)S(1)}, f32[128,256]{1,0:T(8,128)S(1)}, u32[]{:S(2)}, u32[]{:S(2)}) collective-permute-start(f32[128,256]{1,0:T(8,128)S(1)} %slice_bitcast_fusion.1), channel_id=1, source_target_pairs={{0,1},{1,0},{2,3},{3,2},{4,5},{5,4},{6,7},{7,6},{8,9},{9,8},{10,11... | collective-permute-start | bytes 393224 | tf_op jit(solution)/shard_map/ppermute | solution.py:53
  116.9 15.2 %collective-permute-start.11 = (bf16[4,8,128,128]{3,2,1,0:T(8,128)(2,1)S(1)}, bf16[4,8,128,128]{3,2,1,0:T(8,128)(2,1)S(1)}, u32[]{:S(2)}, u32[]{:S(2)}) collective-permute-start(bf16[4,8,128,128]{3,2,1,0:T(8,128)(2,1)S(1)} %all_to_all.23.refs_0_), channel_id=1, source_target_pairs={{0,8},{1,3},{2,10},{3,5},{4,12},{5,7},{6,14},{7,1},{8,16},{9,11},{... | collective-permute-start | bytes 3145736 | tf_op jit(solution)/shard_map/ppermute | solution.py:49
  116.9 15.2 %collective-permute-start.12 = (bf16[4,8,128,128]{3,2,1,0:T(8,128)(2,1)S(1)}, bf16[4,8,128,128]{3,2,1,0:T(8,128)(2,1)S(1)}, u32[]{:S(2)}, u32[]{:S(2)}) collective-permute-start(bf16[4,8,128,128]{3,2,1,0:T(8,128)(2,1)S(1)} %all_to_all.23.refs_0_), channel_id=1, source_target_pairs={{0,24},{1,7},{2,26},{3,1},{4,28},{5,3},{6,30},{7,5},{8,0},{9,15},{... | collective-permute-start | bytes 3145736 | tf_op jit(solution)/shard_map/ppermute | solution.py:49
  132.1 22.2 %collective-permute-start.13 = (bf16[2,8,128,128]{3,2,1,0:T(8,128)(2,1)S(1)}, bf16[2,8,128,128]{3,2,1,0:T(8,128)(2,1)S(1)}, u32[]{:S(2)}, u32[]{:S(2)}) collective-permute-start(bf16[2,8,128,128]{3,2,1,0:T(8,128)(2,1)S(1)} %slice.21), channel_id=1, source_target_pairs={{0,8},{1,3},{2,10},{3,5},{4,12},{5,7},{6,14},{7,1},{8,16},{9,11},{... | collective-permute-start | bytes 1572872 | tf_op jit(solution)/shard_map/ppermute | solution.py:49
  132.3 22.1 %collective-permute-start.14 = (bf16[2,8,128,128]{3,2,1,0:T(8,128)(2,1)S(1)}, bf16[2,8,128,128]{3,2,1,0:T(8,128)(2,1)S(1)}, u32[]{:S(2)}, u32[]{:S(2)}) collective-permute-start(bf16[2,8,128,128]{3,2,1,0:T(8,128)(2,1)S(1)} %slice.22), channel_id=1, source_target_pairs={{0,24},{1,7},{2,26},{3,1},{4,28},{5,3},{6,30},{7,5},{8,0},{9,15},{... | collective-permute-start | bytes 1572872 | tf_op jit(solution)/shard_map/ppermute | solution.py:49
  135.0 8.6 %collective-permute-start.15 = (bf16[2,128,128]{2,1,0:T(8,128)(2,1)S(1)}, bf16[2,128,128]{2,1,0:T(8,128)(2,1)S(1)}, u32[]{:S(2)}, u32[]{:S(2)}) collective-permute-start(bf16[2,128,128]{2,1,0:T(8,128)(2,1)S(1)} %get-tuple-element.44.blocks_ref), channel_id=1, source_target_pairs={{0,2},{1,3},{2,4},{3,5},{4,6},{5,7},{6,8},{7,9},{8,10},{9,11},{10,... | collective-permute-start | bytes 196616 | tf_op jit(solution)/shard_map/ppermute | solution.py:61
  135.0 10.5 %collective-permute-start.16 = (bf16[2,128,128]{2,1,0:T(8,128)(2,1)S(1)}, bf16[2,128,128]{2,1,0:T(8,128)(2,1)S(1)}, u32[]{:S(2)}, u32[]{:S(2)}) collective-permute-start(bf16[2,128,128]{2,1,0:T(8,128)(2,1)S(1)} %get-tuple-element.44.blocks_ref), channel_id=1, source_target_pairs={{0,1},{1,0},{2,3},{3,2},{4,5},{5,4},{6,7},{7,6},{8,9},{9,8},{10,11... | collective-permute-start | bytes 196616 | tf_op jit(solution)/shard_map/ppermute | solution.py:53
  138.7 6.8 %collective-permute-start.17 = (bf16[2,128,128]{2,1,0:T(8,128)(2,1)S(1)}, bf16[2,128,128]{2,1,0:T(8,128)(2,1)S(1)}, u32[]{:S(2)}, u32[]{:S(2)}) collective-permute-start(bf16[2,128,128]{2,1,0:T(8,128)(2,1)S(1)} %get-tuple-element.44.blocks_ref), channel_id=1, source_target_pairs={{0,255},{1,2},{2,1},{3,4},{4,3},{5,6},{6,5},{7,8},{8,7},{9,10},{10... | collective-permute-start | bytes 196616 | tf_op jit(solution)/shard_map/ppermute | solution.py:57
  143.7 3.4 %collective-permute-start.18 = (bf16[2,128,128]{2,1,0:T(8,128)(2,1)S(1)}, bf16[2,128,128]{2,1,0:T(8,128)(2,1)S(1)}, u32[]{:S(2)}, u32[]{:S(2)}) collective-permute-start(bf16[2,128,128]{2,1,0:T(8,128)(2,1)S(1)} %get-tuple-element.44.blocks_ref), channel_id=1, source_target_pairs={{0,254},{1,255},{2,0},{3,1},{4,2},{5,3},{6,4},{7,5},{8,6},{9,7},{1... | collective-permute-start | bytes 196616 | tf_op jit(solution)/shard_map/ppermute | solution.py:61
  157.5 9.6 %collective-permute-start.19 = (f32[128,256]{1,0:T(8,128)S(1)}, f32[128,256]{1,0:T(8,128)S(1)}, u32[]{:S(2)}, u32[]{:S(2)}) collective-permute-start(f32[128,256]{1,0:T(8,128)S(1)} %slice_bitcast_fusion), channel_id=1, source_target_pairs={{0,1},{1,0},{2,3},{3,2},{4,5},{5,4},{6,7},{7,6},{8,9},{9,8},{10,11... | collective-permute-start | bytes 393224 | tf_op jit(solution)/shard_map/ppermute | solution.py:53
  (9 other events, 84.7 us)

commit v3 on v2

--- a/solution.py
+++ b/solution.py
@@ -6,6 +6,7 @@
 from jax.experimental import pallas as pl
 from jax.experimental.pallas import tpu as pltpu
 from jax.sharding import PartitionSpec as P
+
 
 F = 128
 TILE = 128
@@ -20,7 +21,7 @@
 
 SMEM = pl.BlockSpec(memory_space=pltpu.SMEM)
 VMEM = pl.BlockSpec(memory_space=pltpu.VMEM)
-ANY = pl.BlockSpec(memory_space=pl.ANY)
+HBM = pl.BlockSpec(memory_space=pltpu.HBM)
 
 
 def place(index):
@@ -136,35 +137,49 @@
     )(me, row, src, count, wanted, blocks, *fetched, tiles)
 
 
+def collect_kernel(me_ref, own_ref, other_ref, out_ref, sems):
+    core = me_ref[0] % NC
+    copies = [
+        pltpu.make_async_copy(tiles_ref.at[z, :, :, core], out_ref.at[side, z], sems.at[side, z])
+        for side, tiles_ref in enumerate((own_ref, other_ref))
+        for z in range(NZ)
+    ]
+    for copy in copies:
+        copy.start()
+    for copy in copies:
+        copy.wait()
+
+
+def collect(me, own, other):
+    shape = (NZ, NX, NY, NC, TILE, TILE)
+    return pl.pallas_call(
+        collect_kernel,
+        out_shape=jax.ShapeDtypeStruct((NC, NZ, NX, NY, TILE, TILE), jnp.bfloat16),
+        in_specs=[SMEM, HBM, HBM],
+        out_specs=VMEM,
+        scratch_shapes=[pltpu.SemaphoreType.DMA((NC, NZ))],
+        compiler_params=pltpu.CompilerParams(vmem_limit_bytes=12 << 20),
+        cost_estimate=pl.CostEstimate(flops=0, bytes_accessed=2 * SHARDS * TILE**2, transcendentals=0),
+        name="collect",
+    )(me, own.reshape(shape), other.reshape(shape))
+
+
 def dense_kernel(counts, me_ref, shift_ref, own_row_ref, other_row_ref, *refs):
-    chunk_refs, (own_ref, other_ref, start_ref, out_ref, held, sems) = refs[: len(counts)], refs[len(counts) :]
+    chunk_refs, (tiles_ref, start_ref, out_ref) = refs[: len(counts)], refs[len(counts) :]
     me = me_ref[0]
     x, y, core = me // (NY * NC) % NX, me // NC % NY, me % NC
     fixed = (jnp.where(core == 0, x, y) + shift_ref[0]) % SIDE
-    origins = []
-    copies = []
-    for step in range(sum(counts)):
-        at_x = jnp.where(core == 0, fixed, step)
-        at_y = jnp.where(core == 0, step, fixed)
-        origins.append((at_x * NY + at_y) * NC + core)
-        for side, tiles_ref in enumerate((own_ref, other_ref)):
-            copies.append(
-                pltpu.make_async_copy(tiles_ref.at[:, at_x, at_y, core], held.at[step, side], sems.at[step, side])
-            )
-            copies[-1].start()
     out_ref[...] = start_ref[...]
     step = 0
     for chunk_ref, count in zip(chunk_refs, counts):
         for k in range(count):
+            at_x = jnp.where(core == 0, fixed, step)
+            at_y = jnp.where(core == 0, step, fixed)
+            sources = [((z * NX + at_x) * NY + at_y) * NC + core for z in range(NZ)]
             for side, row_ref in enumerate((own_row_ref, other_row_ref)):
-                copies[2 * step + side].wait()
-                left = jnp.concatenate([held[step, side, z] for z in range(NZ)], axis=1)
+                left = jnp.concatenate([tiles_ref[side, z, at_x, at_y] for z in range(NZ)], axis=1)
                 right = jnp.concatenate(
-                    [
-                        placed_pair(chunk_ref[k, z], row_ref[z * (NX * NY * NC) + origins[step]])
-                        for z in range(NZ)
-                    ],
-                    axis=0,
+                    [placed_pair(chunk_ref[k, z], row_ref[source]) for z, source in enumerate(sources)], axis=0
                 )
                 out_ref[side] += jnp.dot(left, right, preferred_element_type=jnp.float32)
             step += 1
@@ -176,18 +191,14 @@
     return pl.pallas_call(
         functools.partial(dense_kernel, counts),
         out_shape=jax.ShapeDtypeStruct((NC, TILE, NB * F), jnp.float32),
-        in_specs=[SMEM] * 4 + [VMEM] * len(chunks) + [ANY, ANY, VMEM],
+        in_specs=[SMEM] * 4 + [VMEM] * (len(chunks) + 2),
         out_specs=VMEM,
-        scratch_shapes=[
-            pltpu.VMEM((steps, NC, NZ, TILE, TILE), jnp.bfloat16),
-            pltpu.SemaphoreType.DMA((steps, NC)),
-        ],
         compiler_params=pltpu.CompilerParams(vmem_limit_bytes=16 << 20),
         cost_estimate=pl.CostEstimate(
             flops=8 * steps * NZ * TILE**3, bytes_accessed=6 * steps * NZ * TILE**2, transcendentals=0
         ),
         name="dense_part",
-    )(me, jnp.array([shift], jnp.int32), *rows, *chunks, *tiles, start)
+    )(me, jnp.array([shift], jnp.int32), *rows, *chunks, tiles, start)
 
 
 def finish_kernel(wide, me_ref, hub_ref, dense_ref, other_ref, sparse_ref, weight_ref, out_ref, *copies):
@@ -233,11 +244,11 @@
     fetch_list,
 ):
     me = lax.axis_index("blk").astype(jnp.int32).reshape(1)
-    tiles = [array.reshape(NZ, NX, NY, NC, TILE, TILE) for array in (dense_tiles, swap_cores(dense_tiles))]
     rows = [dense_row, swap_cores(dense_row)]
+    other_tiles = swap_cores(dense_tiles)
     zeros = jnp.zeros((NC, TILE, NB * F), jnp.float32)
 
-    def propagate(blocks, copies, weight, dtype, wide):
+    def propagate(blocks, copies, weight, dtype, wide, tiles=None):
         column = lax.all_to_all(copies, "blk", 0, 0, axis_index_groups=groups_along_z(), tiled=True)
         plane = lax.all_to_all(
             jnp.broadcast_to(column[None], (SIDE, NZ, TILE, F)),
@@ -247,7 +258,11 @@
             axis_index_groups=groups_crossways(),
             tiled=True,
         )
-        blocks, plane = lax.optimization_barrier((blocks, plane))
+        if tiles is None:
+            blocks, plane, others = lax.optimization_barrier((blocks, plane, other_tiles))
+            tiles = collect(me, dense_tiles, others)
+        else:
+            blocks, plane = lax.optimization_barrier((blocks, plane))
         behind = ring_step(plane, 1)
         ahead = ring_step(plane, -1)
         fetched = [from_behind(blocks, 2), swap_cores(blocks), swap_across(blocks), from_behind(blocks, -2)]
@@ -260,11 +275,11 @@
         far, total, sparse = lax.optimization_barrier((far, total, sparse))
         total = dense_part(me, 2, rows, far, tiles, total)
         returned = swap_cores(total[1])
-        return finish(me, hub_block, total, returned, sparse, weight, dtype, wide)
+        return *finish(me, hub_block, total, returned, sparse, weight, dtype, wide), tiles
 
     blocks, copies = enter(me, hub_block, features)
-    hidden, copies = propagate(blocks, copies, weight_one, jnp.bfloat16, True)
-    (embedded,) = propagate(hidden, copies, weight_two, jnp.float32, False)
+    hidden, copies, tiles = propagate(blocks, copies, weight_one, jnp.bfloat16, True)
+    embedded, _ = propagate(hidden, copies, weight_two, jnp.float32, False, tiles)
     return embedded.reshape(NB * TILE, F)
 
 
@@ -282,6 +297,4 @@
         P("blk"),
         P("blk", None),
     )
-    return jax.shard_map(
-        shards, mesh=mesh, in_specs=placed, out_specs=P("blk", None), check_vma=False
-    )
+    return jax.shard_map(shards, mesh=mesh, in_specs=placed, out_specs=P("blk", None), check_vma=False)

time: 169 us -> 154 us (0.911)
  Pallas kernels: 30 us -> 20.6 us
  starting transfers between devices: 45.8 us -> 39.1 us
    pallas_call x8, Pallas kernels: 25 us -> 10.6 us  [dense_part(): pl.pallas_call(functools.partial(dense_kernel, counts), out_shape=jax.Sha...]
    ppermute x6, starting transfers between devices: 30.7 us -> 23 us  [swap_cores(): return lax.ppermute(array, 'blk', [(i, i ^ 1) for i in range(SHARDS)])]
    ppermute x8, waiting for transfers between devices: 11 us -> 14.3 us  [ring_step(): return lax.ppermute(array, 'blk', pairs)]
    pallas_call x0 -> x1, Pallas kernels: none -> 2.57 us  [collect(): pl.pallas_call(collect_kernel, out_shape=jax.ShapeDtypeStruct((NC, NZ, NX...]
    pallas_call x2, Pallas kernels: 2.11 us -> 4.54 us  [sparse_sums(): pl.pallas_call(sparse_kernel, out_shape=jax.ShapeDtypeStruct((TILE, NB *...]
    unnamed x26 -> x22, local copies, waits for them, and re-layouts: 5.68 us -> 5.01 us
  transfers between devices with their start and end apart: 20 -> 20, of which waited for: 9 -> 9; matrix products, arithmetic and copies ran while one was open for 0% -> 0% of each run, Pallas kernels for 13% -> 10%
where the time goes in v3:
time: 154 us; the launch traced here: 153 us
  blocking collectives  59.6 us (39%)
  starting transfers between devices  39.1 us (25%)
  waiting for transfers between devices  27.4 us (18%)
  Pallas kernels  20.6 us (13%)
  local copies, waits for them, and re-layouts  5.66 us (4%)
    all_to_all x2, blocking collectives, propagate(): lax.all_to_all(copies, 'blk', 0, 0, axis_index_groups=groups_along_z(), t...  33.1 us
    all_to_all x2, blocking collectives, propagate(): lax.all_to_all(jnp.broadcast_to(column[None], (SIDE, NZ, TILE, F)), 'blk'...  26.6 us
    ppermute x6, starting transfers between devices, swap_cores(): return lax.ppermute(array, 'blk', [(i, i ^ 1) for i in range(SHARDS)])  23 us
    ppermute x8, waiting for transfers between devices, ring_step(): return lax.ppermute(array, 'blk', pairs)  14.3 us
    ppermute x8, starting transfers between devices, ring_step(): return lax.ppermute(array, 'blk', pairs)  11.4 us
    ppermute x4, waiting for transfers between devices, from_behind(): lax.ppermute(array, 'blk', [(i, (i + by) % SHARDS) for i in range(SHARDS)])  11.2 us
    pallas_call x8, Pallas kernels, dense_part(): pl.pallas_call(functools.partial(dense_kernel, counts), out_shape=jax.Sha...  10.6 us
    unnamed x22, local copies, waits for them, and re-layouts  5.01 us
  transfers between devices with their start and end apart: 20, of which 9 were waited for; matrix products, arithmetic and copies ran while one was open for 0% of the time, Pallas kernels for 10%

profile of v3, /device:TPU:1, one launch (start us, length us, event | category | flops | bytes accessed | tf_op | source)
XLA Modules:
  0.0 153.4 jit_solution(113102116451471031)
XLA Ops:
  0.0 3.2 %collective-permute-start.1 = (bf16[256,128,128]{2,1,0:T(8,128)(2,1)}, bf16[256,128,128]{2,1,0:T(8,128)(2,1)}, u32[]{:S(2)}, u32[]{:S(2)}) collective-permute-start(bf16[256,128,128]{2,1,0:T(8,128)(2,1)} %param.22), channel_id=1, source_target_pairs={{0,1},{1,0},{2,3},{3,2},{4,5},{5,4},{6,7},{7,6},{8,9},{9,8},{10,11... | collective-permute-start | bytes 25165832 | tf_op jit(solution)/shard_map/ppermute | solution.py:54
  5.4 18.6 %all_to_all.20 = bf16[8,128,128]{2,1,0:T(8,128)(2,1)S(1)} all-to-all(bf16[8,128,128]{2,1,0:T(8,128)(2,1)S(1)} %get-tuple-element.29), channel_id=1, replica_groups={{0,32,64,96,128,160,192,224},{1,33,65,97,129,161,193,225},{2,34,66,98,1..., dimensions={0} | all-to-all | bytes 524288 | tf_op jit(solution)/shard_map/all_to_all | solution.py:252
  24.3 13.8 %all_to_all.21.refs_0_ = bf16[4,8,128,128]{3,2,1,0:T(8,128)(2,1)S(1)} all-to-all(bf16[4,8,128,128]{3,2,1,0:T(8,128)(2,1)S(1)} %broadcast_in_dim.6), channel_id=1, replica_groups={{0,2,4,6},{8,10,12,14},{16,18,20,22},{24,26,28,30},{32,34,36,38},{40,42..., dimensions={0} | all-to-all | bytes 2097152 | tf_op jit(solution)/shard_map/all_to_all | solution.py:253
  39.1 1.6 %collective-permute-start.3 = (bf16[4,8,128,128]{3,2,1,0:T(8,128)(2,1)S(1)}, bf16[4,8,128,128]{3,2,1,0:T(8,128)(2,1)S(1)}, u32[]{:S(2)}, u32[]{:S(2)}) collective-permute-start(bf16[4,8,128,128]{3,2,1,0:T(8,128)(2,1)S(1)} %all_to_all.21.refs_0_), channel_id=1, source_target_pairs={{0,24},{1,7},{2,26},{3,1},{4,28},{5,3},{6,30},{7,5},{8,0},{9,15},{... | collective-permute-start | bytes 3145736 | tf_op jit(solution)/shard_map/ppermute | solution.py:50
  40.8 2.4 %collective-permute-start = (s32[256]{0:T(256)}, s32[256]{0:T(256)S(1)}, u32[]{:S(2)}, u32[]{:S(2)}) collective-permute-start(s32[256]{0:T(256)} %own_row_ref.15), channel_id=1, source_target_pairs={{0,1},{1,0},{2,3},{3,2},{4,5},{5,4},{6,7},{7,6},{8,9},{9,8},{10,11... | collective-permute-start | bytes 3080 | tf_op jit(solution)/shard_map/ppermute | solution.py:54
  43.1 3.4 %copy-done.1 = bf16[256,128,128]{2,1,0:T(8,128)(2,1)S(1)} copy-done((bf16[256,128,128]{2,1,0:T(8,128)(2,1)S(1)}, bf16[256,128,128]{2,1,0:T(8,128)(2,1)}, u32[]{:S(2)}) %copy-start.1) | copy-done | bytes 8388632
  46.5 2.6 %collect.1.refs_1_.refs_2_ = bf16[2,8,4,4,128,128]{5,4,3,2,1,0:T(8,128)(2,1)S(1)} custom-call(s32[1]{0:T(128)} %bitcast.me_ref, bf16[8,4,4,2,128,128]{5,4,3,2,1,0:T(8,128)(2,1)S(1)} %bitcast.8, bf16[8,4,4,2,128,128]{5,4,3,2,1,0:T(8,128)(2,1)} %bitcast.2.other_ref), custom_call_target="tpu_custom_call" | custom-call | bytes 8388608 | tf_op jit(solution)/shard_map/collect/pallas_call | solution.py:155
  50.5 2.7 %collective-permute-done.2.refs_0_ = bf16[4,8,128,128]{3,2,1,0:T(8,128)(2,1)S(1)} collective-permute-done((bf16[4,8,128,128]{3,2,1,0:T(8,128)(2,1)S(1)}, bf16[4,8,128,128]{3,2,1,0:T(8,128)(2,1)S(1)}, u32[]{:S(2)}, u32[]{:S(2)}) %collective-permute-start.2) | collective-permute-done | bytes 1048608 | tf_op jit(solution)/shard_map/ppermute | solution.py:50
  54.5 1.7 %collective-permute-start.5 = (bf16[2,8,128,128]{3,2,1,0:T(8,128)(2,1)S(1)}, bf16[2,8,128,128]{3,2,1,0:T(8,128)(2,1)S(1)}, u32[]{:S(2)}, u32[]{:S(2)}) collective-permute-start(bf16[2,8,128,128]{3,2,1,0:T(8,128)(2,1)S(1)} %slice.19), channel_id=1, source_target_pairs={{0,24},{1,7},{2,26},{3,1},{4,28},{5,3},{6,30},{7,5},{8,0},{9,15},{... | collective-permute-start | bytes 1572872 | tf_op jit(solution)/shard_map/ppermute | solution.py:50
  56.2 4.0 %collective-permute-start.7 = (bf16[2,128,128]{2,1,0:T(8,128)(2,1)S(1)}, bf16[2,128,128]{2,1,0:T(8,128)(2,1)S(1)}, u32[]{:S(2)}, u32[]{:S(2)}) collective-permute-start(bf16[2,128,128]{2,1,0:T(8,128)(2,1)S(1)} %get-tuple-element.35.blocks_ref), channel_id=1, source_target_pairs={{0,1},{1,0},{2,3},{3,2},{4,5},{5,4},{6,7},{7,6},{8,9},{9,8},{10,11... | collective-permute-start | bytes 196616 | tf_op jit(solution)/shard_map/ppermute | solution.py:54
  60.2 4.6 %collective-permute-done.6.behind_ref = bf16[2,128,128]{2,1,0:T(8,128)(2,1)S(1)} collective-permute-done((bf16[2,128,128]{2,1,0:T(8,128)(2,1)S(1)}, bf16[2,128,128]{2,1,0:T(8,128)(2,1)S(1)}, u32[]{:S(2)}, u32[]{:S(2)}) %collective-permute-start.6) | collective-permute-done | bytes 65568 | tf_op jit(solution)/shard_map/ppermute | solution.py:62
  64.8 2.2 %collective-permute-start.9 = (bf16[2,128,128]{2,1,0:T(8,128)(2,1)S(1)}, bf16[2,128,128]{2,1,0:T(8,128)(2,1)S(1)}, u32[]{:S(2)}, u32[]{:S(2)}) collective-permute-start(bf16[2,128,128]{2,1,0:T(8,128)(2,1)S(1)} %get-tuple-element.35.blocks_ref), channel_id=1, source_target_pairs={{0,254},{1,255},{2,0},{3,1},{4,2},{5,3},{6,4},{7,5},{8,6},{9,7},{1... | collective-permute-start | bytes 196616 | tf_op jit(solution)/shard_map/ppermute | solution.py:62
  68.5 2.3 %sparse_sums.2.sparse_ref = f32[128,256]{1,0:T(8,128)S(1)} custom-call(s32[1]{0:T(128)} %bitcast.me_ref, s32[112]{0:T(128)S(1)} %copy-done.8, s32[112]{0:T(128)S(1)} %copy-done.9, s32[1]{0:T(128)S(6)} %copy.20.count_ref, s32[1,4]{1,0:T(1,128)S(1)} %copy-done.10, bf16[2,128,128]{2,1,0:T(8,128)(2,1)S(1)} %get-tuple-element.35.blocks_ref, ...), custom_call_target="tpu_custom_call" | custom-call | flops 469762048 | bytes 3670016 | tf_op jit(solution)/shard_map/sparse_sums/pallas_call | solution.py:128
  74.8 4.5 %collective-permute-start.10 = (f32[128,256]{1,0:T(8,128)S(1)}, f32[128,256]{1,0:T(8,128)S(1)}, u32[]{:S(2)}, u32[]{:S(2)}) collective-permute-start(f32[128,256]{1,0:T(8,128)S(1)} %slice_bitcast_fusion.1), channel_id=1, source_target_pairs={{0,1},{1,0},{2,3},{3,2},{4,5},{5,4},{6,7},{7,6},{8,9},{9,8},{10,11... | collective-permute-start | bytes 393224 | tf_op jit(solution)/shard_map/ppermute | solution.py:54
  81.1 14.4 %all_to_all.22 = bf16[8,128,128]{2,1,0:T(8,128)(2,1)S(1)} all-to-all(bf16[8,128,128]{2,1,0:T(8,128)(2,1)S(1)} %get-tuple-element.41), channel_id=1, replica_groups={{0,32,64,96,128,160,192,224},{1,33,65,97,129,161,193,225},{2,34,66,98,1..., dimensions={0} | all-to-all | bytes 524288 | tf_op jit(solution)/shard_map/all_to_all | solution.py:252
  95.8 12.8 %all_to_all.23.refs_0_ = bf16[4,8,128,128]{3,2,1,0:T(8,128)(2,1)S(1)} all-to-all(bf16[4,8,128,128]{3,2,1,0:T(8,128)(2,1)S(1)} %broadcast_in_dim.8), channel_id=1, replica_groups={{0,2,4,6},{8,10,12,14},{16,18,20,22},{24,26,28,30},{32,34,36,38},{40,42..., dimensions={0} | all-to-all | bytes 2097152 | tf_op jit(solution)/shard_map/all_to_all | solution.py:253
  108.6 1.9 %collective-permute-start.11 = (bf16[4,8,128,128]{3,2,1,0:T(8,128)(2,1)S(1)}, bf16[4,8,128,128]{3,2,1,0:T(8,128)(2,1)S(1)}, u32[]{:S(2)}, u32[]{:S(2)}) collective-permute-start(bf16[4,8,128,128]{3,2,1,0:T(8,128)(2,1)S(1)} %all_to_all.23.refs_0_), channel_id=1, source_target_pairs={{0,8},{1,3},{2,10},{3,5},{4,12},{5,7},{6,14},{7,1},{8,16},{9,11},{... | collective-permute-start | bytes 3145736 | tf_op jit(solution)/shard_map/ppermute | solution.py:50
  112.9 11.1 %collective-permute-done.11.refs_0_ = bf16[4,8,128,128]{3,2,1,0:T(8,128)(2,1)S(1)} collective-permute-done((bf16[4,8,128,128]{3,2,1,0:T(8,128)(2,1)S(1)}, bf16[4,8,128,128]{3,2,1,0:T(8,128)(2,1)S(1)}, u32[]{:S(2)}, u32[]{:S(2)}) %collective-permute-start.11) | collective-permute-done | bytes 1048608 | tf_op jit(solution)/shard_map/ppermute | solution.py:50
  125.1 2.3 %collective-permute-start.14 = (bf16[2,8,128,128]{3,2,1,0:T(8,128)(2,1)S(1)}, bf16[2,8,128,128]{3,2,1,0:T(8,128)(2,1)S(1)}, u32[]{:S(2)}, u32[]{:S(2)}) collective-permute-start(bf16[2,8,128,128]{3,2,1,0:T(8,128)(2,1)S(1)} %slice.22), channel_id=1, source_target_pairs={{0,24},{1,7},{2,26},{3,1},{4,28},{5,3},{6,30},{7,5},{8,0},{9,15},{... | collective-permute-start | bytes 1572872 | tf_op jit(solution)/shard_map/ppermute | solution.py:50
  127.4 4.4 %collective-permute-start.16 = (bf16[2,128,128]{2,1,0:T(8,128)(2,1)S(1)}, bf16[2,128,128]{2,1,0:T(8,128)(2,1)S(1)}, u32[]{:S(2)}, u32[]{:S(2)}) collective-permute-start(bf16[2,128,128]{2,1,0:T(8,128)(2,1)S(1)} %get-tuple-element.46.blocks_ref), channel_id=1, source_target_pairs={{0,1},{1,0},{2,3},{3,2},{4,5},{5,4},{6,7},{7,6},{8,9},{9,8},{10,11... | collective-permute-start | bytes 196616 | tf_op jit(solution)/shard_map/ppermute | solution.py:54
  131.8 4.2 %collective-permute-done.15.behind_ref = bf16[2,128,128]{2,1,0:T(8,128)(2,1)S(1)} collective-permute-done((bf16[2,128,128]{2,1,0:T(8,128)(2,1)S(1)}, bf16[2,128,128]{2,1,0:T(8,128)(2,1)S(1)}, u32[]{:S(2)}, u32[]{:S(2)}) %collective-permute-start.15) | collective-permute-done | bytes 65568 | tf_op jit(solution)/shard_map/ppermute | solution.py:62
  136.0 2.6 %collective-permute-start.18 = (bf16[2,128,128]{2,1,0:T(8,128)(2,1)S(1)}, bf16[2,128,128]{2,1,0:T(8,128)(2,1)S(1)}, u32[]{:S(2)}, u32[]{:S(2)}) collective-permute-start(bf16[2,128,128]{2,1,0:T(8,128)(2,1)S(1)} %get-tuple-element.46.blocks_ref), channel_id=1, source_target_pairs={{0,254},{1,255},{2,0},{3,1},{4,2},{5,3},{6,4},{7,5},{8,6},{9,7},{1... | collective-permute-start | bytes 196616 | tf_op jit(solution)/shard_map/ppermute | solution.py:62
  140.1 2.3 %sparse_sums.3.sparse_ref = f32[128,256]{1,0:T(8,128)S(1)} custom-call(s32[1]{0:T(128)} %bitcast.me_ref, s32[112]{0:T(128)S(1)} %copy-done.8, s32[112]{0:T(128)S(1)} %copy-done.9, s32[1]{0:T(128)S(6)} %copy.20.count_ref, s32[1,4]{1,0:T(1,128)S(1)} %copy-done.10, bf16[2,128,128]{2,1,0:T(8,128)(2,1)S(1)} %get-tuple-element.46.blocks_ref, ...), custom_call_target="tpu_custom_call" | custom-call | flops 469762048 | bytes 3670016 | tf_op jit(solution)/shard_map/sparse_sums/pallas_call | solution.py:128
  146.4 4.5 %collective-permute-start.19 = (f32[128,256]{1,0:T(8,128)S(1)}, f32[128,256]{1,0:T(8,128)S(1)}, u32[]{:S(2)}, u32[]{:S(2)}) collective-permute-start(f32[128,256]{1,0:T(8,128)S(1)} %slice_bitcast_fusion), channel_id=1, source_target_pairs={{0,1},{1,0},{2,3},{3,2},{4,5},{5,4},{6,7},{7,6},{8,9},{9,8},{10,11... | collective-permute-start | bytes 393224 | tf_op jit(solution)/shard_map/ppermute | solution.py:54
  (65 shorter events, 24.4 us)
Async XLA Ops:
  0.0 38.1 %collective-permute-start.1 = (bf16[256,128,128]{2,1,0:T(8,128)(2,1)}, bf16[256,128,128]{2,1,0:T(8,128)(2,1)}, u32[]{:S(2)}, u32[]{:S(2)}) collective-permute-start(bf16[256,128,128]{2,1,0:T(8,128)(2,1)} %param.22), channel_id=1, source_target_pairs={{0,1},{1,0},{2,3},{3,2},{4,5},{5,4},{6,7},{7,6},{8,9},{9,8},{10,11... | collective-permute-start | bytes 25165832 | tf_op jit(solution)/shard_map/ppermute | solution.py:54
  38.1 15.2 %collective-permute-start.2 = (bf16[4,8,128,128]{3,2,1,0:T(8,128)(2,1)S(1)}, bf16[4,8,128,128]{3,2,1,0:T(8,128)(2,1)S(1)}, u32[]{:S(2)}, u32[]{:S(2)}) collective-permute-start(bf16[4,8,128,128]{3,2,1,0:T(8,128)(2,1)S(1)} %all_to_all.21.refs_0_), channel_id=1, source_target_pairs={{0,8},{1,3},{2,10},{3,5},{4,12},{5,7},{6,14},{7,1},{8,16},{9,11},{... | collective-permute-start | bytes 3145736 | tf_op jit(solution)/shard_map/ppermute | solution.py:50
  39.1 14.1 %collective-permute-start.3 = (bf16[4,8,128,128]{3,2,1,0:T(8,128)(2,1)S(1)}, bf16[4,8,128,128]{3,2,1,0:T(8,128)(2,1)S(1)}, u32[]{:S(2)}, u32[]{:S(2)}) collective-permute-start(bf16[4,8,128,128]{3,2,1,0:T(8,128)(2,1)S(1)} %all_to_all.21.refs_0_), channel_id=1, source_target_pairs={{0,24},{1,7},{2,26},{3,1},{4,28},{5,3},{6,30},{7,5},{8,0},{9,15},{... | collective-permute-start | bytes 3145736 | tf_op jit(solution)/shard_map/ppermute | solution.py:50
  40.8 8.4 %collective-permute-start = (s32[256]{0:T(256)}, s32[256]{0:T(256)S(1)}, u32[]{:S(2)}, u32[]{:S(2)}) collective-permute-start(s32[256]{0:T(256)} %own_row_ref.15), channel_id=1, source_target_pairs={{0,1},{1,0},{2,3},{3,2},{4,5},{5,4},{6,7},{7,6},{8,9},{9,8},{10,11... | collective-permute-start | bytes 3080 | tf_op jit(solution)/shard_map/ppermute | solution.py:54
  49.1 19.4 %copy-start = (bf16[112,128,128]{2,1,0:T(8,128)(2,1)S(1)}, bf16[112,128,128]{2,1,0:T(8,128)(2,1)}, u32[]{:S(2)}) copy-start(bf16[112,128,128]{2,1,0:T(8,128)(2,1)} %tiles_ref.3) | copy-start | bytes 11010052
  49.1 19.4 %copy-start.8 = (s32[112]{0:T(128)S(1)}, s32[112]{0:T(128)}, u32[]{:S(2)}) copy-start(s32[112]{0:T(128)} %row_ref.3) | copy-start | bytes 1348
  49.1 19.4 %copy-start.9 = (s32[112]{0:T(128)S(1)}, s32[112]{0:T(128)}, u32[]{:S(2)}) copy-start(s32[112]{0:T(128)} %src_ref.3) | copy-start | bytes 1348
  49.1 19.4 %copy-start.10 = (s32[1,4]{1,0:T(1,128)S(1)}, s32[1,4]{1,0:T(1,128)}, u32[]{:S(2)}) copy-start(s32[1,4]{1,0:T(1,128)} %fetch_ref.3) | copy-start | bytes 52
  53.3 20.2 %collective-permute-start.4 = (bf16[2,8,128,128]{3,2,1,0:T(8,128)(2,1)S(1)}, bf16[2,8,128,128]{3,2,1,0:T(8,128)(2,1)S(1)}, u32[]{:S(2)}, u32[]{:S(2)}) collective-permute-start(bf16[2,8,128,128]{3,2,1,0:T(8,128)(2,1)S(1)} %slice.18), channel_id=1, source_target_pairs={{0,8},{1,3},{2,10},{3,5},{4,12},{5,7},{6,14},{7,1},{8,16},{9,11},{... | collective-permute-start | bytes 1572872 | tf_op jit(solution)/shard_map/ppermute | solution.py:50
  54.5 19.0 %collective-permute-start.5 = (bf16[2,8,128,128]{3,2,1,0:T(8,128)(2,1)S(1)}, bf16[2,8,128,128]{3,2,1,0:T(8,128)(2,1)S(1)}, u32[]{:S(2)}, u32[]{:S(2)}) collective-permute-start(bf16[2,8,128,128]{3,2,1,0:T(8,128)(2,1)S(1)} %slice.19), channel_id=1, source_target_pairs={{0,24},{1,7},{2,26},{3,1},{4,28},{5,3},{6,30},{7,5},{8,0},{9,15},{... | collective-permute-start | bytes 1572872 | tf_op jit(solution)/shard_map/ppermute | solution.py:50
  56.2 8.6 %collective-permute-start.6 = (bf16[2,128,128]{2,1,0:T(8,128)(2,1)S(1)}, bf16[2,128,128]{2,1,0:T(8,128)(2,1)S(1)}, u32[]{:S(2)}, u32[]{:S(2)}) collective-permute-start(bf16[2,128,128]{2,1,0:T(8,128)(2,1)S(1)} %get-tuple-element.35.blocks_ref), channel_id=1, source_target_pairs={{0,2},{1,3},{2,4},{3,5},{4,6},{5,7},{6,8},{7,9},{8,10},{9,11},{10,... | collective-permute-start | bytes 196616 | tf_op jit(solution)/shard_map/ppermute | solution.py:62
  56.2 11.5 %collective-permute-start.7 = (bf16[2,128,128]{2,1,0:T(8,128)(2,1)S(1)}, bf16[2,128,128]{2,1,0:T(8,128)(2,1)S(1)}, u32[]{:S(2)}, u32[]{:S(2)}) collective-permute-start(bf16[2,128,128]{2,1,0:T(8,128)(2,1)S(1)} %get-tuple-element.35.blocks_ref), channel_id=1, source_target_pairs={{0,1},{1,0},{2,3},{3,2},{4,5},{5,4},{6,7},{7,6},{8,9},{9,8},{10,11... | collective-permute-start | bytes 196616 | tf_op jit(solution)/shard_map/ppermute | solution.py:54
  60.2 7.5 %collective-permute-start.8 = (bf16[2,128,128]{2,1,0:T(8,128)(2,1)S(1)}, bf16[2,128,128]{2,1,0:T(8,128)(2,1)S(1)}, u32[]{:S(2)}, u32[]{:S(2)}) collective-permute-start(bf16[2,128,128]{2,1,0:T(8,128)(2,1)S(1)} %get-tuple-element.35.blocks_ref), channel_id=1, source_target_pairs={{0,255},{1,2},{2,1},{3,4},{4,3},{5,6},{6,5},{7,8},{8,7},{9,10},{10... | collective-permute-start | bytes 196616 | tf_op jit(solution)/shard_map/ppermute | solution.py:58
  64.8 3.7 %collective-permute-start.9 = (bf16[2,128,128]{2,1,0:T(8,128)(2,1)S(1)}, bf16[2,128,128]{2,1,0:T(8,128)(2,1)S(1)}, u32[]{:S(2)}, u32[]{:S(2)}) collective-permute-start(bf16[2,128,128]{2,1,0:T(8,128)(2,1)S(1)} %get-tuple-element.35.blocks_ref), channel_id=1, source_target_pairs={{0,254},{1,255},{2,0},{3,1},{4,2},{5,3},{6,4},{7,5},{8,6},{9,7},{1... | collective-permute-start | bytes 196616 | tf_op jit(solution)/shard_map/ppermute | solution.py:62
  74.8 5.5 %collective-permute-start.10 = (f32[128,256]{1,0:T(8,128)S(1)}, f32[128,256]{1,0:T(8,128)S(1)}, u32[]{:S(2)}, u32[]{:S(2)}) collective-permute-start(f32[128,256]{1,0:T(8,128)S(1)} %slice_bitcast_fusion.1), channel_id=1, source_target_pairs={{0,1},{1,0},{2,3},{3,2},{4,5},{5,4},{6,7},{7,6},{8,9},{9,8},{10,11... | collective-permute-start | bytes 393224 | tf_op jit(solution)/shard_map/ppermute | solution.py:54
  108.6 15.5 %collective-permute-start.11 = (bf16[4,8,128,128]{3,2,1,0:T(8,128)(2,1)S(1)}, bf16[4,8,128,128]{3,2,1,0:T(8,128)(2,1)S(1)}, u32[]{:S(2)}, u32[]{:S(2)}) collective-permute-start(bf16[4,8,128,128]{3,2,1,0:T(8,128)(2,1)S(1)} %all_to_all.23.refs_0_), channel_id=1, source_target_pairs={{0,8},{1,3},{2,10},{3,5},{4,12},{5,7},{6,14},{7,1},{8,16},{9,11},{... | collective-permute-start | bytes 3145736 | tf_op jit(solution)/shard_map/ppermute | solution.py:50
  110.5 13.9 %collective-permute-start.12 = (bf16[4,8,128,128]{3,2,1,0:T(8,128)(2,1)S(1)}, bf16[4,8,128,128]{3,2,1,0:T(8,128)(2,1)S(1)}, u32[]{:S(2)}, u32[]{:S(2)}) collective-permute-start(bf16[4,8,128,128]{3,2,1,0:T(8,128)(2,1)S(1)} %all_to_all.23.refs_0_), channel_id=1, source_target_pairs={{0,24},{1,7},{2,26},{3,1},{4,28},{5,3},{6,30},{7,5},{8,0},{9,15},{... | collective-permute-start | bytes 3145736 | tf_op jit(solution)/shard_map/ppermute | solution.py:50
  124.5 20.6 %collective-permute-start.13 = (bf16[2,8,128,128]{3,2,1,0:T(8,128)(2,1)S(1)}, bf16[2,8,128,128]{3,2,1,0:T(8,128)(2,1)S(1)}, u32[]{:S(2)}, u32[]{:S(2)}) collective-permute-start(bf16[2,8,128,128]{3,2,1,0:T(8,128)(2,1)S(1)} %slice.21), channel_id=1, source_target_pairs={{0,8},{1,3},{2,10},{3,5},{4,12},{5,7},{6,14},{7,1},{8,16},{9,11},{... | collective-permute-start | bytes 1572872 | tf_op jit(solution)/shard_map/ppermute | solution.py:50
  125.1 20.0 %collective-permute-start.14 = (bf16[2,8,128,128]{3,2,1,0:T(8,128)(2,1)S(1)}, bf16[2,8,128,128]{3,2,1,0:T(8,128)(2,1)S(1)}, u32[]{:S(2)}, u32[]{:S(2)}) collective-permute-start(bf16[2,8,128,128]{3,2,1,0:T(8,128)(2,1)S(1)} %slice.22), channel_id=1, source_target_pairs={{0,24},{1,7},{2,26},{3,1},{4,28},{5,3},{6,30},{7,5},{8,0},{9,15},{... | collective-permute-start | bytes 1572872 | tf_op jit(solution)/shard_map/ppermute | solution.py:50
  127.4 8.6 %collective-permute-start.15 = (bf16[2,128,128]{2,1,0:T(8,128)(2,1)S(1)}, bf16[2,128,128]{2,1,0:T(8,128)(2,1)S(1)}, u32[]{:S(2)}, u32[]{:S(2)}) collective-permute-start(bf16[2,128,128]{2,1,0:T(8,128)(2,1)S(1)} %get-tuple-element.46.blocks_ref), channel_id=1, source_target_pairs={{0,2},{1,3},{2,4},{3,5},{4,6},{5,7},{6,8},{7,9},{8,10},{9,11},{10,... | collective-permute-start | bytes 196616 | tf_op jit(solution)/shard_map/ppermute | solution.py:62
  127.4 11.2 %collective-permute-start.16 = (bf16[2,128,128]{2,1,0:T(8,128)(2,1)S(1)}, bf16[2,128,128]{2,1,0:T(8,128)(2,1)S(1)}, u32[]{:S(2)}, u32[]{:S(2)}) collective-permute-start(bf16[2,128,128]{2,1,0:T(8,128)(2,1)S(1)} %get-tuple-element.46.blocks_ref), channel_id=1, source_target_pairs={{0,1},{1,0},{2,3},{3,2},{4,5},{5,4},{6,7},{7,6},{8,9},{9,8},{10,11... | collective-permute-start | bytes 196616 | tf_op jit(solution)/shard_map/ppermute | solution.py:54
  131.8 6.8 %collective-permute-start.17 = (bf16[2,128,128]{2,1,0:T(8,128)(2,1)S(1)}, bf16[2,128,128]{2,1,0:T(8,128)(2,1)S(1)}, u32[]{:S(2)}, u32[]{:S(2)}) collective-permute-start(bf16[2,128,128]{2,1,0:T(8,128)(2,1)S(1)} %get-tuple-element.46.blocks_ref), channel_id=1, source_target_pairs={{0,255},{1,2},{2,1},{3,4},{4,3},{5,6},{6,5},{7,8},{8,7},{9,10},{10... | collective-permute-start | bytes 196616 | tf_op jit(solution)/shard_map/ppermute | solution.py:58
  136.0 4.1 %collective-permute-start.18 = (bf16[2,128,128]{2,1,0:T(8,128)(2,1)S(1)}, bf16[2,128,128]{2,1,0:T(8,128)(2,1)S(1)}, u32[]{:S(2)}, u32[]{:S(2)}) collective-permute-start(bf16[2,128,128]{2,1,0:T(8,128)(2,1)S(1)} %get-tuple-element.46.blocks_ref), channel_id=1, source_target_pairs={{0,254},{1,255},{2,0},{3,1},{4,2},{5,3},{6,4},{7,5},{8,6},{9,7},{1... | collective-permute-start | bytes 196616 | tf_op jit(solution)/shard_map/ppermute | solution.py:62
  146.4 5.5 %collective-permute-start.19 = (f32[128,256]{1,0:T(8,128)S(1)}, f32[128,256]{1,0:T(8,128)S(1)}, u32[]{:S(2)}, u32[]{:S(2)}) collective-permute-start(f32[128,256]{1,0:T(8,128)S(1)} %slice_bitcast_fusion), channel_id=1, source_target_pairs={{0,1},{1,0},{2,3},{3,2},{4,5},{5,4},{6,7},{7,6},{8,9},{9,8},{10,11... | collective-permute-start | bytes 393224 | tf_op jit(solution)/shard_map/ppermute | solution.py:54
  (7 other events, 32.1 us)

commit v4 on v3

--- a/solution.py
+++ b/solution.py
@@ -18,6 +18,7 @@
 NZ, NX, NY, NC = 8, 4, 4, 2
 SHARDS = NZ * NX * NY * NC
 SIDE = 4
+TURNS = (0, SIDE - 1, 1, 2)
 
 SMEM = pl.BlockSpec(memory_space=pltpu.SMEM)
 VMEM = pl.BlockSpec(memory_space=pltpu.VMEM)
@@ -36,17 +37,12 @@
     return [[index_of(z, x, y, core) for z in range(NZ)] for x in range(NX) for y in range(NY) for core in range(NC)]
 
 
-def groups_crossways():
-    return [[index_of(z, x, y, 0) for y in range(NY)] for z in range(NZ) for x in range(NX)] + [
-        [index_of(z, x, y, 1) for x in range(NX)] for z in range(NZ) for y in range(NY)
-    ]
-
-
-def ring_step(array, by):
+def step(array, by, across):
     pairs = []
     for index in range(SHARDS):
         z, x, y, core = place(index)
-        pairs.append((index, index_of(z, x + (by if core == 0 else 0), y + (by if core == 1 else 0), core)))
+        along_x = (core == 0) != across
+        pairs.append((index, index_of(z, x + (by if along_x else 0), y + (0 if along_x else by), core)))
     return lax.ppermute(array, "blk", pairs)
 
 
@@ -114,14 +110,14 @@
 
     group = 8
 
-    def step(at, _):
+    def add(at, _):
         first = at * group
         left = jnp.concatenate([tiles_ref[first + k] for k in range(group)], axis=1)
         right = jnp.concatenate([placed_ref[which(first + k)] for k in range(group)], axis=0)
         out_ref[...] += jnp.dot(left, right, preferred_element_type=jnp.float32)
         return 0
 
-    lax.fori_loop(0, (live + group - 1) // group, step, 0)
+    lax.fori_loop(0, (live + group - 1) // group, add, 0)
 
 
 def sparse_sums(me, row, src, count, wanted, blocks, fetched, tiles):
@@ -164,48 +160,47 @@
     )(me, own.reshape(shape), other.reshape(shape))
 
 
-def dense_kernel(counts, me_ref, shift_ref, own_row_ref, other_row_ref, *refs):
-    chunk_refs, (tiles_ref, start_ref, out_ref) = refs[: len(counts)], refs[len(counts) :]
+def dense_kernel(sides, me_ref, shift_ref, *refs):
+    count = len(sides)
+    row_refs, (chunk_ref, tiles_ref), start_refs, out_refs = refs[:count], refs[count : count + 2], refs[count + 2 : -count], refs[-count:]
     me = me_ref[0]
     x, y, core = me // (NY * NC) % NX, me // NC % NY, me % NC
     fixed = (jnp.where(core == 0, x, y) + shift_ref[0]) % SIDE
-    out_ref[...] = start_ref[...]
-    step = 0
-    for chunk_ref, count in zip(chunk_refs, counts):
-        for k in range(count):
-            at_x = jnp.where(core == 0, fixed, step)
-            at_y = jnp.where(core == 0, step, fixed)
-            sources = [((z * NX + at_x) * NY + at_y) * NC + core for z in range(NZ)]
-            for side, row_ref in enumerate((own_row_ref, other_row_ref)):
-                left = jnp.concatenate([tiles_ref[side, z, at_x, at_y] for z in range(NZ)], axis=1)
-                right = jnp.concatenate(
-                    [placed_pair(chunk_ref[k, z], row_ref[source]) for z, source in enumerate(sources)], axis=0
-                )
-                out_ref[side] += jnp.dot(left, right, preferred_element_type=jnp.float32)
-            step += 1
-
-
-def dense_part(me, shift, rows, chunks, tiles, start):
-    counts = tuple(chunk.shape[0] for chunk in chunks)
-    steps = sum(counts)
-    return pl.pallas_call(
-        functools.partial(dense_kernel, counts),
-        out_shape=jax.ShapeDtypeStruct((NC, TILE, NB * F), jnp.float32),
-        in_specs=[SMEM] * 4 + [VMEM] * (len(chunks) + 2),
-        out_specs=VMEM,
+    for start_ref, out_ref in zip(start_refs, out_refs):
+        out_ref[...] = start_ref[...]
+    for k, turn in enumerate(TURNS):
+        along = (jnp.where(core == 0, y, x) + turn) % SIDE
+        at_x = jnp.where(core == 0, fixed, along)
+        at_y = jnp.where(core == 0, along, fixed)
+        sources = [((z * NX + at_x) * NY + at_y) * NC + core for z in range(NZ)]
+        for side, row_ref, out_ref in zip(sides, row_refs, out_refs):
+            left = jnp.concatenate([tiles_ref[side, z, at_x, at_y] for z in range(NZ)], axis=1)
+            right = jnp.concatenate(
+                [placed_pair(chunk_ref[k, z], row_ref[source]) for z, source in enumerate(sources)], axis=0
+            )
+            out_ref[...] += jnp.dot(left, right, preferred_element_type=jnp.float32)
+
+
+def dense_part(me, shift, rows, chunk, tiles, starts, sides=(0, 1)):
+    count = len(sides)
+    return pl.pallas_call(
+        functools.partial(dense_kernel, sides),
+        out_shape=(jax.ShapeDtypeStruct((TILE, NB * F), jnp.float32),) * count,
+        in_specs=[SMEM] * (2 + count) + [VMEM] * (2 + count),
+        out_specs=(VMEM,) * count,
         compiler_params=pltpu.CompilerParams(vmem_limit_bytes=16 << 20),
         cost_estimate=pl.CostEstimate(
-            flops=8 * steps * NZ * TILE**3, bytes_accessed=6 * steps * NZ * TILE**2, transcendentals=0
+            flops=4 * count * SIDE * NZ * TILE**3, bytes_accessed=3 * count * SIDE * NZ * TILE**2, transcendentals=0
         ),
         name="dense_part",
-    )(me, jnp.array([shift], jnp.int32), *rows, *chunks, tiles, start)
+    )(me, jnp.array([shift], jnp.int32), *(rows[side] for side in sides), chunk, tiles, *starts)
 
 
 def finish_kernel(wide, me_ref, hub_ref, dense_ref, other_ref, sparse_ref, weight_ref, out_ref, *copies):
     blocks = []
     for block in range(NB):
         columns = slice(block * F, (block + 1) * F)
-        summed = dense_ref[0, :, columns] + other_ref[:, columns] + sparse_ref[:, columns]
+        summed = dense_ref[:, columns] + other_ref[:, columns] + sparse_ref[:, columns]
         projected = jnp.dot(
             summed, weight_ref[...], precision=lax.Precision.HIGHEST, preferred_element_type=jnp.float32
         )
@@ -246,35 +241,29 @@
     me = lax.axis_index("blk").astype(jnp.int32).reshape(1)
     rows = [dense_row, swap_cores(dense_row)]
     other_tiles = swap_cores(dense_tiles)
-    zeros = jnp.zeros((NC, TILE, NB * F), jnp.float32)
+    zeros = jnp.zeros((TILE, NB * F), jnp.float32)
 
     def propagate(blocks, copies, weight, dtype, wide, tiles=None):
         column = lax.all_to_all(copies, "blk", 0, 0, axis_index_groups=groups_along_z(), tiled=True)
-        plane = lax.all_to_all(
-            jnp.broadcast_to(column[None], (SIDE, NZ, TILE, F)),
-            "blk",
-            0,
-            0,
-            axis_index_groups=groups_crossways(),
-            tiled=True,
-        )
+        sides = [step(column, 1, True), step(column, -1, True), step(column, 2, True)]
+        plane = jnp.stack([column, *sides])
         if tiles is None:
             blocks, plane, others = lax.optimization_barrier((blocks, plane, other_tiles))
             tiles = collect(me, dense_tiles, others)
         else:
             blocks, plane = lax.optimization_barrier((blocks, plane))
-        behind = ring_step(plane, 1)
-        ahead = ring_step(plane, -1)
+        behind = step(plane, 1, False)
+        ahead = step(plane, -1, False)
+        far = step(plane, 2, False)
         fetched = [from_behind(blocks, 2), swap_cores(blocks), swap_across(blocks), from_behind(blocks, -2)]
-        total = dense_part(me, 0, rows, [plane], tiles, zeros)
-        behind, ahead, total = lax.optimization_barrier((behind, ahead, total))
-        far = (ring_step(behind[: SIDE // 2], 1), ring_step(ahead[SIDE // 2 :], -1))
-        total = dense_part(me, SIDE - 1, rows, [behind], tiles, total)
-        total = dense_part(me, 1, rows, [ahead], tiles, total)
+        totals = dense_part(me, 0, rows, plane, tiles, (zeros, zeros))
         sparse = sparse_sums(me, sparse_row, sparse_src, sparse_count, fetch_list, blocks, fetched, sparse_tiles)
-        far, total, sparse = lax.optimization_barrier((far, total, sparse))
-        total = dense_part(me, 2, rows, far, tiles, total)
-        returned = swap_cores(total[1])
+        totals = dense_part(me, SIDE - 1, rows, behind, tiles, totals)
+        totals = dense_part(me, 1, rows, ahead, tiles, totals)
+        far, own, other, sparse = lax.optimization_barrier((far, *totals, sparse))
+        (other,) = dense_part(me, 2, rows, far, tiles, (other,), (1,))
+        returned = swap_cores(other)
+        (total,) = dense_part(me, 2, rows, far, tiles, (own,), (0,))
         return *finish(me, hub_block, total, returned, sparse, weight, dtype, wide), tiles
 
     blocks, copies = enter(me, hub_block, features)

time: 154 us -> 153 us (level)
  the two profiles are of different devices: /device:TPU:1 before, /device:TPU:5 now
where the time goes in v4:
time: 153 us
  starting transfers between devices  43.4 us (28%)
  waiting for transfers between devices  43.4 us (28%)
  blocking collectives  35.1 us (23%)
  Pallas kernels  24 us (16%)
  local copies, waits for them, and re-layouts  5.65 us (4%)
    all_to_all x2, blocking collectives, propagate(): lax.all_to_all(copies, 'blk', 0, 0, axis_index_groups=groups_along_z(), t...  35.1 us
    ppermute x4, starting transfers between devices, from_behind(): lax.ppermute(array, 'blk', [(i, (i + by) % SHARDS) for i in range(SHARDS)])  17.2 us
    ppermute x4, waiting for transfers between devices, from_behind(): lax.ppermute(array, 'blk', [(i, (i + by) % SHARDS) for i in range(SHARDS)])  16.8 us
    ppermute x12, starting transfers between devices, step(): return lax.ppermute(array, 'blk', pairs)  14.5 us
    ppermute x2, waiting for transfers between devices, swap_across(): lax.ppermute(array, 'blk', [(i, (i + (1 if i % 2 else -1)) % SHARDS) for...  13.9 us
    ppermute x12, waiting for transfers between devices, step(): return lax.ppermute(array, 'blk', pairs)  12.2 us
    pallas_call x10, Pallas kernels, dense_part(): pl.pallas_call(functools.partial(dense_kernel, sides), out_shape=(jax.Sha...  12.1 us
    ppermute x6, starting transfers between devices, swap_cores(): return lax.ppermute(array, 'blk', [(i, i ^ 1) for i in range(SHARDS)])  10.7 us
  transfers between devices with their start and end apart: 24, of which 10 were waited for; matrix products, arithmetic and copies ran while one was open for 0% of the time, Pallas kernels for 13%

profile of v4, /device:TPU:5, one launch (start us, length us, event | category | flops | bytes accessed | tf_op | source)
XLA Modules:
  0.0 152.9 jit_solution(10594240319937329716)
XLA Ops:
  2.9 20.3 %all_to_all.10 = bf16[8,128,128]{2,1,0:T(8,128)(2,1)S(1)} all-to-all(bf16[8,128,128]{2,1,0:T(8,128)(2,1)S(1)} %get-tuple-element.35), channel_id=1, replica_groups={{0,32,64,96,128,160,192,224},{1,33,65,97,129,161,193,225},{2,34,66,98,1..., dimensions={0} | all-to-all | bytes 524288 | tf_op jit(solution)/shard_map/all_to_all | solution.py:247
  24.7 1.4 collective-permute-start.2
  26.1 2.6 %collective-permute-done = bf16[8,128,128]{2,1,0:T(8,128)(2,1)S(1)} collective-permute-done((bf16[8,128,128]{2,1,0:T(8,128)(2,1)S(1)}, bf16[8,128,128]{2,1,0:T(8,128)(2,1)S(1)}, u32[]{:S(2)}, u32[]{:S(2)}) %collective-permute-start) | collective-permute-done | bytes 262176 | tf_op jit(solution)/shard_map/ppermute | solution.py:46
  29.6 1.8 %collective-permute-done.2 = bf16[8,128,128]{2,1,0:T(8,128)(2,1)S(1)} collective-permute-done((bf16[8,128,128]{2,1,0:T(8,128)(2,1)S(1)}, bf16[8,128,128]{2,1,0:T(8,128)(2,1)S(1)}, u32[]{:S(2)}, u32[]{:S(2)}) %collective-permute-start.2) | collective-permute-done | bytes 262176 | tf_op jit(solution)/shard_map/ppermute | solution.py:46
  32.9 1.8 %collective-permute-start.6 = (bf16[4,8,128,128]{3,2,1,0:T(8,128)(2,1)S(1)}, bf16[4,8,128,128]{3,2,1,0:T(8,128)(2,1)S(1)}, u32[]{:S(2)}, u32[]{:S(2)}) collective-permute-start(bf16[4,8,128,128]{3,2,1,0:T(8,128)(2,1)S(1)} %pad_maximum_fusion.refs_2_), channel_id=1, source_target_pairs={{0,24},{1,7},{2,26},{3,1},{4,28},{5,3},{6,30},{7,5},{8,0},{9,15},{... | collective-permute-start | bytes 3145736 | tf_op jit(solution)/shard_map/ppermute | solution.py:46
  34.7 1.6 %collective-permute-start.4 = (bf16[4,8,128,128]{3,2,1,0:T(8,128)(2,1)S(1)}, bf16[4,8,128,128]{3,2,1,0:T(8,128)(2,1)S(1)}, u32[]{:S(2)}, u32[]{:S(2)}) collective-permute-start(bf16[4,8,128,128]{3,2,1,0:T(8,128)(2,1)S(1)} %pad_maximum_fusion.refs_2_), channel_id=1, source_target_pairs={{0,16},{1,5},{2,18},{3,7},{4,20},{5,1},{6,22},{7,3},{8,24},{9,13},... | collective-permute-start | bytes 3145736 | tf_op jit(solution)/shard_map/ppermute | solution.py:46
  36.3 3.0 %collective-permute-start.5 = (s32[256]{0:T(256)}, s32[256]{0:T(256)S(1)}, u32[]{:S(2)}, u32[]{:S(2)}) collective-permute-start(s32[256]{0:T(256)} %refs_0_.15), channel_id=1, source_target_pairs={{0,1},{1,0},{2,3},{3,2},{4,5},{5,4},{6,7},{7,6},{8,9},{9,8},{10,11... | collective-permute-start | bytes 3080 | tf_op jit(solution)/shard_map/ppermute | solution.py:50
  40.3 2.4 %collective-permute-start.11 = (bf16[2,128,128]{2,1,0:T(8,128)(2,1)S(1)}, bf16[2,128,128]{2,1,0:T(8,128)(2,1)S(1)}, u32[]{:S(2)}, u32[]{:S(2)}) collective-permute-start(bf16[2,128,128]{2,1,0:T(8,128)(2,1)S(1)} %get-tuple-element.44.blocks_ref), channel_id=1, source_target_pairs={{0,254},{1,255},{2,0},{3,1},{4,2},{5,3},{6,4},{7,5},{8,6},{9,7},{1... | collective-permute-start | bytes 196616 | tf_op jit(solution)/shard_map/ppermute | solution.py:58
  42.7 13.9 %collective-permute-done.10.across_ref = bf16[2,128,128]{2,1,0:T(8,128)(2,1)S(1)} collective-permute-done((bf16[2,128,128]{2,1,0:T(8,128)(2,1)S(1)}, bf16[2,128,128]{2,1,0:T(8,128)(2,1)S(1)}, u32[]{:S(2)}, u32[]{:S(2)}) %collective-permute-start.10) | collective-permute-done | bytes 65568 | tf_op jit(solution)/shard_map/ppermute | solution.py:54
  56.6 1.5 %collective-permute-start.8 = (bf16[2,128,128]{2,1,0:T(8,128)(2,1)S(1)}, bf16[2,128,128]{2,1,0:T(8,128)(2,1)S(1)}, u32[]{:S(2)}, u32[]{:S(2)}) collective-permute-start(bf16[2,128,128]{2,1,0:T(8,128)(2,1)S(1)} %get-tuple-element.44.blocks_ref), channel_id=1, source_target_pairs={{0,2},{1,3},{2,4},{3,5},{4,6},{5,7},{6,8},{7,9},{8,10},{9,11},{10,... | collective-permute-start | bytes 196616 | tf_op jit(solution)/shard_map/ppermute | solution.py:58
  58.2 2.1 %collective-permute-done.11.ahead_ref = bf16[2,128,128]{2,1,0:T(8,128)(2,1)S(1)} collective-permute-done((bf16[2,128,128]{2,1,0:T(8,128)(2,1)S(1)}, bf16[2,128,128]{2,1,0:T(8,128)(2,1)S(1)}, u32[]{:S(2)}, u32[]{:S(2)}) %collective-permute-start.11) | collective-permute-done | bytes 65568 | tf_op jit(solution)/shard_map/ppermute | solution.py:58
  60.3 2.9 %collective-permute-start.9 = (bf16[2,128,128]{2,1,0:T(8,128)(2,1)S(1)}, bf16[2,128,128]{2,1,0:T(8,128)(2,1)S(1)}, u32[]{:S(2)}, u32[]{:S(2)}) collective-permute-start(bf16[2,128,128]{2,1,0:T(8,128)(2,1)S(1)} %get-tuple-element.44.blocks_ref), channel_id=1, source_target_pairs={{0,1},{1,0},{2,3},{3,2},{4,5},{5,4},{6,7},{7,6},{8,9},{9,8},{10,11... | collective-permute-start | bytes 196616 | tf_op jit(solution)/shard_map/ppermute | solution.py:50
  63.9 3.4 %copy-done.1 = bf16[256,128,128]{2,1,0:T(8,128)(2,1)S(1)} copy-done((bf16[256,128,128]{2,1,0:T(8,128)(2,1)S(1)}, bf16[256,128,128]{2,1,0:T(8,128)(2,1)}, u32[]{:S(2)}) %copy-start.1) | copy-done | bytes 8388632
  67.3 2.6 %collect.1.refs_3_.refs_2_ = bf16[2,8,4,4,128,128]{5,4,3,2,1,0:T(8,128)(2,1)S(1)} custom-call(s32[1]{0:T(128)} %bitcast.me_ref, bf16[8,4,4,2,128,128]{5,4,3,2,1,0:T(8,128)(2,1)S(1)} %bitcast.12, bf16[8,4,4,2,128,128]{5,4,3,2,1,0:T(8,128)(2,1)} %bitcast.6.other_ref), custom_call_target="tpu_custom_call" | custom-call | bytes 8388608 | tf_op jit(solution)/shard_map/collect/pallas_call | solution.py:151
  71.9 3.2 %sparse_sums.2.sparse_ref = f32[128,256]{1,0:T(8,128)S(1)} custom-call(s32[1]{0:T(128)} %bitcast.me_ref, s32[112]{0:T(128)S(1)} %copy-done.8, s32[112]{0:T(128)S(1)} %copy-done.9, s32[1]{0:T(128)S(6)} %copy.22.count_ref, s32[1,4]{1,0:T(1,128)S(1)} %copy-done.10, bf16[2,128,128]{2,1,0:T(8,128)(2,1)S(1)} %get-tuple-element.44.blocks_ref, ...), custom_call_target="tpu_custom_call" | custom-call | flops 469762048 | bytes 3670016 | tf_op jit(solution)/shard_map/sparse_sums/pallas_call | solution.py:124
  81.3 14.8 %all_to_all.11 = bf16[8,128,128]{2,1,0:T(8,128)(2,1)S(1)} all-to-all(bf16[8,128,128]{2,1,0:T(8,128)(2,1)S(1)} %get-tuple-element.50), channel_id=1, replica_groups={{0,32,64,96,128,160,192,224},{1,33,65,97,129,161,193,225},{2,34,66,98,1..., dimensions={0} | all-to-all | bytes 524288 | tf_op jit(solution)/shard_map/all_to_all | solution.py:247
  97.7 5.4 %collective-permute-done.15 = bf16[8,128,128]{2,1,0:T(8,128)(2,1)S(1)} collective-permute-done((bf16[8,128,128]{2,1,0:T(8,128)(2,1)S(1)}, bf16[8,128,128]{2,1,0:T(8,128)(2,1)S(1)}, u32[]{:S(2)}, u32[]{:S(2)}) %collective-permute-start.15) | collective-permute-done | bytes 262176 | tf_op jit(solution)/shard_map/ppermute | solution.py:46
  103.1 1.4 collective-permute-done.13
  104.8 4.1 %collective-permute-start.17 = (bf16[4,8,128,128]{3,2,1,0:T(8,128)(2,1)S(1)}, bf16[4,8,128,128]{3,2,1,0:T(8,128)(2,1)S(1)}, u32[]{:S(2)}, u32[]{:S(2)}) collective-permute-start(bf16[4,8,128,128]{3,2,1,0:T(8,128)(2,1)S(1)} %pad_maximum_fusion.1.refs_2_), channel_id=1, source_target_pairs={{0,24},{1,7},{2,26},{3,1},{4,28},{5,3},{6,30},{7,5},{8,0},{9,15},{... | collective-permute-start | bytes 3145736 | tf_op jit(solution)/shard_map/ppermute | solution.py:46
  110.8 3.8 %collective-permute-start.20 = (bf16[2,128,128]{2,1,0:T(8,128)(2,1)S(1)}, bf16[2,128,128]{2,1,0:T(8,128)(2,1)S(1)}, u32[]{:S(2)}, u32[]{:S(2)}) collective-permute-start(bf16[2,128,128]{2,1,0:T(8,128)(2,1)S(1)} %get-tuple-element.58.blocks_ref), channel_id=1, source_target_pairs={{0,1},{1,0},{2,3},{3,2},{4,5},{5,4},{6,7},{7,6},{8,9},{9,8},{10,11... | collective-permute-start | bytes 196616 | tf_op jit(solution)/shard_map/ppermute | solution.py:50
  114.6 14.6 %collective-permute-done.19.behind_ref = bf16[2,128,128]{2,1,0:T(8,128)(2,1)S(1)} collective-permute-done((bf16[2,128,128]{2,1,0:T(8,128)(2,1)S(1)}, bf16[2,128,128]{2,1,0:T(8,128)(2,1)S(1)}, u32[]{:S(2)}, u32[]{:S(2)}) %collective-permute-start.19) | collective-permute-done | bytes 65568 | tf_op jit(solution)/shard_map/ppermute | solution.py:58
  129.2 12.4 %collective-permute-start.22 = (bf16[2,128,128]{2,1,0:T(8,128)(2,1)S(1)}, bf16[2,128,128]{2,1,0:T(8,128)(2,1)S(1)}, u32[]{:S(2)}, u32[]{:S(2)}) collective-permute-start(bf16[2,128,128]{2,1,0:T(8,128)(2,1)S(1)} %get-tuple-element.58.blocks_ref), channel_id=1, source_target_pairs={{0,254},{1,255},{2,0},{3,1},{4,2},{5,3},{6,4},{7,5},{8,6},{9,7},{1... | collective-permute-start | bytes 196616 | tf_op jit(solution)/shard_map/ppermute | solution.py:58
  142.9 3.2 %sparse_sums.3.sparse_ref = f32[128,256]{1,0:T(8,128)S(1)} custom-call(s32[1]{0:T(128)} %bitcast.me_ref, s32[112]{0:T(128)S(1)} %copy-done.8, s32[112]{0:T(128)S(1)} %copy-done.9, s32[1]{0:T(128)S(6)} %copy.22.count_ref, s32[1,4]{1,0:T(1,128)S(1)} %copy-done.10, bf16[2,128,128]{2,1,0:T(8,128)(2,1)S(1)} %get-tuple-element.58.blocks_ref, ...), custom_call_target="tpu_custom_call" | custom-call | flops 469762048 | bytes 3670016 | tf_op jit(solution)/shard_map/sparse_sums/pallas_call | solution.py:124
  151.4 1.5 finish.3
  (67 shorter events, 26.1 us)
Async XLA Ops:
  0.0 31.5 %collective-permute-start.3 = (bf16[256,128,128]{2,1,0:T(8,128)(2,1)}, bf16[256,128,128]{2,1,0:T(8,128)(2,1)}, u32[]{:S(2)}, u32[]{:S(2)}) collective-permute-start(bf16[256,128,128]{2,1,0:T(8,128)(2,1)} %param.24), channel_id=1, source_target_pairs={{0,1},{1,0},{2,3},{3,2},{4,5},{5,4},{6,7},{7,6},{8,9},{9,8},{10,11... | collective-permute-start | bytes 25165832 | tf_op jit(solution)/shard_map/ppermute | solution.py:50
  23.2 5.5 %collective-permute-start = (bf16[8,128,128]{2,1,0:T(8,128)(2,1)S(1)}, bf16[8,128,128]{2,1,0:T(8,128)(2,1)S(1)}, u32[]{:S(2)}, u32[]{:S(2)}) collective-permute-start(bf16[8,128,128]{2,1,0:T(8,128)(2,1)S(1)} %all_to_all.10), channel_id=1, source_target_pairs={{0,2},{1,9},{2,4},{3,11},{4,6},{5,13},{6,0},{7,15},{8,10},{9,17},{... | collective-permute-start | bytes 786440 | tf_op jit(solution)/shard_map/ppermute | solution.py:46
  24.1 5.5 %collective-permute-start.1 = (bf16[8,128,128]{2,1,0:T(8,128)(2,1)S(1)}, bf16[8,128,128]{2,1,0:T(8,128)(2,1)S(1)}, u32[]{:S(2)}, u32[]{:S(2)}) collective-permute-start(bf16[8,128,128]{2,1,0:T(8,128)(2,1)S(1)} %all_to_all.10), channel_id=1, source_target_pairs={{0,6},{1,25},{2,0},{3,27},{4,2},{5,29},{6,4},{7,31},{8,14},{9,1},{... | collective-permute-start | bytes 786440 | tf_op jit(solution)/shard_map/ppermute | solution.py:46
  24.7 6.7 %collective-permute-start.2 = (bf16[8,128,128]{2,1,0:T(8,128)(2,1)S(1)}, bf16[8,128,128]{2,1,0:T(8,128)(2,1)S(1)}, u32[]{:S(2)}, u32[]{:S(2)}) collective-permute-start(bf16[8,128,128]{2,1,0:T(8,128)(2,1)S(1)} %all_to_all.10), channel_id=1, source_target_pairs={{0,4},{1,17},{2,6},{3,19},{4,0},{5,21},{6,2},{7,23},{8,12},{9,25},... | collective-permute-start | bytes 786440 | tf_op jit(solution)/shard_map/ppermute | solution.py:46
  31.5 43.6 %collective-permute-start.7 = (bf16[4,8,128,128]{3,2,1,0:T(8,128)(2,1)S(1)}, bf16[4,8,128,128]{3,2,1,0:T(8,128)(2,1)S(1)}, u32[]{:S(2)}, u32[]{:S(2)}) collective-permute-start(bf16[4,8,128,128]{3,2,1,0:T(8,128)(2,1)S(1)} %pad_maximum_fusion.refs_2_), channel_id=1, source_target_pairs={{0,8},{1,3},{2,10},{3,5},{4,12},{5,7},{6,14},{7,1},{8,16},{9,11},{... | collective-permute-start | bytes 3145736 | tf_op jit(solution)/shard_map/ppermute | solution.py:46
  32.9 43.5 %collective-permute-start.6 = (bf16[4,8,128,128]{3,2,1,0:T(8,128)(2,1)S(1)}, bf16[4,8,128,128]{3,2,1,0:T(8,128)(2,1)S(1)}, u32[]{:S(2)}, u32[]{:S(2)}) collective-permute-start(bf16[4,8,128,128]{3,2,1,0:T(8,128)(2,1)S(1)} %pad_maximum_fusion.refs_2_), channel_id=1, source_target_pairs={{0,24},{1,7},{2,26},{3,1},{4,28},{5,3},{6,30},{7,5},{8,0},{9,15},{... | collective-permute-start | bytes 3145736 | tf_op jit(solution)/shard_map/ppermute | solution.py:46
  34.7 43.0 %collective-permute-start.4 = (bf16[4,8,128,128]{3,2,1,0:T(8,128)(2,1)S(1)}, bf16[4,8,128,128]{3,2,1,0:T(8,128)(2,1)S(1)}, u32[]{:S(2)}, u32[]{:S(2)}) collective-permute-start(bf16[4,8,128,128]{3,2,1,0:T(8,128)(2,1)S(1)} %pad_maximum_fusion.refs_2_), channel_id=1, source_target_pairs={{0,16},{1,5},{2,18},{3,7},{4,20},{5,1},{6,22},{7,3},{8,24},{9,13},... | collective-permute-start | bytes 3145736 | tf_op jit(solution)/shard_map/ppermute | solution.py:46
  36.3 4.0 %collective-permute-start.5 = (s32[256]{0:T(256)}, s32[256]{0:T(256)S(1)}, u32[]{:S(2)}, u32[]{:S(2)}) collective-permute-start(s32[256]{0:T(256)} %refs_0_.15), channel_id=1, source_target_pairs={{0,1},{1,0},{2,3},{3,2},{4,5},{5,4},{6,7},{7,6},{8,9},{9,8},{10,11... | collective-permute-start | bytes 3080 | tf_op jit(solution)/shard_map/ppermute | solution.py:50
  39.3 17.4 %collective-permute-start.10 = (bf16[2,128,128]{2,1,0:T(8,128)(2,1)S(1)}, bf16[2,128,128]{2,1,0:T(8,128)(2,1)S(1)}, u32[]{:S(2)}, u32[]{:S(2)}) collective-permute-start(bf16[2,128,128]{2,1,0:T(8,128)(2,1)S(1)} %get-tuple-element.44.blocks_ref), channel_id=1, source_target_pairs={{0,255},{1,2},{2,1},{3,4},{4,3},{5,6},{6,5},{7,8},{8,7},{9,10},{10... | collective-permute-start | bytes 196616 | tf_op jit(solution)/shard_map/ppermute | solution.py:54
  40.3 20.0 %collective-permute-start.11 = (bf16[2,128,128]{2,1,0:T(8,128)(2,1)S(1)}, bf16[2,128,128]{2,1,0:T(8,128)(2,1)S(1)}, u32[]{:S(2)}, u32[]{:S(2)}) collective-permute-start(bf16[2,128,128]{2,1,0:T(8,128)(2,1)S(1)} %get-tuple-element.44.blocks_ref), channel_id=1, source_target_pairs={{0,254},{1,255},{2,0},{3,1},{4,2},{5,3},{6,4},{7,5},{8,6},{9,7},{1... | collective-permute-start | bytes 196616 | tf_op jit(solution)/shard_map/ppermute | solution.py:58
  56.6 14.6 %collective-permute-start.8 = (bf16[2,128,128]{2,1,0:T(8,128)(2,1)S(1)}, bf16[2,128,128]{2,1,0:T(8,128)(2,1)S(1)}, u32[]{:S(2)}, u32[]{:S(2)}) collective-permute-start(bf16[2,128,128]{2,1,0:T(8,128)(2,1)S(1)} %get-tuple-element.44.blocks_ref), channel_id=1, source_target_pairs={{0,2},{1,3},{2,4},{3,5},{4,6},{5,7},{6,8},{7,9},{8,10},{9,11},{10,... | collective-permute-start | bytes 196616 | tf_op jit(solution)/shard_map/ppermute | solution.py:58
  60.3 10.9 %collective-permute-start.9 = (bf16[2,128,128]{2,1,0:T(8,128)(2,1)S(1)}, bf16[2,128,128]{2,1,0:T(8,128)(2,1)S(1)}, u32[]{:S(2)}, u32[]{:S(2)}) collective-permute-start(bf16[2,128,128]{2,1,0:T(8,128)(2,1)S(1)} %get-tuple-element.44.blocks_ref), channel_id=1, source_target_pairs={{0,1},{1,0},{2,3},{3,2},{4,5},{5,4},{6,7},{7,6},{8,9},{9,8},{10,11... | collective-permute-start | bytes 196616 | tf_op jit(solution)/shard_map/ppermute | solution.py:50
  78.8 1.6 %collective-permute-start.12 = (f32[128,256]{1,0:T(8,128)S(1)}, f32[128,256]{1,0:T(8,128)S(1)}, u32[]{:S(2)}, u32[]{:S(2)}) collective-permute-start(f32[128,256]{1,0:T(8,128)S(1)} %dense_part.14), channel_id=1, source_target_pairs={{0,1},{1,0},{2,3},{3,2},{4,5},{5,4},{6,7},{7,6},{8,9},{9,8},{10,11... | collective-permute-start | bytes 393224 | tf_op jit(solution)/shard_map/ppermute | solution.py:50
  96.1 7.1 %collective-permute-start.15 = (bf16[8,128,128]{2,1,0:T(8,128)(2,1)S(1)}, bf16[8,128,128]{2,1,0:T(8,128)(2,1)S(1)}, u32[]{:S(2)}, u32[]{:S(2)}) collective-permute-start(bf16[8,128,128]{2,1,0:T(8,128)(2,1)S(1)} %all_to_all.11), channel_id=1, source_target_pairs={{0,4},{1,17},{2,6},{3,19},{4,0},{5,21},{6,2},{7,23},{8,12},{9,25},... | collective-permute-start | bytes 786440 | tf_op jit(solution)/shard_map/ppermute | solution.py:46
  96.1 8.5 %collective-permute-start.13 = (bf16[8,128,128]{2,1,0:T(8,128)(2,1)S(1)}, bf16[8,128,128]{2,1,0:T(8,128)(2,1)S(1)}, u32[]{:S(2)}, u32[]{:S(2)}) collective-permute-start(bf16[8,128,128]{2,1,0:T(8,128)(2,1)S(1)} %all_to_all.11), channel_id=1, source_target_pairs={{0,2},{1,9},{2,4},{3,11},{4,6},{5,13},{6,0},{7,15},{8,10},{9,17},{... | collective-permute-start | bytes 786440 | tf_op jit(solution)/shard_map/ppermute | solution.py:46
  97.4 7.2 %collective-permute-start.14 = (bf16[8,128,128]{2,1,0:T(8,128)(2,1)S(1)}, bf16[8,128,128]{2,1,0:T(8,128)(2,1)S(1)}, u32[]{:S(2)}, u32[]{:S(2)}) collective-permute-start(bf16[8,128,128]{2,1,0:T(8,128)(2,1)S(1)} %all_to_all.11), channel_id=1, source_target_pairs={{0,6},{1,25},{2,0},{3,27},{4,2},{5,29},{6,4},{7,31},{8,14},{9,1},{... | collective-permute-start | bytes 786440 | tf_op jit(solution)/shard_map/ppermute | solution.py:46
  104.7 41.5 %collective-permute-start.18 = (bf16[4,8,128,128]{3,2,1,0:T(8,128)(2,1)S(1)}, bf16[4,8,128,128]{3,2,1,0:T(8,128)(2,1)S(1)}, u32[]{:S(2)}, u32[]{:S(2)}) collective-permute-start(bf16[4,8,128,128]{3,2,1,0:T(8,128)(2,1)S(1)} %pad_maximum_fusion.1.refs_2_), channel_id=1, source_target_pairs={{0,8},{1,3},{2,10},{3,5},{4,12},{5,7},{6,14},{7,1},{8,16},{9,11},{... | collective-permute-start | bytes 3145736 | tf_op jit(solution)/shard_map/ppermute | solution.py:46
  104.8 42.7 %collective-permute-start.17 = (bf16[4,8,128,128]{3,2,1,0:T(8,128)(2,1)S(1)}, bf16[4,8,128,128]{3,2,1,0:T(8,128)(2,1)S(1)}, u32[]{:S(2)}, u32[]{:S(2)}) collective-permute-start(bf16[4,8,128,128]{3,2,1,0:T(8,128)(2,1)S(1)} %pad_maximum_fusion.1.refs_2_), channel_id=1, source_target_pairs={{0,24},{1,7},{2,26},{3,1},{4,28},{5,3},{6,30},{7,5},{8,0},{9,15},{... | collective-permute-start | bytes 3145736 | tf_op jit(solution)/shard_map/ppermute | solution.py:46
  108.9 40.0 %collective-permute-start.16 = (bf16[4,8,128,128]{3,2,1,0:T(8,128)(2,1)S(1)}, bf16[4,8,128,128]{3,2,1,0:T(8,128)(2,1)S(1)}, u32[]{:S(2)}, u32[]{:S(2)}) collective-permute-start(bf16[4,8,128,128]{3,2,1,0:T(8,128)(2,1)S(1)} %pad_maximum_fusion.1.refs_2_), channel_id=1, source_target_pairs={{0,16},{1,5},{2,18},{3,7},{4,20},{5,1},{6,22},{7,3},{8,24},{9,13},... | collective-permute-start | bytes 3145736 | tf_op jit(solution)/shard_map/ppermute | solution.py:46
  110.0 19.3 %collective-permute-start.19 = (bf16[2,128,128]{2,1,0:T(8,128)(2,1)S(1)}, bf16[2,128,128]{2,1,0:T(8,128)(2,1)S(1)}, u32[]{:S(2)}, u32[]{:S(2)}) collective-permute-start(bf16[2,128,128]{2,1,0:T(8,128)(2,1)S(1)} %get-tuple-element.58.blocks_ref), channel_id=1, source_target_pairs={{0,2},{1,3},{2,4},{3,5},{4,6},{5,7},{6,8},{7,9},{8,10},{9,11},{10,... | collective-permute-start | bytes 196616 | tf_op jit(solution)/shard_map/ppermute | solution.py:58
  110.8 18.4 %collective-permute-start.20 = (bf16[2,128,128]{2,1,0:T(8,128)(2,1)S(1)}, bf16[2,128,128]{2,1,0:T(8,128)(2,1)S(1)}, u32[]{:S(2)}, u32[]{:S(2)}) collective-permute-start(bf16[2,128,128]{2,1,0:T(8,128)(2,1)S(1)} %get-tuple-element.58.blocks_ref), channel_id=1, source_target_pairs={{0,1},{1,0},{2,3},{3,2},{4,5},{5,4},{6,7},{7,6},{8,9},{9,8},{10,11... | collective-permute-start | bytes 196616 | tf_op jit(solution)/shard_map/ppermute | solution.py:50
  129.2 13.7 %collective-permute-start.21 = (bf16[2,128,128]{2,1,0:T(8,128)(2,1)S(1)}, bf16[2,128,128]{2,1,0:T(8,128)(2,1)S(1)}, u32[]{:S(2)}, u32[]{:S(2)}) collective-permute-start(bf16[2,128,128]{2,1,0:T(8,128)(2,1)S(1)} %get-tuple-element.58.blocks_ref), channel_id=1, source_target_pairs={{0,255},{1,2},{2,1},{3,4},{4,3},{5,6},{6,5},{7,8},{8,7},{9,10},{10... | collective-permute-start | bytes 196616 | tf_op jit(solution)/shard_map/ppermute | solution.py:54
  129.2 13.7 %collective-permute-start.22 = (bf16[2,128,128]{2,1,0:T(8,128)(2,1)S(1)}, bf16[2,128,128]{2,1,0:T(8,128)(2,1)S(1)}, u32[]{:S(2)}, u32[]{:S(2)}) collective-permute-start(bf16[2,128,128]{2,1,0:T(8,128)(2,1)S(1)} %get-tuple-element.58.blocks_ref), channel_id=1, source_target_pairs={{0,254},{1,255},{2,0},{3,1},{4,2},{5,3},{6,4},{7,5},{8,6},{9,7},{1... | collective-permute-start | bytes 196616 | tf_op jit(solution)/shard_map/ppermute | solution.py:58
  149.9 1.4 collective-permute-start.23
  (11 other events, 23.6 us)

commit v5 on v4

--- a/solution.py
+++ b/solution.py
@@ -154,53 +154,51 @@
         in_specs=[SMEM, HBM, HBM],
         out_specs=VMEM,
         scratch_shapes=[pltpu.SemaphoreType.DMA((NC, NZ))],
-        compiler_params=pltpu.CompilerParams(vmem_limit_bytes=12 << 20),
+        compiler_params=pltpu.CompilerParams(vmem_limit_bytes=44 << 20),
         cost_estimate=pl.CostEstimate(flops=0, bytes_accessed=2 * SHARDS * TILE**2, transcendentals=0),
         name="collect",
     )(me, own.reshape(shape), other.reshape(shape))
 
 
-def dense_kernel(sides, me_ref, shift_ref, *refs):
-    count = len(sides)
-    row_refs, (chunk_ref, tiles_ref), start_refs, out_refs = refs[:count], refs[count : count + 2], refs[count + 2 : -count], refs[-count:]
+def dense_kernel(halves, me_ref, shift_ref, own_row_ref, other_row_ref, *refs):
+    chunk_refs, (tiles_ref, start_ref, out_ref) = refs[:halves], refs[halves:]
     me = me_ref[0]
     x, y, core = me // (NY * NC) % NX, me // NC % NY, me % NC
     fixed = (jnp.where(core == 0, x, y) + shift_ref[0]) % SIDE
-    for start_ref, out_ref in zip(start_refs, out_refs):
-        out_ref[...] = start_ref[...]
+    out_ref[...] = start_ref[...]
     for k, turn in enumerate(TURNS):
+        chunk_ref, at = chunk_refs[k * halves // SIDE], k % (SIDE // halves)
         along = (jnp.where(core == 0, y, x) + turn) % SIDE
         at_x = jnp.where(core == 0, fixed, along)
         at_y = jnp.where(core == 0, along, fixed)
         sources = [((z * NX + at_x) * NY + at_y) * NC + core for z in range(NZ)]
-        for side, row_ref, out_ref in zip(sides, row_refs, out_refs):
+        for side, row_ref in enumerate((own_row_ref, other_row_ref)):
             left = jnp.concatenate([tiles_ref[side, z, at_x, at_y] for z in range(NZ)], axis=1)
             right = jnp.concatenate(
-                [placed_pair(chunk_ref[k, z], row_ref[source]) for z, source in enumerate(sources)], axis=0
+                [placed_pair(chunk_ref[at, z], row_ref[source]) for z, source in enumerate(sources)], axis=0
             )
-            out_ref[...] += jnp.dot(left, right, preferred_element_type=jnp.float32)
-
-
-def dense_part(me, shift, rows, chunk, tiles, starts, sides=(0, 1)):
-    count = len(sides)
-    return pl.pallas_call(
-        functools.partial(dense_kernel, sides),
-        out_shape=(jax.ShapeDtypeStruct((TILE, NB * F), jnp.float32),) * count,
-        in_specs=[SMEM] * (2 + count) + [VMEM] * (2 + count),
-        out_specs=(VMEM,) * count,
+            out_ref[side] += jnp.dot(left, right, preferred_element_type=jnp.float32)
+
+
+def dense_part(me, shift, rows, chunks, tiles, start):
+    return pl.pallas_call(
+        functools.partial(dense_kernel, len(chunks)),
+        out_shape=jax.ShapeDtypeStruct((NC, TILE, NB * F), jnp.float32),
+        in_specs=[SMEM] * 4 + [VMEM] * (len(chunks) + 2),
+        out_specs=VMEM,
         compiler_params=pltpu.CompilerParams(vmem_limit_bytes=16 << 20),
         cost_estimate=pl.CostEstimate(
-            flops=4 * count * SIDE * NZ * TILE**3, bytes_accessed=3 * count * SIDE * NZ * TILE**2, transcendentals=0
+            flops=8 * SIDE * NZ * TILE**3, bytes_accessed=6 * SIDE * NZ * TILE**2, transcendentals=0
         ),
         name="dense_part",
-    )(me, jnp.array([shift], jnp.int32), *(rows[side] for side in sides), chunk, tiles, *starts)
+    )(me, jnp.array([shift], jnp.int32), *rows, *chunks, tiles, start)
 
 
 def finish_kernel(wide, me_ref, hub_ref, dense_ref, other_ref, sparse_ref, weight_ref, out_ref, *copies):
     blocks = []
     for block in range(NB):
         columns = slice(block * F, (block + 1) * F)
-        summed = dense_ref[:, columns] + other_ref[:, columns] + sparse_ref[:, columns]
+        summed = dense_ref[0, :, columns] + other_ref[:, columns] + sparse_ref[:, columns]
         projected = jnp.dot(
             summed, weight_ref[...], precision=lax.Precision.HIGHEST, preferred_element_type=jnp.float32
         )
@@ -241,29 +239,27 @@
     me = lax.axis_index("blk").astype(jnp.int32).reshape(1)
     rows = [dense_row, swap_cores(dense_row)]
     other_tiles = swap_cores(dense_tiles)
-    zeros = jnp.zeros((TILE, NB * F), jnp.float32)
+    zeros = jnp.zeros((NC, TILE, NB * F), jnp.float32)
 
     def propagate(blocks, copies, weight, dtype, wide, tiles=None):
         column = lax.all_to_all(copies, "blk", 0, 0, axis_index_groups=groups_along_z(), tiled=True)
-        sides = [step(column, 1, True), step(column, -1, True), step(column, 2, True)]
-        plane = jnp.stack([column, *sides])
+        blocks, column = lax.optimization_barrier((blocks, column))
+        near = [step(column, 1, True), step(column, -1, True)]
+        opposite = step(column, 2, True)
+        fetched = [from_behind(blocks, 2), swap_cores(blocks), swap_across(blocks), from_behind(blocks, -2)]
+        first, last = jnp.stack([column, near[0]]), jnp.stack([near[1], opposite])
         if tiles is None:
-            blocks, plane, others = lax.optimization_barrier((blocks, plane, other_tiles))
-            tiles = collect(me, dense_tiles, others)
-        else:
-            blocks, plane = lax.optimization_barrier((blocks, plane))
-        behind = step(plane, 1, False)
-        ahead = step(plane, -1, False)
-        far = step(plane, 2, False)
-        fetched = [from_behind(blocks, 2), swap_cores(blocks), swap_across(blocks), from_behind(blocks, -2)]
-        totals = dense_part(me, 0, rows, plane, tiles, (zeros, zeros))
+            tiles = collect(me, dense_tiles, lax.optimization_barrier((first, other_tiles))[1])
+        behind_first, ahead_last = step(first, 1, False), step(last, -1, False)
+        behind_last, ahead_first = step(last, 1, False), step(first, -1, False)
+        far = (step(behind_first, 1, False), step(ahead_last, -1, False))
+        total = dense_part(me, 0, rows, (first, last), tiles, zeros)
         sparse = sparse_sums(me, sparse_row, sparse_src, sparse_count, fetch_list, blocks, fetched, sparse_tiles)
-        totals = dense_part(me, SIDE - 1, rows, behind, tiles, totals)
-        totals = dense_part(me, 1, rows, ahead, tiles, totals)
-        far, own, other, sparse = lax.optimization_barrier((far, *totals, sparse))
-        (other,) = dense_part(me, 2, rows, far, tiles, (other,), (1,))
-        returned = swap_cores(other)
-        (total,) = dense_part(me, 2, rows, far, tiles, (own,), (0,))
+        total = dense_part(me, SIDE - 1, rows, (behind_first, behind_last), tiles, total)
+        total = dense_part(me, 1, rows, (ahead_first, ahead_last), tiles, total)
+        far, total, sparse = lax.optimization_barrier((far, total, sparse))
+        total = dense_part(me, 2, rows, far, tiles, total)
+        returned = swap_cores(total[1])
         return *finish(me, hub_block, total, returned, sparse, weight, dtype, wide), tiles
 
     blocks, copies = enter(me, hub_block, features)

time: 153 us -> 155 us (1.013)
  the two profiles are of different devices: /device:TPU:5 before, /device:TPU:1 now
where the time goes in v5:
time: 155 us; the launch traced here: 154 us
  starting transfers between devices  48.8 us (31%)
  waiting for transfers between devices  42.9 us (28%)
  blocking collectives  33.9 us (22%)
  Pallas kernels  21.7 us (14%)
  local copies, waits for them, and re-layouts  5.67 us (4%)
    all_to_all x2, blocking collectives, propagate(): lax.all_to_all(copies, 'blk', 0, 0, axis_index_groups=groups_along_z(), t...  33.9 us
    ppermute x18, waiting for transfers between devices, step(): return lax.ppermute(array, 'blk', pairs)  18.5 us
    ppermute x18, starting transfers between devices, step(): return lax.ppermute(array, 'blk', pairs)  18.3 us
    ppermute x4, waiting for transfers between devices, from_behind(): lax.ppermute(array, 'blk', [(i, (i + by) % SHARDS) for i in range(SHARDS)])  17.4 us
    ppermute x4, starting transfers between devices, from_behind(): lax.ppermute(array, 'blk', [(i, (i + by) % SHARDS) for i in range(SHARDS)])  15.8 us
    ppermute x6, starting transfers between devices, swap_cores(): return lax.ppermute(array, 'blk', [(i, i ^ 1) for i in range(SHARDS)])  14.7 us
    pallas_call x8, Pallas kernels, dense_part(): pl.pallas_call(functools.partial(dense_kernel, len(chunks)), out_shape=ja...  10.6 us
    unnamed x28, local copies, waits for them, and re-layouts  5.63 us
  transfers between devices with their start and end apart: 30, of which 15 were waited for; matrix products, arithmetic and copies ran while one was open for 0% of the time, Pallas kernels for 11%

profile of v5, /device:TPU:1, one launch (start us, length us, event | category | flops | bytes accessed | tf_op | source)
XLA Modules:
  0.0 154.2 jit_solution(4069875398445280014)
XLA Ops:
  0.0 3.2 %collective-permute-start.9 = (bf16[256,128,128]{2,1,0:T(8,128)(2,1)}, bf16[256,128,128]{2,1,0:T(8,128)(2,1)}, u32[]{:S(2)}, u32[]{:S(2)}) collective-permute-start(bf16[256,128,128]{2,1,0:T(8,128)(2,1)} %param.22), channel_id=1, source_target_pairs={{0,1},{1,0},{2,3},{3,2},{4,5},{5,4},{6,7},{7,6},{8,9},{9,8},{10,11... | collective-permute-start | bytes 25165832 | tf_op jit(solution)/shard_map/ppermute | solution.py:50
  5.4 18.6 %all_to_all.10 = bf16[8,128,128]{2,1,0:T(8,128)(2,1)S(1)} all-to-all(bf16[8,128,128]{2,1,0:T(8,128)(2,1)S(1)} %get-tuple-element.23), channel_id=1, replica_groups={{0,32,64,96,128,160,192,224},{1,33,65,97,129,161,193,225},{2,34,66,98,1..., dimensions={0} | all-to-all | bytes 524288 | tf_op jit(solution)/shard_map/all_to_all | solution.py:245
  28.2 2.5 %collective-permute-done.1 = bf16[8,128,128]{2,1,0:T(8,128)(2,1)S(1)} collective-permute-done((bf16[8,128,128]{2,1,0:T(8,128)(2,1)S(1)}, bf16[8,128,128]{2,1,0:T(8,128)(2,1)S(1)}, u32[]{:S(2)}, u32[]{:S(2)}) %collective-permute-start.1) | collective-permute-done | bytes 262176 | tf_op jit(solution)/shard_map/ppermute | solution.py:46
  31.9 2.7 %collective-permute-done.5 = bf16[8,128,128]{2,1,0:T(8,128)(2,1)S(1)} collective-permute-done((bf16[8,128,128]{2,1,0:T(8,128)(2,1)S(1)}, bf16[8,128,128]{2,1,0:T(8,128)(2,1)S(1)}, u32[]{:S(2)}, u32[]{:S(2)}) %collective-permute-start.5) | collective-permute-done | bytes 262176 | tf_op jit(solution)/shard_map/ppermute | solution.py:46
  34.6 2.8 %collective-permute-start.6 = (bf16[2,8,128,128]{3,2,1,0:T(8,128)(2,1)S(1)}, bf16[2,8,128,128]{3,2,1,0:T(8,128)(2,1)S(1)}, u32[]{:S(2)}, u32[]{:S(2)}) collective-permute-start(bf16[2,8,128,128]{3,2,1,0:T(8,128)(2,1)S(1)} %pad_maximum_fusion.1.refs_1_), channel_id=1, source_target_pairs={{0,24},{1,7},{2,26},{3,1},{4,28},{5,3},{6,30},{7,5},{8,0},{9,15},{... | collective-permute-start | bytes 1572872 | tf_op jit(solution)/shard_map/ppermute | solution.py:46
  37.4 3.0 %collective-permute-start.12 = (bf16[2,128,128]{2,1,0:T(8,128)(2,1)S(1)}, bf16[2,128,128]{2,1,0:T(8,128)(2,1)S(1)}, u32[]{:S(2)}, u32[]{:S(2)}) collective-permute-start(bf16[2,128,128]{2,1,0:T(8,128)(2,1)S(1)} %get-tuple-element.26.blocks_ref), channel_id=1, source_target_pairs={{0,1},{1,0},{2,3},{3,2},{4,5},{5,4},{6,7},{7,6},{8,9},{9,8},{10,11... | collective-permute-start | bytes 196616 | tf_op jit(solution)/shard_map/ppermute | solution.py:50
  40.4 5.5 %collective-permute-done.11.behind_ref = bf16[2,128,128]{2,1,0:T(8,128)(2,1)S(1)} collective-permute-done((bf16[2,128,128]{2,1,0:T(8,128)(2,1)S(1)}, bf16[2,128,128]{2,1,0:T(8,128)(2,1)S(1)}, u32[]{:S(2)}, u32[]{:S(2)}) %collective-permute-start.11) | collective-permute-done | bytes 65568 | tf_op jit(solution)/shard_map/ppermute | solution.py:58
  46.0 10.4 %collective-permute-start.14 = (bf16[2,128,128]{2,1,0:T(8,128)(2,1)S(1)}, bf16[2,128,128]{2,1,0:T(8,128)(2,1)S(1)}, u32[]{:S(2)}, u32[]{:S(2)}) collective-permute-start(bf16[2,128,128]{2,1,0:T(8,128)(2,1)S(1)} %get-tuple-element.26.blocks_ref), channel_id=1, source_target_pairs={{0,254},{1,255},{2,0},{3,1},{4,2},{5,3},{6,4},{7,5},{8,6},{9,7},{1... | collective-permute-start | bytes 196616 | tf_op jit(solution)/shard_map/ppermute | solution.py:58
  59.2 2.6 %collective-permute-start.7 = (bf16[2,8,128,128]{3,2,1,0:T(8,128)(2,1)S(1)}, bf16[2,8,128,128]{3,2,1,0:T(8,128)(2,1)S(1)}, u32[]{:S(2)}, u32[]{:S(2)}) collective-permute-start(bf16[2,8,128,128]{3,2,1,0:T(8,128)(2,1)S(1)} %collective-permute-done.6.refs_1_), channel_id=1, source_target_pairs={{0,24},{1,7},{2,26},{3,1},{4,28},{5,3},{6,30},{7,5},{8,0},{9,15},{... | collective-permute-start | bytes 1572872 | tf_op jit(solution)/shard_map/ppermute | solution.py:46
  62.4 3.6 %collective-permute-start = (s32[256]{0:T(256)}, s32[256]{0:T(256)S(1)}, u32[]{:S(2)}, u32[]{:S(2)}) collective-permute-start(s32[256]{0:T(256)} %own_row_ref.15), channel_id=1, source_target_pairs={{0,1},{1,0},{2,3},{3,2},{4,5},{5,4},{6,7},{7,6},{8,9},{9,8},{10,11... | collective-permute-start | bytes 3080 | tf_op jit(solution)/shard_map/ppermute | solution.py:50
  66.1 2.0 %copy-done = bf16[112,128,128]{2,1,0:T(8,128)(2,1)S(1)} copy-done((bf16[112,128,128]{2,1,0:T(8,128)(2,1)S(1)}, bf16[112,128,128]{2,1,0:T(8,128)(2,1)}, u32[]{:S(2)}) %copy-start) | copy-done | bytes 3670040
  70.1 2.5 %sparse_sums.2.sparse_ref = f32[128,256]{1,0:T(8,128)S(1)} custom-call(s32[1]{0:T(128)} %bitcast.me_ref, s32[112]{0:T(128)S(1)} %copy-done.8, s32[112]{0:T(128)S(1)} %copy-done.10, s32[1]{0:T(128)S(6)} %copy.20.count_ref, s32[1,4]{1,0:T(1,128)S(1)} %copy-done.12, bf16[2,128,128]{2,1,0:T(8,128)(2,1)S(1)} %get-tuple-element.26.blocks_ref, ...), custom_call_target="tpu_custom_call" | custom-call | flops 469762048 | bytes 3670016 | tf_op jit(solution)/shard_map/sparse_sums/pallas_call | solution.py:124
  72.5 3.5 %collect.1.refs_2_ = bf16[2,8,4,4,128,128]{5,4,3,2,1,0:T(8,128)(2,1)S(1)} custom-call(s32[1]{0:T(128)} %bitcast.me_ref, bf16[8,4,4,2,128,128]{5,4,3,2,1,0:T(8,128)(2,1)} %bitcast.16, bf16[8,4,4,2,128,128]{5,4,3,2,1,0:T(8,128)(2,1)} %bitcast.6.other_ref), custom_call_target="tpu_custom_call" | custom-call | bytes 8388608 | tf_op jit(solution)/shard_map/collect/pallas_call | solution.py:151
  83.8 15.3 %all_to_all.11 = bf16[8,128,128]{2,1,0:T(8,128)(2,1)S(1)} all-to-all(bf16[8,128,128]{2,1,0:T(8,128)(2,1)S(1)} %get-tuple-element.32), channel_id=1, replica_groups={{0,32,64,96,128,160,192,224},{1,33,65,97,129,161,193,225},{2,34,66,98,1..., dimensions={0} | all-to-all | bytes 524288 | tf_op jit(solution)/shard_map/all_to_all | solution.py:245
  100.5 4.0 %collective-permute-done.19 = bf16[8,128,128]{2,1,0:T(8,128)(2,1)S(1)} collective-permute-done((bf16[8,128,128]{2,1,0:T(8,128)(2,1)S(1)}, bf16[8,128,128]{2,1,0:T(8,128)(2,1)S(1)}, u32[]{:S(2)}, u32[]{:S(2)}) %collective-permute-start.19) | collective-permute-done | bytes 262176 | tf_op jit(solution)/shard_map/ppermute | solution.py:46
  106.4 2.6 %collective-permute-done.16 = bf16[8,128,128]{2,1,0:T(8,128)(2,1)S(1)} collective-permute-done((bf16[8,128,128]{2,1,0:T(8,128)(2,1)S(1)}, bf16[8,128,128]{2,1,0:T(8,128)(2,1)S(1)}, u32[]{:S(2)}, u32[]{:S(2)}) %collective-permute-start.16) | collective-permute-done | bytes 262176 | tf_op jit(solution)/shard_map/ppermute | solution.py:46
  109.2 2.7 %collective-permute-start.23 = (bf16[2,8,128,128]{3,2,1,0:T(8,128)(2,1)S(1)}, bf16[2,8,128,128]{3,2,1,0:T(8,128)(2,1)S(1)}, u32[]{:S(2)}, u32[]{:S(2)}) collective-permute-start(bf16[2,8,128,128]{3,2,1,0:T(8,128)(2,1)S(1)} %pad_maximum_fusion.2.refs_0_), channel_id=1, source_target_pairs={{0,24},{1,7},{2,26},{3,1},{4,28},{5,3},{6,30},{7,5},{8,0},{9,15},{... | collective-permute-start | bytes 1572872 | tf_op jit(solution)/shard_map/ppermute | solution.py:46
  111.9 2.8 %collective-permute-done.21.refs_1_ = bf16[2,8,128,128]{3,2,1,0:T(8,128)(2,1)S(1)} collective-permute-done((bf16[2,8,128,128]{3,2,1,0:T(8,128)(2,1)S(1)}, bf16[2,8,128,128]{3,2,1,0:T(8,128)(2,1)S(1)}, u32[]{:S(2)}, u32[]{:S(2)}) %collective-permute-start.21) | collective-permute-done | bytes 524320 | tf_op jit(solution)/shard_map/ppermute | solution.py:46
  116.4 2.2 %collective-permute-done.17.refs_0_ = bf16[2,8,128,128]{3,2,1,0:T(8,128)(2,1)S(1)} collective-permute-done((bf16[2,8,128,128]{3,2,1,0:T(8,128)(2,1)S(1)}, bf16[2,8,128,128]{3,2,1,0:T(8,128)(2,1)S(1)}, u32[]{:S(2)}, u32[]{:S(2)}) %collective-permute-start.17) | collective-permute-done | bytes 524320 | tf_op jit(solution)/shard_map/ppermute | solution.py:46
  118.7 9.2 %collective-permute-done.25.behind_ref = bf16[2,128,128]{2,1,0:T(8,128)(2,1)S(1)} collective-permute-done((bf16[2,128,128]{2,1,0:T(8,128)(2,1)S(1)}, bf16[2,128,128]{2,1,0:T(8,128)(2,1)S(1)}, u32[]{:S(2)}, u32[]{:S(2)}) %collective-permute-start.25) | collective-permute-done | bytes 65568 | tf_op jit(solution)/shard_map/ppermute | solution.py:58
  127.9 2.8 %collective-permute-start.26 = (bf16[2,128,128]{2,1,0:T(8,128)(2,1)S(1)}, bf16[2,128,128]{2,1,0:T(8,128)(2,1)S(1)}, u32[]{:S(2)}, u32[]{:S(2)}) collective-permute-start(bf16[2,128,128]{2,1,0:T(8,128)(2,1)S(1)} %get-tuple-element.34.blocks_ref), channel_id=1, source_target_pairs={{0,1},{1,0},{2,3},{3,2},{4,5},{5,4},{6,7},{7,6},{8,9},{9,8},{10,11... | collective-permute-start | bytes 196616 | tf_op jit(solution)/shard_map/ppermute | solution.py:50
  131.5 3.7 %collective-permute-done.27.across_ref = bf16[2,128,128]{2,1,0:T(8,128)(2,1)S(1)} collective-permute-done((bf16[2,128,128]{2,1,0:T(8,128)(2,1)S(1)}, bf16[2,128,128]{2,1,0:T(8,128)(2,1)S(1)}, u32[]{:S(2)}, u32[]{:S(2)}) %collective-permute-start.27) | collective-permute-done | bytes 65568 | tf_op jit(solution)/shard_map/ppermute | solution.py:54
  135.2 5.4 %collective-permute-start.28 = (bf16[2,128,128]{2,1,0:T(8,128)(2,1)S(1)}, bf16[2,128,128]{2,1,0:T(8,128)(2,1)S(1)}, u32[]{:S(2)}, u32[]{:S(2)}) collective-permute-start(bf16[2,128,128]{2,1,0:T(8,128)(2,1)S(1)} %get-tuple-element.34.blocks_ref), channel_id=1, source_target_pairs={{0,254},{1,255},{2,0},{3,1},{4,2},{5,3},{6,4},{7,5},{8,6},{9,7},{1... | collective-permute-start | bytes 196616 | tf_op jit(solution)/shard_map/ppermute | solution.py:58
  142.0 2.3 %sparse_sums.3.sparse_ref = f32[128,256]{1,0:T(8,128)S(1)} custom-call(s32[1]{0:T(128)} %bitcast.me_ref, s32[112]{0:T(128)S(1)} %copy-done.9, s32[112]{0:T(128)S(1)} %copy-done.11, s32[1]{0:T(128)S(6)} %copy.20.count_ref, s32[1,4]{1,0:T(1,128)S(1)} %copy-done.13, bf16[2,128,128]{2,1,0:T(8,128)(2,1)S(1)} %get-tuple-element.34.blocks_ref, ...), custom_call_target="tpu_custom_call" | custom-call | flops 469762048 | bytes 3670016 | tf_op jit(solution)/shard_map/sparse_sums/pallas_call | solution.py:124
  (87 shorter events, 37.2 us)
Async XLA Ops:
  0.0 62.4 %collective-permute-start.9 = (bf16[256,128,128]{2,1,0:T(8,128)(2,1)}, bf16[256,128,128]{2,1,0:T(8,128)(2,1)}, u32[]{:S(2)}, u32[]{:S(2)}) collective-permute-start(bf16[256,128,128]{2,1,0:T(8,128)(2,1)} %param.22), channel_id=1, source_target_pairs={{0,1},{1,0},{2,3},{3,2},{4,5},{5,4},{6,7},{7,6},{8,9},{9,8},{10,11... | collective-permute-start | bytes 25165832 | tf_op jit(solution)/shard_map/ppermute | solution.py:50
  24.0 6.7 %collective-permute-start.1 = (bf16[8,128,128]{2,1,0:T(8,128)(2,1)S(1)}, bf16[8,128,128]{2,1,0:T(8,128)(2,1)S(1)}, u32[]{:S(2)}, u32[]{:S(2)}) collective-permute-start(bf16[8,128,128]{2,1,0:T(8,128)(2,1)S(1)} %all_to_all.10), channel_id=1, source_target_pairs={{0,2},{1,9},{2,4},{3,11},{4,6},{5,13},{6,0},{7,15},{8,10},{9,17},{... | collective-permute-start | bytes 786440 | tf_op jit(solution)/shard_map/ppermute | solution.py:46
  26.7 7.8 %collective-permute-start.5 = (bf16[8,128,128]{2,1,0:T(8,128)(2,1)S(1)}, bf16[8,128,128]{2,1,0:T(8,128)(2,1)S(1)}, u32[]{:S(2)}, u32[]{:S(2)}) collective-permute-start(bf16[8,128,128]{2,1,0:T(8,128)(2,1)S(1)} %all_to_all.10), channel_id=1, source_target_pairs={{0,4},{1,17},{2,6},{3,19},{4,0},{5,21},{6,2},{7,23},{8,12},{9,25},... | collective-permute-start | bytes 786440 | tf_op jit(solution)/shard_map/ppermute | solution.py:46
  30.8 28.3 %collective-permute-start.2 = (bf16[2,8,128,128]{3,2,1,0:T(8,128)(2,1)S(1)}, bf16[2,8,128,128]{3,2,1,0:T(8,128)(2,1)S(1)}, u32[]{:S(2)}, u32[]{:S(2)}) collective-permute-start(bf16[2,8,128,128]{3,2,1,0:T(8,128)(2,1)S(1)} %pad_maximum_fusion.refs_0_), channel_id=1, source_target_pairs={{0,8},{1,3},{2,10},{3,5},{4,12},{5,7},{6,14},{7,1},{8,16},{9,11},{... | collective-permute-start | bytes 1572872 | tf_op jit(solution)/shard_map/ppermute | solution.py:46
  34.6 24.6 %collective-permute-start.6 = (bf16[2,8,128,128]{3,2,1,0:T(8,128)(2,1)S(1)}, bf16[2,8,128,128]{3,2,1,0:T(8,128)(2,1)S(1)}, u32[]{:S(2)}, u32[]{:S(2)}) collective-permute-start(bf16[2,8,128,128]{3,2,1,0:T(8,128)(2,1)S(1)} %pad_maximum_fusion.1.refs_1_), channel_id=1, source_target_pairs={{0,24},{1,7},{2,26},{3,1},{4,28},{5,3},{6,30},{7,5},{8,0},{9,15},{... | collective-permute-start | bytes 1572872 | tf_op jit(solution)/shard_map/ppermute | solution.py:46
  37.4 8.5 %collective-permute-start.11 = (bf16[2,128,128]{2,1,0:T(8,128)(2,1)S(1)}, bf16[2,128,128]{2,1,0:T(8,128)(2,1)S(1)}, u32[]{:S(2)}, u32[]{:S(2)}) collective-permute-start(bf16[2,128,128]{2,1,0:T(8,128)(2,1)S(1)} %get-tuple-element.26.blocks_ref), channel_id=1, source_target_pairs={{0,2},{1,3},{2,4},{3,5},{4,6},{5,7},{6,8},{7,9},{8,10},{9,11},{10,... | collective-permute-start | bytes 196616 | tf_op jit(solution)/shard_map/ppermute | solution.py:58
  37.4 8.5 %collective-permute-start.12 = (bf16[2,128,128]{2,1,0:T(8,128)(2,1)S(1)}, bf16[2,128,128]{2,1,0:T(8,128)(2,1)S(1)}, u32[]{:S(2)}, u32[]{:S(2)}) collective-permute-start(bf16[2,128,128]{2,1,0:T(8,128)(2,1)S(1)} %get-tuple-element.26.blocks_ref), channel_id=1, source_target_pairs={{0,1},{1,0},{2,3},{3,2},{4,5},{5,4},{6,7},{7,6},{8,9},{9,8},{10,11... | collective-permute-start | bytes 196616 | tf_op jit(solution)/shard_map/ppermute | solution.py:50
  46.0 10.4 %collective-permute-start.13 = (bf16[2,128,128]{2,1,0:T(8,128)(2,1)S(1)}, bf16[2,128,128]{2,1,0:T(8,128)(2,1)S(1)}, u32[]{:S(2)}, u32[]{:S(2)}) collective-permute-start(bf16[2,128,128]{2,1,0:T(8,128)(2,1)S(1)} %get-tuple-element.26.blocks_ref), channel_id=1, source_target_pairs={{0,255},{1,2},{2,1},{3,4},{4,3},{5,6},{6,5},{7,8},{8,7},{9,10},{10... | collective-permute-start | bytes 196616 | tf_op jit(solution)/shard_map/ppermute | solution.py:54
  46.0 11.8 %collective-permute-start.14 = (bf16[2,128,128]{2,1,0:T(8,128)(2,1)S(1)}, bf16[2,128,128]{2,1,0:T(8,128)(2,1)S(1)}, u32[]{:S(2)}, u32[]{:S(2)}) collective-permute-start(bf16[2,128,128]{2,1,0:T(8,128)(2,1)S(1)} %get-tuple-element.26.blocks_ref), channel_id=1, source_target_pairs={{0,254},{1,255},{2,0},{3,1},{4,2},{5,3},{6,4},{7,5},{8,6},{9,7},{1... | collective-permute-start | bytes 196616 | tf_op jit(solution)/shard_map/ppermute | solution.py:58
  56.4 21.0 %collective-permute-start.10 = (bf16[2,8,128,128]{3,2,1,0:T(8,128)(2,1)S(1)}, bf16[2,8,128,128]{3,2,1,0:T(8,128)(2,1)S(1)}, u32[]{:S(2)}, u32[]{:S(2)}) collective-permute-start(bf16[2,8,128,128]{3,2,1,0:T(8,128)(2,1)S(1)} %pad_maximum_fusion.1.refs_1_), channel_id=1, source_target_pairs={{0,8},{1,3},{2,10},{3,5},{4,12},{5,7},{6,14},{7,1},{8,16},{9,11},{... | collective-permute-start | bytes 1572872 | tf_op jit(solution)/shard_map/ppermute | solution.py:46
  57.7 21.1 %collective-permute-start.8 = (bf16[2,8,128,128]{3,2,1,0:T(8,128)(2,1)S(1)}, bf16[2,8,128,128]{3,2,1,0:T(8,128)(2,1)S(1)}, u32[]{:S(2)}, u32[]{:S(2)}) collective-permute-start(bf16[2,8,128,128]{3,2,1,0:T(8,128)(2,1)S(1)} %pad_maximum_fusion.refs_0_), channel_id=1, source_target_pairs={{0,24},{1,7},{2,26},{3,1},{4,28},{5,3},{6,30},{7,5},{8,0},{9,15},{... | collective-permute-start | bytes 1572872 | tf_op jit(solution)/shard_map/ppermute | solution.py:46
  59.1 21.1 %collective-permute-start.3 = (bf16[2,8,128,128]{3,2,1,0:T(8,128)(2,1)S(1)}, bf16[2,8,128,128]{3,2,1,0:T(8,128)(2,1)S(1)}, u32[]{:S(2)}, u32[]{:S(2)}) collective-permute-start(bf16[2,8,128,128]{3,2,1,0:T(8,128)(2,1)S(1)} %collective-permute-done.2.refs_0_), channel_id=1, source_target_pairs={{0,8},{1,3},{2,10},{3,5},{4,12},{5,7},{6,14},{7,1},{8,16},{9,11},{... | collective-permute-start | bytes 1572872 | tf_op jit(solution)/shard_map/ppermute | solution.py:46
  59.2 21.0 %collective-permute-start.7 = (bf16[2,8,128,128]{3,2,1,0:T(8,128)(2,1)S(1)}, bf16[2,8,128,128]{3,2,1,0:T(8,128)(2,1)S(1)}, u32[]{:S(2)}, u32[]{:S(2)}) collective-permute-start(bf16[2,8,128,128]{3,2,1,0:T(8,128)(2,1)S(1)} %collective-permute-done.6.refs_1_), channel_id=1, source_target_pairs={{0,24},{1,7},{2,26},{3,1},{4,28},{5,3},{6,30},{7,5},{8,0},{9,15},{... | collective-permute-start | bytes 1572872 | tf_op jit(solution)/shard_map/ppermute | solution.py:46
  62.4 13.6 %collective-permute-start = (s32[256]{0:T(256)}, s32[256]{0:T(256)S(1)}, u32[]{:S(2)}, u32[]{:S(2)}) collective-permute-start(s32[256]{0:T(256)} %own_row_ref.15), channel_id=1, source_target_pairs={{0,1},{1,0},{2,3},{3,2},{4,5},{5,4},{6,7},{7,6},{8,9},{9,8},{10,11... | collective-permute-start | bytes 3080 | tf_op jit(solution)/shard_map/ppermute | solution.py:50
  99.2 7.1 %collective-permute-start.20 = (bf16[8,128,128]{2,1,0:T(8,128)(2,1)S(1)}, bf16[8,128,128]{2,1,0:T(8,128)(2,1)S(1)}, u32[]{:S(2)}, u32[]{:S(2)}) collective-permute-start(bf16[8,128,128]{2,1,0:T(8,128)(2,1)S(1)} %all_to_all.11), channel_id=1, source_target_pairs={{0,4},{1,17},{2,6},{3,19},{4,0},{5,21},{6,2},{7,23},{8,12},{9,25},... | collective-permute-start | bytes 786440 | tf_op jit(solution)/shard_map/ppermute | solution.py:46
  99.2 9.8 %collective-permute-start.16 = (bf16[8,128,128]{2,1,0:T(8,128)(2,1)S(1)}, bf16[8,128,128]{2,1,0:T(8,128)(2,1)S(1)}, u32[]{:S(2)}, u32[]{:S(2)}) collective-permute-start(bf16[8,128,128]{2,1,0:T(8,128)(2,1)S(1)} %all_to_all.11), channel_id=1, source_target_pairs={{0,2},{1,9},{2,4},{3,11},{4,6},{5,13},{6,0},{7,15},{8,10},{9,17},{... | collective-permute-start | bytes 786440 | tf_op jit(solution)/shard_map/ppermute | solution.py:46
  106.3 8.4 %collective-permute-start.21 = (bf16[2,8,128,128]{3,2,1,0:T(8,128)(2,1)S(1)}, bf16[2,8,128,128]{3,2,1,0:T(8,128)(2,1)S(1)}, u32[]{:S(2)}, u32[]{:S(2)}) collective-permute-start(bf16[2,8,128,128]{3,2,1,0:T(8,128)(2,1)S(1)} %pad_maximum_fusion.3.refs_1_), channel_id=1, source_target_pairs={{0,24},{1,7},{2,26},{3,1},{4,28},{5,3},{6,30},{7,5},{8,0},{9,15},{... | collective-permute-start | bytes 1572872 | tf_op jit(solution)/shard_map/ppermute | solution.py:46
  109.0 9.6 %collective-permute-start.17 = (bf16[2,8,128,128]{3,2,1,0:T(8,128)(2,1)S(1)}, bf16[2,8,128,128]{3,2,1,0:T(8,128)(2,1)S(1)}, u32[]{:S(2)}, u32[]{:S(2)}) collective-permute-start(bf16[2,8,128,128]{3,2,1,0:T(8,128)(2,1)S(1)} %pad_maximum_fusion.2.refs_0_), channel_id=1, source_target_pairs={{0,8},{1,3},{2,10},{3,5},{4,12},{5,7},{6,14},{7,1},{8,16},{9,11},{... | collective-permute-start | bytes 1572872 | tf_op jit(solution)/shard_map/ppermute | solution.py:46
  109.1 36.5 %collective-permute-start.24 = (bf16[2,8,128,128]{3,2,1,0:T(8,128)(2,1)S(1)}, bf16[2,8,128,128]{3,2,1,0:T(8,128)(2,1)S(1)}, u32[]{:S(2)}, u32[]{:S(2)}) collective-permute-start(bf16[2,8,128,128]{3,2,1,0:T(8,128)(2,1)S(1)} %pad_maximum_fusion.3.refs_1_), channel_id=1, source_target_pairs={{0,8},{1,3},{2,10},{3,5},{4,12},{5,7},{6,14},{7,1},{8,16},{9,11},{... | collective-permute-start | bytes 1572872 | tf_op jit(solution)/shard_map/ppermute | solution.py:46
  109.2 37.7 %collective-permute-start.23 = (bf16[2,8,128,128]{3,2,1,0:T(8,128)(2,1)S(1)}, bf16[2,8,128,128]{3,2,1,0:T(8,128)(2,1)S(1)}, u32[]{:S(2)}, u32[]{:S(2)}) collective-permute-start(bf16[2,8,128,128]{3,2,1,0:T(8,128)(2,1)S(1)} %pad_maximum_fusion.2.refs_0_), channel_id=1, source_target_pairs={{0,24},{1,7},{2,26},{3,1},{4,28},{5,3},{6,30},{7,5},{8,0},{9,15},{... | collective-permute-start | bytes 1572872 | tf_op jit(solution)/shard_map/ppermute | solution.py:46
  114.7 33.6 %collective-permute-start.22 = (bf16[2,8,128,128]{3,2,1,0:T(8,128)(2,1)S(1)}, bf16[2,8,128,128]{3,2,1,0:T(8,128)(2,1)S(1)}, u32[]{:S(2)}, u32[]{:S(2)}) collective-permute-start(bf16[2,8,128,128]{3,2,1,0:T(8,128)(2,1)S(1)} %collective-permute-done.21.refs_1_), channel_id=1, source_target_pairs={{0,24},{1,7},{2,26},{3,1},{4,28},{5,3},{6,30},{7,5},{8,0},{9,15},{... | collective-permute-start | bytes 1572872 | tf_op jit(solution)/shard_map/ppermute | solution.py:46
  118.7 29.7 %collective-permute-start.18 = (bf16[2,8,128,128]{3,2,1,0:T(8,128)(2,1)S(1)}, bf16[2,8,128,128]{3,2,1,0:T(8,128)(2,1)S(1)}, u32[]{:S(2)}, u32[]{:S(2)}) collective-permute-start(bf16[2,8,128,128]{3,2,1,0:T(8,128)(2,1)S(1)} %collective-permute-done.17.refs_0_), channel_id=1, source_target_pairs={{0,8},{1,3},{2,10},{3,5},{4,12},{5,7},{6,14},{7,1},{8,16},{9,11},{... | collective-permute-start | bytes 1572872 | tf_op jit(solution)/shard_map/ppermute | solution.py:46
  118.7 9.2 %collective-permute-start.25 = (bf16[2,128,128]{2,1,0:T(8,128)(2,1)S(1)}, bf16[2,128,128]{2,1,0:T(8,128)(2,1)S(1)}, u32[]{:S(2)}, u32[]{:S(2)}) collective-permute-start(bf16[2,128,128]{2,1,0:T(8,128)(2,1)S(1)} %get-tuple-element.34.blocks_ref), channel_id=1, source_target_pairs={{0,2},{1,3},{2,4},{3,5},{4,6},{5,7},{6,8},{7,9},{8,10},{9,11},{10,... | collective-permute-start | bytes 196616 | tf_op jit(solution)/shard_map/ppermute | solution.py:58
  135.2 6.7 %collective-permute-start.28 = (bf16[2,128,128]{2,1,0:T(8,128)(2,1)S(1)}, bf16[2,128,128]{2,1,0:T(8,128)(2,1)S(1)}, u32[]{:S(2)}, u32[]{:S(2)}) collective-permute-start(bf16[2,128,128]{2,1,0:T(8,128)(2,1)S(1)} %get-tuple-element.34.blocks_ref), channel_id=1, source_target_pairs={{0,254},{1,255},{2,0},{3,1},{4,2},{5,3},{6,4},{7,5},{8,6},{9,7},{1... | collective-permute-start | bytes 196616 | tf_op jit(solution)/shard_map/ppermute | solution.py:58
  (20 other events, 294.6 us)

commit v6 on v5

--- a/solution.py
+++ b/solution.py
@@ -50,10 +50,6 @@
     return lax.ppermute(array, "blk", [(i, i ^ 1) for i in range(SHARDS)])
 
 
-def swap_across(array):
-    return lax.ppermute(array, "blk", [(i, (i + (1 if i % 2 else -1)) % SHARDS) for i in range(SHARDS)])
-
-
 def from_behind(array, by):
     return lax.ppermute(array, "blk", [(i, (i + by) % SHARDS) for i in range(SHARDS)])
 
@@ -86,17 +82,17 @@
     )(me, hub_block, features)
 
 
-def sparse_kernel(me_ref, row_ref, src_ref, count_ref, fetch_ref, blocks_ref, behind_ref, swap_ref, across_ref, ahead_ref, tiles_ref, out_ref, placed_ref):
+def sparse_kernel(me_ref, row_ref, src_ref, count_ref, fetch_ref, blocks_ref, beside_ref, behind_ref, ahead_ref, tiles_ref, out_ref, placed_ref):
     zeros = jnp.zeros((TILE, F), jnp.bfloat16)
     even = me_ref[0] % 2 == 0
     before, after = fetch_ref[0, 1], fetch_ref[0, 2]
     blocks = [
         blocks_ref[0],
         blocks_ref[1],
-        behind_ref[fetch_ref[0, 0]],
-        jnp.where(even, across_ref[before], swap_ref[before]),
-        jnp.where(even, swap_ref[after], across_ref[after]),
-        ahead_ref[fetch_ref[0, 3]],
+        behind_ref[0, fetch_ref[0, 0]],
+        jnp.where(even, behind_ref[1, before], beside_ref[before]),
+        jnp.where(even, beside_ref[after], ahead_ref[1, after]),
+        ahead_ref[0, fetch_ref[0, 3]],
     ]
     for source in range(SOURCES):
         placed_ref[2 * source] = jnp.concatenate([blocks[source], zeros], axis=1)
@@ -120,17 +116,17 @@
     lax.fori_loop(0, (live + group - 1) // group, add, 0)
 
 
-def sparse_sums(me, row, src, count, wanted, blocks, fetched, tiles):
+def sparse_sums(me, row, src, count, wanted, near_blocks, tiles):
     return pl.pallas_call(
         sparse_kernel,
         out_shape=jax.ShapeDtypeStruct((TILE, NB * F), jnp.float32),
-        in_specs=[SMEM] * 5 + [VMEM] * (2 + 2 * HOPS),
+        in_specs=[SMEM] * 5 + [VMEM] * 5,
         out_specs=VMEM,
         scratch_shapes=[pltpu.VMEM((2 * SOURCES + 1, TILE, NB * F), jnp.bfloat16)],
         cost_estimate=pl.CostEstimate(flops=2 * KS * TILE**3, bytes_accessed=2 * KS * TILE**2, transcendentals=0),
         compiler_params=pltpu.CompilerParams(vmem_limit_bytes=16 << 20),
         name="sparse_sums",
-    )(me, row, src, count, wanted, blocks, *fetched, tiles)
+    )(me, row, src, count, wanted, *near_blocks, tiles)
 
 
 def collect_kernel(me_ref, own_ref, other_ref, out_ref, sems):
@@ -243,10 +239,12 @@
 
     def propagate(blocks, copies, weight, dtype, wide, tiles=None):
         column = lax.all_to_all(copies, "blk", 0, 0, axis_index_groups=groups_along_z(), tiled=True)
-        blocks, column = lax.optimization_barrier((blocks, column))
+        beside = swap_cores(blocks)
+        pair = jnp.stack([blocks, beside])
+        fetched = [from_behind(pair, NC), from_behind(pair, -NC)]
+        column, fetched = lax.optimization_barrier((column, fetched))
         near = [step(column, 1, True), step(column, -1, True)]
         opposite = step(column, 2, True)
-        fetched = [from_behind(blocks, 2), swap_cores(blocks), swap_across(blocks), from_behind(blocks, -2)]
         first, last = jnp.stack([column, near[0]]), jnp.stack([near[1], opposite])
         if tiles is None:
             tiles = collect(me, dense_tiles, lax.optimization_barrier((first, other_tiles))[1])
@@ -254,7 +252,8 @@
         behind_last, ahead_first = step(last, 1, False), step(first, -1, False)
         far = (step(behind_first, 1, False), step(ahead_last, -1, False))
         total = dense_part(me, 0, rows, (first, last), tiles, zeros)
-        sparse = sparse_sums(me, sparse_row, sparse_src, sparse_count, fetch_list, blocks, fetched, sparse_tiles)
+        near_blocks, total = lax.optimization_barrier(((blocks, beside, *fetched), total))
+        sparse = sparse_sums(me, sparse_row, sparse_src, sparse_count, fetch_list, near_blocks, sparse_tiles)
         total = dense_part(me, SIDE - 1, rows, (behind_first, behind_last), tiles, total)
         total = dense_part(me, 1, rows, (ahead_first, ahead_last), tiles, total)
         far, total, sparse = lax.optimization_barrier((far, total, sparse))

time: 155 us -> 133 us (0.86)
  blocking collectives: 33.9 us -> 0 us
  local copies, waits for them, and re-layouts: 5.67 us -> 11 us
  starting transfers between devices: 48.8 us -> 54 us
    all_to_all x2 -> x0, blocking collectives: 33.9 us -> none  [propagate(): lax.all_to_all(copies, 'blk', 0, 0, axis_index_groups=groups_along_z(), t...]
    all_to_all x0 -> x2, starting transfers between devices: none -> 12.6 us  [propagate(): lax.all_to_all(copies, 'blk', 0, 0, axis_index_groups=groups_along_z(), t...]
    ppermute x4, waiting for transfers between devices: 17.4 us -> 11.1 us  [from_behind(): lax.ppermute(array, 'blk', [(i, (i + by) % SHARDS) for i in range(SHARDS)])]
    ppermute x18, waiting for transfers between devices: 18.5 us -> 24.3 us  [step(): return lax.ppermute(array, 'blk', pairs)]
    unnamed x28, local copies, waits for them, and re-layouts: 5.63 us -> 11 us
    ppermute x6, starting transfers between devices: 14.7 us -> 9.42 us  [swap_cores(): return lax.ppermute(array, 'blk', [(i, i ^ 1) for i in range(SHARDS)])]
    ppermute x2 -> x0, waiting for transfers between devices: 3.69 us -> none  [swap_across(): lax.ppermute(array, 'blk', [(i, (i + (1 if i % 2 else -1)) % SHARDS) for...]
    ppermute x18, starting transfers between devices: 18.3 us -> 14.7 us  [step(): return lax.ppermute(array, 'blk', pairs)]
  transfers between devices with their start and end apart: 30 -> 30, of which waited for: 15 -> 16; matrix products, arithmetic and copies ran while one was open for 0% -> 0% of each run, Pallas kernels for 11% -> 13%
where the time goes in v6:
time: 133 us; the launch traced here: 131 us
  starting transfers between devices  54 us (41%)
  waiting for transfers between devices  42.1 us (32%)
  Pallas kernels  23.1 us (17%)
  local copies, waits for them, and re-layouts  11 us (8%)
    ppermute x18, waiting for transfers between devices, step(): return lax.ppermute(array, 'blk', pairs)  24.3 us
    ppermute x4, starting transfers between devices, from_behind(): lax.ppermute(array, 'blk', [(i, (i + by) % SHARDS) for i in range(SHARDS)])  17.3 us
    ppermute x18, starting transfers between devices, step(): return lax.ppermute(array, 'blk', pairs)  14.7 us
    all_to_all x2, starting transfers between devices, propagate(): lax.all_to_all(copies, 'blk', 0, 0, axis_index_groups=groups_along_z(), t...  12.6 us
    ppermute x4, waiting for transfers between devices, from_behind(): lax.ppermute(array, 'blk', [(i, (i + by) % SHARDS) for i in range(SHARDS)])  11.1 us
    unnamed x28, local copies, waits for them, and re-layouts  11 us
    pallas_call x8, Pallas kernels, dense_part(): pl.pallas_call(functools.partial(dense_kernel, len(chunks)), out_shape=ja...  10.5 us
    ppermute x6, starting transfers between devices, swap_cores(): return lax.ppermute(array, 'blk', [(i, i ^ 1) for i in range(SHARDS)])  9.42 us
  transfers between devices with their start and end apart: 30, of which 16 were waited for; matrix products, arithmetic and copies ran while one was open for 0% of the time, Pallas kernels for 13%

profile of v6, /device:TPU:1, one launch (start us, length us, event | category | flops | bytes accessed | tf_op | source)
XLA Modules:
  0.0 131.4 jit_solution(1105023027426464212)
XLA Ops:
  0.0 3.2 %collective-permute-start.12 = (bf16[256,128,128]{2,1,0:T(8,128)(2,1)}, bf16[256,128,128]{2,1,0:T(8,128)(2,1)}, u32[]{:S(2)}, u32[]{:S(2)}) collective-permute-start(bf16[256,128,128]{2,1,0:T(8,128)(2,1)} %param.22), channel_id=1, source_target_pairs={{0,1},{1,0},{2,3},{3,2},{4,5},{5,4},{6,7},{7,6},{8,9},{9,8},{10,11... | collective-permute-start | bytes 25165832 | tf_op jit(solution)/shard_map/ppermute | solution.py:50
  6.1 6.5 %all-to-all-start = ((bf16[8,128,128]{2,1,0:T(8,128)(2,1)}), bf16[8,128,128]{2,1,0:T(8,128)(2,1)S(1)}, u32[]{:S(2)}, u32[]{:S(2)}) async-start(bf16[8,128,128]{2,1,0:T(8,128)(2,1)} %get-tuple-element.34), calls=%async_computation | async-start | bytes 524288 | tf_op jit(solution)/shard_map/all_to_all | solution.py:241
  12.9 3.5 %collective-permute-done.1.beside_ref = bf16[2,128,128]{2,1,0:T(8,128)(2,1)S(1)} collective-permute-done((bf16[2,128,128]{2,1,0:T(8,128)(2,1)S(1)}, bf16[2,128,128]{2,1,0:T(8,128)(2,1)S(1)}, u32[]{:S(2)}, u32[]{:S(2)}) %collective-permute-start.1) | collective-permute-done | bytes 65568 | tf_op jit(solution)/shard_map/ppermute | solution.py:50
  16.4 8.6 %collective-permute-start.3 = (bf16[2,2,128,128]{3,2,1,0:T(8,128)(2,1)S(1)}, bf16[2,2,128,128]{3,2,1,0:T(8,128)(2,1)S(1)}, u32[]{:S(2)}, u32[]{:S(2)}) collective-permute-start(bf16[2,2,128,128]{3,2,1,0:T(8,128)(2,1)S(1)} %pad_maximum_fusion.4), channel_id=1, source_target_pairs={{0,254},{1,255},{2,0},{3,1},{4,2},{5,3},{6,4},{7,5},{8,6},{9,7},{1... | collective-permute-start | bytes 393224 | tf_op jit(solution)/shard_map/ppermute | solution.py:54
  25.0 4.4 %collective-permute-done.2.behind_ref = bf16[2,2,128,128]{3,2,1,0:T(8,128)(2,1)S(1)} collective-permute-done((bf16[2,2,128,128]{3,2,1,0:T(8,128)(2,1)S(1)}, bf16[2,2,128,128]{3,2,1,0:T(8,128)(2,1)S(1)}, u32[]{:S(2)}, u32[]{:S(2)}) %collective-permute-start.2) | collective-permute-done | bytes 131104 | tf_op jit(solution)/shard_map/ppermute | solution.py:54
  30.9 4.0 %collective-permute-done.7 = bf16[8,128,128]{2,1,0:T(8,128)(2,1)S(1)} collective-permute-done((bf16[8,128,128]{2,1,0:T(8,128)(2,1)S(1)}, bf16[8,128,128]{2,1,0:T(8,128)(2,1)S(1)}, u32[]{:S(2)}, u32[]{:S(2)}) %collective-permute-start.7) | collective-permute-done | bytes 262176 | tf_op jit(solution)/shard_map/ppermute | solution.py:46
  37.0 2.4 %collective-permute-done.4 = bf16[8,128,128]{2,1,0:T(8,128)(2,1)S(1)} collective-permute-done((bf16[8,128,128]{2,1,0:T(8,128)(2,1)S(1)}, bf16[8,128,128]{2,1,0:T(8,128)(2,1)S(1)}, u32[]{:S(2)}, u32[]{:S(2)}) %collective-permute-start.4) | collective-permute-done | bytes 262176 | tf_op jit(solution)/shard_map/ppermute | solution.py:46
  39.7 2.5 %collective-permute-start.11 = (bf16[2,8,128,128]{3,2,1,0:T(8,128)(2,1)S(1)}, bf16[2,8,128,128]{3,2,1,0:T(8,128)(2,1)S(1)}, u32[]{:S(2)}, u32[]{:S(2)}) collective-permute-start(bf16[2,8,128,128]{3,2,1,0:T(8,128)(2,1)S(1)} %pad_maximum_fusion.refs_0_), channel_id=1, source_target_pairs={{0,24},{1,7},{2,26},{3,1},{4,28},{5,3},{6,30},{7,5},{8,0},{9,15},{... | collective-permute-start | bytes 1572872 | tf_op jit(solution)/shard_map/ppermute | solution.py:46
  42.2 2.8 %collective-permute-done.9.refs_1_ = bf16[2,8,128,128]{3,2,1,0:T(8,128)(2,1)S(1)} collective-permute-done((bf16[2,8,128,128]{3,2,1,0:T(8,128)(2,1)S(1)}, bf16[2,8,128,128]{3,2,1,0:T(8,128)(2,1)S(1)}, u32[]{:S(2)}, u32[]{:S(2)}) %collective-permute-start.9) | collective-permute-done | bytes 524320 | tf_op jit(solution)/shard_map/ppermute | solution.py:46
  49.0 2.8 %collective-permute-start = (s32[256]{0:T(256)}, s32[256]{0:T(256)S(1)}, u32[]{:S(2)}, u32[]{:S(2)}) collective-permute-start(s32[256]{0:T(256)} %own_row_ref.15), channel_id=1, source_target_pairs={{0,1},{1,0},{2,3},{3,2},{4,5},{5,4},{6,7},{7,6},{8,9},{9,8},{10,11... | collective-permute-start | bytes 3080 | tf_op jit(solution)/shard_map/ppermute | solution.py:50
  52.4 3.5 %collect.1.refs_2_ = bf16[2,8,4,4,128,128]{5,4,3,2,1,0:T(8,128)(2,1)S(1)} custom-call(s32[1]{0:T(128)} %bitcast.me_ref, bf16[8,4,4,2,128,128]{5,4,3,2,1,0:T(8,128)(2,1)} %bitcast.24, bf16[8,4,4,2,128,128]{5,4,3,2,1,0:T(8,128)(2,1)} %bitcast.8.other_ref), custom_call_target="tpu_custom_call" | custom-call | bytes 8388608 | tf_op jit(solution)/shard_map/collect/pallas_call | solution.py:147
  57.4 3.4 %copy-done.3 = bf16[112,128,128]{2,1,0:T(8,128)(2,1)S(1)} copy-done((bf16[112,128,128]{2,1,0:T(8,128)(2,1)S(1)}, bf16[112,128,128]{2,1,0:T(8,128)(2,1)}, u32[]{:S(2)}) %copy-start.3) | copy-done | bytes 3670040
  60.8 2.5 %sparse_sums.2.sparse_ref = f32[128,256]{1,0:T(8,128)S(1)} custom-call(s32[1]{0:T(128)} %bitcast.me_ref, s32[112]{0:T(128)S(1)} %copy-done.11, s32[112]{0:T(128)S(1)} %copy-done.12, s32[1]{0:T(128)S(6)} %copy.20.count_ref, s32[1,4]{1,0:T(1,128)S(1)} %copy-done.13, bf16[2,128,128]{2,1,0:T(8,128)(2,1)S(1)} %get-tuple-element.41.blocks_ref, ...), custom_call_target="tpu_custom_call" | custom-call | flops 469762048 | bytes 3670016 | tf_op jit(solution)/shard_map/sparse_sums/pallas_call | solution.py:120
  70.3 6.1 %all-to-all-start.1 = ((bf16[8,128,128]{2,1,0:T(8,128)(2,1)}), bf16[8,128,128]{2,1,0:T(8,128)(2,1)S(1)}, u32[]{:S(2)}, u32[]{:S(2)}) async-start(bf16[8,128,128]{2,1,0:T(8,128)(2,1)} %get-tuple-element.49), calls=%async_computation.1 | async-start | bytes 524288 | tf_op jit(solution)/shard_map/all_to_all | solution.py:241
  78.4 8.2 %collective-permute-start.17 = (bf16[2,2,128,128]{3,2,1,0:T(8,128)(2,1)S(1)}, bf16[2,2,128,128]{3,2,1,0:T(8,128)(2,1)S(1)}, u32[]{:S(2)}, u32[]{:S(2)}) collective-permute-start(bf16[2,2,128,128]{3,2,1,0:T(8,128)(2,1)S(1)} %pad_maximum_fusion.5), channel_id=1, source_target_pairs={{0,254},{1,255},{2,0},{3,1},{4,2},{5,3},{6,4},{7,5},{8,6},{9,7},{1... | collective-permute-start | bytes 393224 | tf_op jit(solution)/shard_map/ppermute | solution.py:54
  86.6 6.7 %collective-permute-done.16.behind_ref = bf16[2,2,128,128]{3,2,1,0:T(8,128)(2,1)S(1)} collective-permute-done((bf16[2,2,128,128]{3,2,1,0:T(8,128)(2,1)S(1)}, bf16[2,2,128,128]{3,2,1,0:T(8,128)(2,1)S(1)}, u32[]{:S(2)}, u32[]{:S(2)}) %collective-permute-start.16) | collective-permute-done | bytes 131104 | tf_op jit(solution)/shard_map/ppermute | solution.py:54
  94.8 4.0 %collective-permute-done.21 = bf16[8,128,128]{2,1,0:T(8,128)(2,1)S(1)} collective-permute-done((bf16[8,128,128]{2,1,0:T(8,128)(2,1)S(1)}, bf16[8,128,128]{2,1,0:T(8,128)(2,1)S(1)}, u32[]{:S(2)}, u32[]{:S(2)}) %collective-permute-start.21) | collective-permute-done | bytes 262176 | tf_op jit(solution)/shard_map/ppermute | solution.py:46
  103.5 2.7 %collective-permute-start.25 = (bf16[2,8,128,128]{3,2,1,0:T(8,128)(2,1)S(1)}, bf16[2,8,128,128]{3,2,1,0:T(8,128)(2,1)S(1)}, u32[]{:S(2)}, u32[]{:S(2)}) collective-permute-start(bf16[2,8,128,128]{3,2,1,0:T(8,128)(2,1)S(1)} %pad_maximum_fusion.2.refs_0_), channel_id=1, source_target_pairs={{0,24},{1,7},{2,26},{3,1},{4,28},{5,3},{6,30},{7,5},{8,0},{9,15},{... | collective-permute-start | bytes 1572872 | tf_op jit(solution)/shard_map/ppermute | solution.py:46
  106.1 3.3 %collective-permute-done.23.refs_1_ = bf16[2,8,128,128]{3,2,1,0:T(8,128)(2,1)S(1)} collective-permute-done((bf16[2,8,128,128]{3,2,1,0:T(8,128)(2,1)S(1)}, bf16[2,8,128,128]{3,2,1,0:T(8,128)(2,1)S(1)}, u32[]{:S(2)}, u32[]{:S(2)}) %collective-permute-start.23) | collective-permute-done | bytes 524320 | tf_op jit(solution)/shard_map/ppermute | solution.py:46
  109.4 2.4 %collective-permute-start.24 = (bf16[2,8,128,128]{3,2,1,0:T(8,128)(2,1)S(1)}, bf16[2,8,128,128]{3,2,1,0:T(8,128)(2,1)S(1)}, u32[]{:S(2)}, u32[]{:S(2)}) collective-permute-start(bf16[2,8,128,128]{3,2,1,0:T(8,128)(2,1)S(1)} %collective-permute-done.23.refs_1_), channel_id=1, source_target_pairs={{0,24},{1,7},{2,26},{3,1},{4,28},{5,3},{6,30},{7,5},{8,0},{9,15},{... | collective-permute-start | bytes 1572872 | tf_op jit(solution)/shard_map/ppermute | solution.py:46
  112.9 3.4 %copy-done.1 = bf16[2,8,4,4,128,128]{5,4,3,2,1,0:T(8,128)(2,1)S(1)} copy-done((bf16[2,8,4,4,128,128]{5,4,3,2,1,0:T(8,128)(2,1)S(1)}, bf16[2,8,4,4,128,128]{5,4,3,2,1,0:T(8,128)(2,1)}, u32[]{:S(2)}) %copy-start.1) | copy-done | bytes 8388632
  117.6 2.6 %copy-done.4 = bf16[112,128,128]{2,1,0:T(8,128)(2,1)S(1)} copy-done((bf16[112,128,128]{2,1,0:T(8,128)(2,1)S(1)}, bf16[112,128,128]{2,1,0:T(8,128)(2,1)}, u32[]{:S(2)}) %copy-start.4) | copy-done | bytes 3670040
  120.2 2.3 %sparse_sums.3.sparse_ref = f32[128,256]{1,0:T(8,128)S(1)} custom-call(s32[1]{0:T(128)} %bitcast.me_ref, s32[112]{0:T(128)S(1)} %copy-done.11, s32[112]{0:T(128)S(1)} %copy-done.12, s32[1]{0:T(128)S(6)} %copy.20.count_ref, s32[1,4]{1,0:T(1,128)S(1)} %copy-done.13, bf16[2,128,128]{2,1,0:T(8,128)(2,1)S(1)} %get-tuple-element.55.blocks_ref, ...), custom_call_target="tpu_custom_call" | custom-call | flops 469762048 | bytes 3670016 | tf_op jit(solution)/shard_map/sparse_sums/pallas_call | solution.py:120
  126.5 2.4 %collective-permute-start.27 = (f32[128,256]{1,0:T(8,128)S(1)}, f32[128,256]{1,0:T(8,128)S(1)}, u32[]{:S(2)}, u32[]{:S(2)}) collective-permute-start(f32[128,256]{1,0:T(8,128)S(1)} %slice_bitcast_fusion), channel_id=1, source_target_pairs={{0,1},{1,0},{2,3},{3,2},{4,5},{5,4},{6,7},{7,6},{8,9},{9,8},{10,11... | collective-permute-start | bytes 393224 | tf_op jit(solution)/shard_map/ppermute | solution.py:50
  (87 shorter events, 36.3 us)
Async XLA Ops:
  0.0 49.0 %collective-permute-start.12 = (bf16[256,128,128]{2,1,0:T(8,128)(2,1)}, bf16[256,128,128]{2,1,0:T(8,128)(2,1)}, u32[]{:S(2)}, u32[]{:S(2)}) collective-permute-start(bf16[256,128,128]{2,1,0:T(8,128)(2,1)} %param.22), channel_id=1, source_target_pairs={{0,1},{1,0},{2,3},{3,2},{4,5},{5,4},{6,7},{7,6},{8,9},{9,8},{10,11... | collective-permute-start | bytes 25165832 | tf_op jit(solution)/shard_map/ppermute | solution.py:50
  6.1 23.3 %all-to-all-start = ((bf16[8,128,128]{2,1,0:T(8,128)(2,1)}), bf16[8,128,128]{2,1,0:T(8,128)(2,1)S(1)}, u32[]{:S(2)}, u32[]{:S(2)}) async-start(bf16[8,128,128]{2,1,0:T(8,128)(2,1)} %get-tuple-element.34), calls=%async_computation | async-start | bytes 524288 | tf_op jit(solution)/shard_map/all_to_all | solution.py:241
  16.3 13.0 %collective-permute-start.2 = (bf16[2,2,128,128]{3,2,1,0:T(8,128)(2,1)S(1)}, bf16[2,2,128,128]{3,2,1,0:T(8,128)(2,1)S(1)}, u32[]{:S(2)}, u32[]{:S(2)}) collective-permute-start(bf16[2,2,128,128]{3,2,1,0:T(8,128)(2,1)S(1)} %pad_maximum_fusion.4), channel_id=1, source_target_pairs={{0,2},{1,3},{2,4},{3,5},{4,6},{5,7},{6,8},{7,9},{8,10},{9,11},{10,... | collective-permute-start | bytes 393224 | tf_op jit(solution)/shard_map/ppermute | solution.py:54
  16.4 13.0 %collective-permute-start.3 = (bf16[2,2,128,128]{3,2,1,0:T(8,128)(2,1)S(1)}, bf16[2,2,128,128]{3,2,1,0:T(8,128)(2,1)S(1)}, u32[]{:S(2)}, u32[]{:S(2)}) collective-permute-start(bf16[2,2,128,128]{3,2,1,0:T(8,128)(2,1)S(1)} %pad_maximum_fusion.4), channel_id=1, source_target_pairs={{0,254},{1,255},{2,0},{3,1},{4,2},{5,3},{6,4},{7,5},{8,6},{9,7},{1... | collective-permute-start | bytes 393224 | tf_op jit(solution)/shard_map/ppermute | solution.py:54
  29.4 7.2 %collective-permute-start.8 = (bf16[8,128,128]{2,1,0:T(8,128)(2,1)S(1)}, bf16[8,128,128]{2,1,0:T(8,128)(2,1)S(1)}, u32[]{:S(2)}, u32[]{:S(2)}) collective-permute-start(bf16[8,128,128]{2,1,0:T(8,128)(2,1)S(1)} %all-to-all-done), channel_id=1, source_target_pairs={{0,4},{1,17},{2,6},{3,19},{4,0},{5,21},{6,2},{7,23},{8,12},{9,25},... | collective-permute-start | bytes 786440 | tf_op jit(solution)/shard_map/ppermute | solution.py:46
  29.5 9.8 %collective-permute-start.4 = (bf16[8,128,128]{2,1,0:T(8,128)(2,1)S(1)}, bf16[8,128,128]{2,1,0:T(8,128)(2,1)S(1)}, u32[]{:S(2)}, u32[]{:S(2)}) collective-permute-start(bf16[8,128,128]{2,1,0:T(8,128)(2,1)S(1)} %all-to-all-done), channel_id=1, source_target_pairs={{0,2},{1,9},{2,4},{3,11},{4,6},{5,13},{6,0},{7,15},{8,10},{9,17},{... | collective-permute-start | bytes 786440 | tf_op jit(solution)/shard_map/ppermute | solution.py:46
  36.6 8.4 %collective-permute-start.9 = (bf16[2,8,128,128]{3,2,1,0:T(8,128)(2,1)S(1)}, bf16[2,8,128,128]{3,2,1,0:T(8,128)(2,1)S(1)}, u32[]{:S(2)}, u32[]{:S(2)}) collective-permute-start(bf16[2,8,128,128]{3,2,1,0:T(8,128)(2,1)S(1)} %pad_maximum_fusion.1.refs_1_), channel_id=1, source_target_pairs={{0,24},{1,7},{2,26},{3,1},{4,28},{5,3},{6,30},{7,5},{8,0},{9,15},{... | collective-permute-start | bytes 1572872 | tf_op jit(solution)/shard_map/ppermute | solution.py:46
  39.4 9.6 %collective-permute-start.5 = (bf16[2,8,128,128]{3,2,1,0:T(8,128)(2,1)S(1)}, bf16[2,8,128,128]{3,2,1,0:T(8,128)(2,1)S(1)}, u32[]{:S(2)}, u32[]{:S(2)}) collective-permute-start(bf16[2,8,128,128]{3,2,1,0:T(8,128)(2,1)S(1)} %pad_maximum_fusion.refs_0_), channel_id=1, source_target_pairs={{0,8},{1,3},{2,10},{3,5},{4,12},{5,7},{6,14},{7,1},{8,16},{9,11},{... | collective-permute-start | bytes 1572872 | tf_op jit(solution)/shard_map/ppermute | solution.py:46
  39.5 23.8 %collective-permute-start.13 = (bf16[2,8,128,128]{3,2,1,0:T(8,128)(2,1)S(1)}, bf16[2,8,128,128]{3,2,1,0:T(8,128)(2,1)S(1)}, u32[]{:S(2)}, u32[]{:S(2)}) collective-permute-start(bf16[2,8,128,128]{3,2,1,0:T(8,128)(2,1)S(1)} %pad_maximum_fusion.1.refs_1_), channel_id=1, source_target_pairs={{0,8},{1,3},{2,10},{3,5},{4,12},{5,7},{6,14},{7,1},{8,16},{9,11},{... | collective-permute-start | bytes 1572872 | tf_op jit(solution)/shard_map/ppermute | solution.py:46
  39.7 24.9 %collective-permute-start.11 = (bf16[2,8,128,128]{3,2,1,0:T(8,128)(2,1)S(1)}, bf16[2,8,128,128]{3,2,1,0:T(8,128)(2,1)S(1)}, u32[]{:S(2)}, u32[]{:S(2)}) collective-permute-start(bf16[2,8,128,128]{3,2,1,0:T(8,128)(2,1)S(1)} %pad_maximum_fusion.refs_0_), channel_id=1, source_target_pairs={{0,24},{1,7},{2,26},{3,1},{4,28},{5,3},{6,30},{7,5},{8,0},{9,15},{... | collective-permute-start | bytes 1572872 | tf_op jit(solution)/shard_map/ppermute | solution.py:46
  45.0 20.9 %collective-permute-start.10 = (bf16[2,8,128,128]{3,2,1,0:T(8,128)(2,1)S(1)}, bf16[2,8,128,128]{3,2,1,0:T(8,128)(2,1)S(1)}, u32[]{:S(2)}, u32[]{:S(2)}) collective-permute-start(bf16[2,8,128,128]{3,2,1,0:T(8,128)(2,1)S(1)} %collective-permute-done.9.refs_1_), channel_id=1, source_target_pairs={{0,24},{1,7},{2,26},{3,1},{4,28},{5,3},{6,30},{7,5},{8,0},{9,15},{... | collective-permute-start | bytes 1572872 | tf_op jit(solution)/shard_map/ppermute | solution.py:46
  49.0 16.9 %collective-permute-start.6 = (bf16[2,8,128,128]{3,2,1,0:T(8,128)(2,1)S(1)}, bf16[2,8,128,128]{3,2,1,0:T(8,128)(2,1)S(1)}, u32[]{:S(2)}, u32[]{:S(2)}) collective-permute-start(bf16[2,8,128,128]{3,2,1,0:T(8,128)(2,1)S(1)} %collective-permute-done.5.refs_0_), channel_id=1, source_target_pairs={{0,8},{1,3},{2,10},{3,5},{4,12},{5,7},{6,14},{7,1},{8,16},{9,11},{... | collective-permute-start | bytes 1572872 | tf_op jit(solution)/shard_map/ppermute | solution.py:46
  49.0 7.0 %collective-permute-start = (s32[256]{0:T(256)}, s32[256]{0:T(256)S(1)}, u32[]{:S(2)}, u32[]{:S(2)}) collective-permute-start(s32[256]{0:T(256)} %own_row_ref.15), channel_id=1, source_target_pairs={{0,1},{1,0},{2,3},{3,2},{4,5},{5,4},{6,7},{7,6},{8,9},{9,8},{10,11... | collective-permute-start | bytes 3080 | tf_op jit(solution)/shard_map/ppermute | solution.py:50
  70.3 23.0 %all-to-all-start.1 = ((bf16[8,128,128]{2,1,0:T(8,128)(2,1)}), bf16[8,128,128]{2,1,0:T(8,128)(2,1)S(1)}, u32[]{:S(2)}, u32[]{:S(2)}) async-start(bf16[8,128,128]{2,1,0:T(8,128)(2,1)} %get-tuple-element.49), calls=%async_computation.1 | async-start | bytes 524288 | tf_op jit(solution)/shard_map/all_to_all | solution.py:241
  78.0 15.3 %collective-permute-start.16 = (bf16[2,2,128,128]{3,2,1,0:T(8,128)(2,1)S(1)}, bf16[2,2,128,128]{3,2,1,0:T(8,128)(2,1)S(1)}, u32[]{:S(2)}, u32[]{:S(2)}) collective-permute-start(bf16[2,2,128,128]{3,2,1,0:T(8,128)(2,1)S(1)} %pad_maximum_fusion.5), channel_id=1, source_target_pairs={{0,2},{1,3},{2,4},{3,5},{4,6},{5,7},{6,8},{7,9},{8,10},{9,11},{10,... | collective-permute-start | bytes 393224 | tf_op jit(solution)/shard_map/ppermute | solution.py:54
  78.4 14.9 %collective-permute-start.17 = (bf16[2,2,128,128]{3,2,1,0:T(8,128)(2,1)S(1)}, bf16[2,2,128,128]{3,2,1,0:T(8,128)(2,1)S(1)}, u32[]{:S(2)}, u32[]{:S(2)}) collective-permute-start(bf16[2,2,128,128]{3,2,1,0:T(8,128)(2,1)S(1)} %pad_maximum_fusion.5), channel_id=1, source_target_pairs={{0,254},{1,255},{2,0},{3,1},{4,2},{5,3},{6,4},{7,5},{8,6},{9,7},{1... | collective-permute-start | bytes 393224 | tf_op jit(solution)/shard_map/ppermute | solution.py:54
  93.3 7.2 %collective-permute-start.22 = (bf16[8,128,128]{2,1,0:T(8,128)(2,1)S(1)}, bf16[8,128,128]{2,1,0:T(8,128)(2,1)S(1)}, u32[]{:S(2)}, u32[]{:S(2)}) collective-permute-start(bf16[8,128,128]{2,1,0:T(8,128)(2,1)S(1)} %all-to-all-done.1), channel_id=1, source_target_pairs={{0,4},{1,17},{2,6},{3,19},{4,0},{5,21},{6,2},{7,23},{8,12},{9,25},... | collective-permute-start | bytes 786440 | tf_op jit(solution)/shard_map/ppermute | solution.py:46
  93.4 9.8 %collective-permute-start.18 = (bf16[8,128,128]{2,1,0:T(8,128)(2,1)S(1)}, bf16[8,128,128]{2,1,0:T(8,128)(2,1)S(1)}, u32[]{:S(2)}, u32[]{:S(2)}) collective-permute-start(bf16[8,128,128]{2,1,0:T(8,128)(2,1)S(1)} %all-to-all-done.1), channel_id=1, source_target_pairs={{0,2},{1,9},{2,4},{3,11},{4,6},{5,13},{6,0},{7,15},{8,10},{9,17},{... | collective-permute-start | bytes 786440 | tf_op jit(solution)/shard_map/ppermute | solution.py:46
  100.5 8.9 %collective-permute-start.23 = (bf16[2,8,128,128]{3,2,1,0:T(8,128)(2,1)S(1)}, bf16[2,8,128,128]{3,2,1,0:T(8,128)(2,1)S(1)}, u32[]{:S(2)}, u32[]{:S(2)}) collective-permute-start(bf16[2,8,128,128]{3,2,1,0:T(8,128)(2,1)S(1)} %pad_maximum_fusion.3.refs_1_), channel_id=1, source_target_pairs={{0,24},{1,7},{2,26},{3,1},{4,28},{5,3},{6,30},{7,5},{8,0},{9,15},{... | collective-permute-start | bytes 1572872 | tf_op jit(solution)/shard_map/ppermute | solution.py:46
  103.3 9.6 %collective-permute-start.19 = (bf16[2,8,128,128]{3,2,1,0:T(8,128)(2,1)S(1)}, bf16[2,8,128,128]{3,2,1,0:T(8,128)(2,1)S(1)}, u32[]{:S(2)}, u32[]{:S(2)}) collective-permute-start(bf16[2,8,128,128]{3,2,1,0:T(8,128)(2,1)S(1)} %pad_maximum_fusion.2.refs_0_), channel_id=1, source_target_pairs={{0,8},{1,3},{2,10},{3,5},{4,12},{5,7},{6,14},{7,1},{8,16},{9,11},{... | collective-permute-start | bytes 1572872 | tf_op jit(solution)/shard_map/ppermute | solution.py:46
  103.4 19.1 %collective-permute-start.26 = (bf16[2,8,128,128]{3,2,1,0:T(8,128)(2,1)S(1)}, bf16[2,8,128,128]{3,2,1,0:T(8,128)(2,1)S(1)}, u32[]{:S(2)}, u32[]{:S(2)}) collective-permute-start(bf16[2,8,128,128]{3,2,1,0:T(8,128)(2,1)S(1)} %pad_maximum_fusion.3.refs_1_), channel_id=1, source_target_pairs={{0,8},{1,3},{2,10},{3,5},{4,12},{5,7},{6,14},{7,1},{8,16},{9,11},{... | collective-permute-start | bytes 1572872 | tf_op jit(solution)/shard_map/ppermute | solution.py:46
  103.5 20.4 %collective-permute-start.25 = (bf16[2,8,128,128]{3,2,1,0:T(8,128)(2,1)S(1)}, bf16[2,8,128,128]{3,2,1,0:T(8,128)(2,1)S(1)}, u32[]{:S(2)}, u32[]{:S(2)}) collective-permute-start(bf16[2,8,128,128]{3,2,1,0:T(8,128)(2,1)S(1)} %pad_maximum_fusion.2.refs_0_), channel_id=1, source_target_pairs={{0,24},{1,7},{2,26},{3,1},{4,28},{5,3},{6,30},{7,5},{8,0},{9,15},{... | collective-permute-start | bytes 1572872 | tf_op jit(solution)/shard_map/ppermute | solution.py:46
  109.4 15.8 %collective-permute-start.24 = (bf16[2,8,128,128]{3,2,1,0:T(8,128)(2,1)S(1)}, bf16[2,8,128,128]{3,2,1,0:T(8,128)(2,1)S(1)}, u32[]{:S(2)}, u32[]{:S(2)}) collective-permute-start(bf16[2,8,128,128]{3,2,1,0:T(8,128)(2,1)S(1)} %collective-permute-done.23.refs_1_), channel_id=1, source_target_pairs={{0,24},{1,7},{2,26},{3,1},{4,28},{5,3},{6,30},{7,5},{8,0},{9,15},{... | collective-permute-start | bytes 1572872 | tf_op jit(solution)/shard_map/ppermute | solution.py:46
  112.9 12.3 %collective-permute-start.20 = (bf16[2,8,128,128]{3,2,1,0:T(8,128)(2,1)S(1)}, bf16[2,8,128,128]{3,2,1,0:T(8,128)(2,1)S(1)}, u32[]{:S(2)}, u32[]{:S(2)}) collective-permute-start(bf16[2,8,128,128]{3,2,1,0:T(8,128)(2,1)S(1)} %collective-permute-done.19.refs_0_), channel_id=1, source_target_pairs={{0,8},{1,3},{2,10},{3,5},{4,12},{5,7},{6,14},{7,1},{8,16},{9,11},{... | collective-permute-start | bytes 1572872 | tf_op jit(solution)/shard_map/ppermute | solution.py:46
  (20 other events, 82.1 us)

commit v7 on v6

--- a/solution.py
+++ b/solution.py
@@ -50,8 +50,8 @@
     return lax.ppermute(array, "blk", [(i, i ^ 1) for i in range(SHARDS)])
 
 
-def from_behind(array, by):
-    return lax.ppermute(array, "blk", [(i, (i + by) % SHARDS) for i in range(SHARDS)])
+def from_chips(array):
+    return lax.ppermute(array, "blk", [(i, (i + (-NC if i % NC else NC)) % SHARDS) for i in range(SHARDS)])
 
 
 def placed_pair(block, row):
@@ -82,17 +82,17 @@
     )(me, hub_block, features)
 
 
-def sparse_kernel(me_ref, row_ref, src_ref, count_ref, fetch_ref, blocks_ref, beside_ref, behind_ref, ahead_ref, tiles_ref, out_ref, placed_ref):
+def sparse_kernel(me_ref, row_ref, src_ref, count_ref, fetch_ref, blocks_ref, beside_ref, fetched_ref, shared_ref, tiles_ref, out_ref, placed_ref):
     zeros = jnp.zeros((TILE, F), jnp.bfloat16)
-    even = me_ref[0] % 2 == 0
-    before, after = fetch_ref[0, 1], fetch_ref[0, 2]
+    even = me_ref[0] % NC == 0
+    wanted = [fetch_ref[0, entry] for entry in range(2 * HOPS)]
     blocks = [
         blocks_ref[0],
         blocks_ref[1],
-        behind_ref[0, fetch_ref[0, 0]],
-        jnp.where(even, behind_ref[1, before], beside_ref[before]),
-        jnp.where(even, beside_ref[after], ahead_ref[1, after]),
-        ahead_ref[0, fetch_ref[0, 3]],
+        jnp.where(even, fetched_ref[0, wanted[0]], shared_ref[1, wanted[0]]),
+        jnp.where(even, fetched_ref[1, wanted[1]], beside_ref[wanted[1]]),
+        jnp.where(even, beside_ref[wanted[2]], fetched_ref[1, wanted[2]]),
+        jnp.where(even, shared_ref[1, wanted[3]], fetched_ref[0, wanted[3]]),
     ]
     for source in range(SOURCES):
         placed_ref[2 * source] = jnp.concatenate([blocks[source], zeros], axis=1)
@@ -239,20 +239,23 @@
 
     def propagate(blocks, copies, weight, dtype, wide, tiles=None):
         column = lax.all_to_all(copies, "blk", 0, 0, axis_index_groups=groups_along_z(), tiled=True)
+        blocks, column = lax.optimization_barrier((blocks, column))
         beside = swap_cores(blocks)
         pair = jnp.stack([blocks, beside])
-        fetched = [from_behind(pair, NC), from_behind(pair, -NC)]
-        column, fetched = lax.optimization_barrier((column, fetched))
-        near = [step(column, 1, True), step(column, -1, True)]
+        side_behind = step(column, 1, True)
+        side_ahead = step(column, -1, True)
         opposite = step(column, 2, True)
-        first, last = jnp.stack([column, near[0]]), jnp.stack([near[1], opposite])
+        fetched = from_chips(pair)
+        first, last = jnp.stack([column, side_behind]), jnp.stack([side_ahead, opposite])
         if tiles is None:
             tiles = collect(me, dense_tiles, lax.optimization_barrier((first, other_tiles))[1])
-        behind_first, ahead_last = step(first, 1, False), step(last, -1, False)
+        behind_first = step(first, 1, False)
+        ahead_last = step(last, -1, False)
         behind_last, ahead_first = step(last, 1, False), step(first, -1, False)
+        shared = swap_cores(fetched)
         far = (step(behind_first, 1, False), step(ahead_last, -1, False))
         total = dense_part(me, 0, rows, (first, last), tiles, zeros)
-        near_blocks, total = lax.optimization_barrier(((blocks, beside, *fetched), total))
+        near_blocks, total = lax.optimization_barrier(((blocks, beside, fetched, shared), total))
         sparse = sparse_sums(me, sparse_row, sparse_src, sparse_count, fetch_list, near_blocks, sparse_tiles)
         total = dense_part(me, SIDE - 1, rows, (behind_first, behind_last), tiles, total)
         total = dense_part(me, 1, rows, (ahead_first, ahead_last), tiles, total)

time: 133 us -> 133 us (level)
  the two profiles are of different devices: /device:TPU:1 before, /device:TPU:35 now
where the time goes in v7:
time: 133 us
  starting transfers between devices  48.1 us (36%)
  waiting for transfers between devices  28.4 us (21%)
  blocking collectives  28.3 us (21%)
  Pallas kernels  24.5 us (18%)
  local copies, waits for them, and re-layouts  2.3 us (2%)
    all_to_all x2, blocking collectives, propagate(): lax.all_to_all(copies, 'blk', 0, 0, axis_index_groups=groups_along_z(), t...  28.3 us
    ppermute x8, starting transfers between devices, swap_cores(): return lax.ppermute(array, 'blk', [(i, i ^ 1) for i in range(SHARDS)])  22.2 us
    ppermute x18, starting transfers between devices, step(): return lax.ppermute(array, 'blk', pairs)  21 us
    ppermute x18, waiting for transfers between devices, step(): return lax.ppermute(array, 'blk', pairs)  13.3 us
    pallas_call x8, Pallas kernels, dense_part(): pl.pallas_call(functools.partial(dense_kernel, len(chunks)), out_shape=ja...  10.5 us
    ppermute x2, waiting for transfers between devices, from_chips(): lax.ppermute(array, 'blk', [(i, (i + (-NC if i % NC else NC)) % SHARDS) f...  10.1 us
    pallas_call x2, Pallas kernels, sparse_sums(): pl.pallas_call(sparse_kernel, out_shape=jax.ShapeDtypeStruct((TILE, NB *...  7.55 us
    ppermute x8, waiting for transfers between devices, swap_cores(): return lax.ppermute(array, 'blk', [(i, i ^ 1) for i in range(SHARDS)])  4.95 us
  transfers between devices with their start and end apart: 28, of which 11 were waited for; matrix products, arithmetic and copies ran while one was open for 0% of the time, Pallas kernels for 15%

profile of v7, /device:TPU:35, one launch (start us, length us, event | category | flops | bytes accessed | tf_op | source)
XLA Modules:
  0.0 132.8 jit_solution(15904465428986492707)
XLA Ops:
  2.9 16.9 %all_to_all.10 = bf16[8,128,128]{2,1,0:T(8,128)(2,1)S(1)} all-to-all(bf16[8,128,128]{2,1,0:T(8,128)(2,1)S(1)} %get-tuple-element.33), channel_id=1, replica_groups={{0,32,64,96,128,160,192,224},{1,33,65,97,129,161,193,225},{2,34,66,98,1..., dimensions={0} | all-to-all | bytes 524288 | tf_op jit(solution)/shard_map/all_to_all | solution.py:241
  21.2 1.8 %collective-permute-start.5 = (bf16[8,128,128]{2,1,0:T(8,128)(2,1)S(1)}, bf16[8,128,128]{2,1,0:T(8,128)(2,1)S(1)}, u32[]{:S(2)}, u32[]{:S(2)}) collective-permute-start(bf16[8,128,128]{2,1,0:T(8,128)(2,1)S(1)} %all_to_all.10), channel_id=1, source_target_pairs={{0,4},{1,17},{2,6},{3,19},{4,0},{5,21},{6,2},{7,23},{8,12},{9,25},... | collective-permute-start | bytes 786440 | tf_op jit(solution)/shard_map/ppermute | solution.py:46
  23.0 1.9 %collective-permute-done.1 = bf16[8,128,128]{2,1,0:T(8,128)(2,1)S(1)} collective-permute-done((bf16[8,128,128]{2,1,0:T(8,128)(2,1)S(1)}, bf16[8,128,128]{2,1,0:T(8,128)(2,1)S(1)}, u32[]{:S(2)}, u32[]{:S(2)}) %collective-permute-start.1) | collective-permute-done | bytes 262176 | tf_op jit(solution)/shard_map/ppermute | solution.py:46
  25.0 1.4 %collective-permute-start.2 = (bf16[2,8,128,128]{3,2,1,0:T(8,128)(2,1)S(1)}, bf16[2,8,128,128]{3,2,1,0:T(8,128)(2,1)S(1)}, u32[]{:S(2)}, u32[]{:S(2)}) collective-permute-start(bf16[2,8,128,128]{3,2,1,0:T(8,128)(2,1)S(1)} %pad_maximum_fusion.refs_0_), channel_id=1, source_target_pairs={{0,8},{1,3},{2,10},{3,5},{4,12},{5,7},{6,14},{7,1},{8,16},{9,11},{... | collective-permute-start | bytes 1572872 | tf_op jit(solution)/shard_map/ppermute | solution.py:46
  26.4 3.5 %collective-permute-done.5 = bf16[8,128,128]{2,1,0:T(8,128)(2,1)S(1)} collective-permute-done((bf16[8,128,128]{2,1,0:T(8,128)(2,1)S(1)}, bf16[8,128,128]{2,1,0:T(8,128)(2,1)S(1)}, u32[]{:S(2)}, u32[]{:S(2)}) %collective-permute-start.5) | collective-permute-done | bytes 262176 | tf_op jit(solution)/shard_map/ppermute | solution.py:46
  30.0 2.8 %collective-permute-start.6 = (bf16[2,8,128,128]{3,2,1,0:T(8,128)(2,1)S(1)}, bf16[2,8,128,128]{3,2,1,0:T(8,128)(2,1)S(1)}, u32[]{:S(2)}, u32[]{:S(2)}) collective-permute-start(bf16[2,8,128,128]{3,2,1,0:T(8,128)(2,1)S(1)} %pad_maximum_fusion.1.refs_1_), channel_id=1, source_target_pairs={{0,24},{1,7},{2,26},{3,1},{4,28},{5,3},{6,30},{7,5},{8,0},{9,15},{... | collective-permute-start | bytes 1572872 | tf_op jit(solution)/shard_map/ppermute | solution.py:46
  32.8 4.7 %collective-permute-start.11 = (bf16[2,128,128]{2,1,0:T(8,128)(2,1)S(1)}, bf16[2,128,128]{2,1,0:T(8,128)(2,1)S(1)}, u32[]{:S(2)}, u32[]{:S(2)}) collective-permute-start(bf16[2,128,128]{2,1,0:T(8,128)(2,1)S(1)} %get-tuple-element.38.blocks_ref), channel_id=1, source_target_pairs={{0,1},{1,0},{2,3},{3,2},{4,5},{5,4},{6,7},{7,6},{8,9},{9,8},{10,11... | collective-permute-start | bytes 196616 | tf_op jit(solution)/shard_map/ppermute | solution.py:50
  39.8 1.4 %collective-permute-done.other_row_ref = s32[256]{0:T(256)S(1)} collective-permute-done((s32[256]{0:T(256)}, s32[256]{0:T(256)S(1)}, u32[]{:S(2)}, u32[]{:S(2)}) %collective-permute-start) | collective-permute-done | bytes 1056 | tf_op jit(solution)/shard_map/ppermute | solution.py:50
  41.3 1.8 %collective-permute-done.12.fetched_ref = bf16[2,2,128,128]{3,2,1,0:T(8,128)(2,1)S(1)} collective-permute-done((bf16[2,2,128,128]{3,2,1,0:T(8,128)(2,1)S(1)}, bf16[2,2,128,128]{3,2,1,0:T(8,128)(2,1)S(1)}, u32[]{:S(2)}, u32[]{:S(2)}) %collective-permute-start.12) | collective-permute-done | bytes 131104 | tf_op jit(solution)/shard_map/ppermute | solution.py:54
  43.1 3.2 %collective-permute-start.8 = (bf16[2,8,128,128]{3,2,1,0:T(8,128)(2,1)S(1)}, bf16[2,8,128,128]{3,2,1,0:T(8,128)(2,1)S(1)}, u32[]{:S(2)}, u32[]{:S(2)}) collective-permute-start(bf16[2,8,128,128]{3,2,1,0:T(8,128)(2,1)S(1)} %pad_maximum_fusion.refs_0_), channel_id=1, source_target_pairs={{0,24},{1,7},{2,26},{3,1},{4,28},{5,3},{6,30},{7,5},{8,0},{9,15},{... | collective-permute-start | bytes 1572872 | tf_op jit(solution)/shard_map/ppermute | solution.py:46
  46.3 2.7 %collective-permute-start.7 = (bf16[2,8,128,128]{3,2,1,0:T(8,128)(2,1)S(1)}, bf16[2,8,128,128]{3,2,1,0:T(8,128)(2,1)S(1)}, u32[]{:S(2)}, u32[]{:S(2)}) collective-permute-start(bf16[2,8,128,128]{3,2,1,0:T(8,128)(2,1)S(1)} %collective-permute-done.6.refs_1_), channel_id=1, source_target_pairs={{0,24},{1,7},{2,26},{3,1},{4,28},{5,3},{6,30},{7,5},{8,0},{9,15},{... | collective-permute-start | bytes 1572872 | tf_op jit(solution)/shard_map/ppermute | solution.py:46
  49.0 4.4 %collective-permute-start.13 = (bf16[2,2,128,128]{3,2,1,0:T(8,128)(2,1)S(1)}, bf16[2,2,128,128]{3,2,1,0:T(8,128)(2,1)S(1)}, u32[]{:S(2)}, u32[]{:S(2)}) collective-permute-start(bf16[2,2,128,128]{3,2,1,0:T(8,128)(2,1)S(1)} %collective-permute-done.12.fetched_ref), channel_id=1, source_target_pairs={{0,1},{1,0},{2,3},{3,2},{4,5},{5,4},{6,7},{7,6},{8,9},{9,8},{10,11... | collective-permute-start | bytes 393224 | tf_op jit(solution)/shard_map/ppermute | solution.py:50
  54.0 3.5 %collect.1.refs_2_ = bf16[2,8,4,4,128,128]{5,4,3,2,1,0:T(8,128)(2,1)S(1)} custom-call(s32[1]{0:T(128)} %bitcast.me_ref, bf16[8,4,4,2,128,128]{5,4,3,2,1,0:T(8,128)(2,1)} %bitcast.24, bf16[8,4,4,2,128,128]{5,4,3,2,1,0:T(8,128)(2,1)} %bitcast.6.other_ref), custom_call_target="tpu_custom_call" | custom-call | bytes 8388608 | tf_op jit(solution)/shard_map/collect/pallas_call | solution.py:147
  59.6 3.9 %sparse_sums.2.sparse_ref = f32[128,256]{1,0:T(8,128)S(1)} custom-call(s32[1]{0:T(128)} %bitcast.me_ref, s32[112]{0:T(128)S(1)} %copy-done.7, s32[112]{0:T(128)S(1)} %copy-done.8, s32[1]{0:T(128)S(6)} %copy.20.count_ref, s32[1,4]{1,0:T(1,128)S(1)} %copy-done.9, bf16[2,128,128]{2,1,0:T(8,128)(2,1)S(1)} %get-tuple-element.38.blocks_ref, ...), custom_call_target="tpu_custom_call" | custom-call | flops 469762048 | bytes 3670016 | tf_op jit(solution)/shard_map/sparse_sums/pallas_call | solution.py:120
  69.8 11.4 %all_to_all.11 = bf16[8,128,128]{2,1,0:T(8,128)(2,1)S(1)} all-to-all(bf16[8,128,128]{2,1,0:T(8,128)(2,1)S(1)} %get-tuple-element.47), channel_id=1, replica_groups={{0,32,64,96,128,160,192,224},{1,33,65,97,129,161,193,225},{2,34,66,98,1..., dimensions={0} | all-to-all | bytes 524288 | tf_op jit(solution)/shard_map/all_to_all | solution.py:241
  83.5 6.0 %collective-permute-done.18 = bf16[8,128,128]{2,1,0:T(8,128)(2,1)S(1)} collective-permute-done((bf16[8,128,128]{2,1,0:T(8,128)(2,1)S(1)}, bf16[8,128,128]{2,1,0:T(8,128)(2,1)S(1)}, u32[]{:S(2)}, u32[]{:S(2)}) %collective-permute-start.18) | collective-permute-done | bytes 262176 | tf_op jit(solution)/shard_map/ppermute | solution.py:46
  89.7 1.7 %collective-permute-done.15 = bf16[8,128,128]{2,1,0:T(8,128)(2,1)S(1)} collective-permute-done((bf16[8,128,128]{2,1,0:T(8,128)(2,1)S(1)}, bf16[8,128,128]{2,1,0:T(8,128)(2,1)S(1)}, u32[]{:S(2)}, u32[]{:S(2)}) %collective-permute-start.15) | collective-permute-done | bytes 262176 | tf_op jit(solution)/shard_map/ppermute | solution.py:46
  91.6 4.2 %collective-permute-start.24 = (bf16[2,128,128]{2,1,0:T(8,128)(2,1)S(1)}, bf16[2,128,128]{2,1,0:T(8,128)(2,1)S(1)}, u32[]{:S(2)}, u32[]{:S(2)}) collective-permute-start(bf16[2,128,128]{2,1,0:T(8,128)(2,1)S(1)} %get-tuple-element.51.blocks_ref), channel_id=1, source_target_pairs={{0,1},{1,0},{2,3},{3,2},{4,5},{5,4},{6,7},{7,6},{8,9},{9,8},{10,11... | collective-permute-start | bytes 196616 | tf_op jit(solution)/shard_map/ppermute | solution.py:50
  95.7 3.6 %collective-permute-start.22 = (bf16[2,8,128,128]{3,2,1,0:T(8,128)(2,1)S(1)}, bf16[2,8,128,128]{3,2,1,0:T(8,128)(2,1)S(1)}, u32[]{:S(2)}, u32[]{:S(2)}) collective-permute-start(bf16[2,8,128,128]{3,2,1,0:T(8,128)(2,1)S(1)} %pad_maximum_fusion.2.refs_0_), channel_id=1, source_target_pairs={{0,24},{1,7},{2,26},{3,1},{4,28},{5,3},{6,30},{7,5},{8,0},{9,15},{... | collective-permute-start | bytes 1572872 | tf_op jit(solution)/shard_map/ppermute | solution.py:46
  100.9 3.5 %collective-permute-start.25 = (bf16[2,2,128,128]{3,2,1,0:T(8,128)(2,1)S(1)}, bf16[2,2,128,128]{3,2,1,0:T(8,128)(2,1)S(1)}, u32[]{:S(2)}, u32[]{:S(2)}) collective-permute-start(bf16[2,2,128,128]{3,2,1,0:T(8,128)(2,1)S(1)} %pad_maximum_fusion.5), channel_id=1, source_target_pairs={{0,2},{1,255},{2,4},{3,1},{4,6},{5,3},{6,8},{7,5},{8,10},{9,7},{10... | collective-permute-start | bytes 393224 | tf_op jit(solution)/shard_map/ppermute | solution.py:54
  104.4 8.3 %collective-permute-done.25.fetched_ref = bf16[2,2,128,128]{3,2,1,0:T(8,128)(2,1)S(1)} collective-permute-done((bf16[2,2,128,128]{3,2,1,0:T(8,128)(2,1)S(1)}, bf16[2,2,128,128]{3,2,1,0:T(8,128)(2,1)S(1)}, u32[]{:S(2)}, u32[]{:S(2)}) %collective-permute-start.25) | collective-permute-done | bytes 131104 | tf_op jit(solution)/shard_map/ppermute | solution.py:54
  112.7 8.0 %collective-permute-start.26 = (bf16[2,2,128,128]{3,2,1,0:T(8,128)(2,1)S(1)}, bf16[2,2,128,128]{3,2,1,0:T(8,128)(2,1)S(1)}, u32[]{:S(2)}, u32[]{:S(2)}) collective-permute-start(bf16[2,2,128,128]{3,2,1,0:T(8,128)(2,1)S(1)} %collective-permute-done.25.fetched_ref), channel_id=1, source_target_pairs={{0,1},{1,0},{2,3},{3,2},{4,5},{5,4},{6,7},{7,6},{8,9},{9,8},{10,11... | collective-permute-start | bytes 393224 | tf_op jit(solution)/shard_map/ppermute | solution.py:50
  122.1 3.7 %sparse_sums.3.sparse_ref = f32[128,256]{1,0:T(8,128)S(1)} custom-call(s32[1]{0:T(128)} %bitcast.me_ref, s32[112]{0:T(128)S(1)} %copy-done.7, s32[112]{0:T(128)S(1)} %copy-done.8, s32[1]{0:T(128)S(6)} %copy.20.count_ref, s32[1,4]{1,0:T(1,128)S(1)} %copy-done.9, bf16[2,128,128]{2,1,0:T(8,128)(2,1)S(1)} %get-tuple-element.51.blocks_ref, ...), custom_call_target="tpu_custom_call" | custom-call | flops 469762048 | bytes 3670016 | tf_op jit(solution)/shard_map/sparse_sums/pallas_call | solution.py:120
  131.3 1.5 %finish.3 = f32[2,128,128]{2,1,0:T(8,128)} custom-call(s32[1]{0:T(128)} %bitcast.me_ref, s32[256]{0:T(256)S(1)} %copy-done.6, f32[2,128,256]{2,1,0:T(8,128)S(1)} %dense_part.15.dense_ref, f32[128,256]{1,0:T(8,128)S(1)} %collective-permute-done.27.other_ref, f32[128,256]{1,0:T(8,128)S(1)} %sparse_sums.3.sparse_ref, f32[128,128]{1,0:T(8,128)S(1)} %copy-done.3), custom_call_target="tpu_custom_call" | custom-call | tf_op jit(solution)/shard_map/finish/pallas_call | solution.py:212
  (77 shorter events, 26.1 us)
Async XLA Ops:
  0.0 49.0 %collective-permute-start.9 = (bf16[256,128,128]{2,1,0:T(8,128)(2,1)}, bf16[256,128,128]{2,1,0:T(8,128)(2,1)}, u32[]{:S(2)}, u32[]{:S(2)}) collective-permute-start(bf16[256,128,128]{2,1,0:T(8,128)(2,1)} %param.22), channel_id=1, source_target_pairs={{0,1},{1,0},{2,3},{3,2},{4,5},{5,4},{6,7},{7,6},{8,9},{9,8},{10,11... | collective-permute-start | bytes 25165832 | tf_op jit(solution)/shard_map/ppermute | solution.py:50
  19.7 5.2 %collective-permute-start.1 = (bf16[8,128,128]{2,1,0:T(8,128)(2,1)S(1)}, bf16[8,128,128]{2,1,0:T(8,128)(2,1)S(1)}, u32[]{:S(2)}, u32[]{:S(2)}) collective-permute-start(bf16[8,128,128]{2,1,0:T(8,128)(2,1)S(1)} %all_to_all.10), channel_id=1, source_target_pairs={{0,2},{1,9},{2,4},{3,11},{4,6},{5,13},{6,0},{7,15},{8,10},{9,17},{... | collective-permute-start | bytes 786440 | tf_op jit(solution)/shard_map/ppermute | solution.py:46
  20.9 5.4 %collective-permute-start.4 = (bf16[8,128,128]{2,1,0:T(8,128)(2,1)S(1)}, bf16[8,128,128]{2,1,0:T(8,128)(2,1)S(1)}, u32[]{:S(2)}, u32[]{:S(2)}) collective-permute-start(bf16[8,128,128]{2,1,0:T(8,128)(2,1)S(1)} %all_to_all.10), channel_id=1, source_target_pairs={{0,6},{1,25},{2,0},{3,27},{4,2},{5,29},{6,4},{7,31},{8,14},{9,1},{... | collective-permute-start | bytes 786440 | tf_op jit(solution)/shard_map/ppermute | solution.py:46
  21.2 8.7 %collective-permute-start.5 = (bf16[8,128,128]{2,1,0:T(8,128)(2,1)S(1)}, bf16[8,128,128]{2,1,0:T(8,128)(2,1)S(1)}, u32[]{:S(2)}, u32[]{:S(2)}) collective-permute-start(bf16[8,128,128]{2,1,0:T(8,128)(2,1)S(1)} %all_to_all.10), channel_id=1, source_target_pairs={{0,4},{1,17},{2,6},{3,19},{4,0},{5,21},{6,2},{7,23},{8,12},{9,25},... | collective-permute-start | bytes 786440 | tf_op jit(solution)/shard_map/ppermute | solution.py:46
  25.0 21.3 %collective-permute-start.2 = (bf16[2,8,128,128]{3,2,1,0:T(8,128)(2,1)S(1)}, bf16[2,8,128,128]{3,2,1,0:T(8,128)(2,1)S(1)}, u32[]{:S(2)}, u32[]{:S(2)}) collective-permute-start(bf16[2,8,128,128]{3,2,1,0:T(8,128)(2,1)S(1)} %pad_maximum_fusion.refs_0_), channel_id=1, source_target_pairs={{0,8},{1,3},{2,10},{3,5},{4,12},{5,7},{6,14},{7,1},{8,16},{9,11},{... | collective-permute-start | bytes 1572872 | tf_op jit(solution)/shard_map/ppermute | solution.py:46
  30.0 16.3 %collective-permute-start.6 = (bf16[2,8,128,128]{3,2,1,0:T(8,128)(2,1)S(1)}, bf16[2,8,128,128]{3,2,1,0:T(8,128)(2,1)S(1)}, u32[]{:S(2)}, u32[]{:S(2)}) collective-permute-start(bf16[2,8,128,128]{3,2,1,0:T(8,128)(2,1)S(1)} %pad_maximum_fusion.1.refs_1_), channel_id=1, source_target_pairs={{0,24},{1,7},{2,26},{3,1},{4,28},{5,3},{6,30},{7,5},{8,0},{9,15},{... | collective-permute-start | bytes 1572872 | tf_op jit(solution)/shard_map/ppermute | solution.py:46
  32.8 5.6 %collective-permute-start.11 = (bf16[2,128,128]{2,1,0:T(8,128)(2,1)S(1)}, bf16[2,128,128]{2,1,0:T(8,128)(2,1)S(1)}, u32[]{:S(2)}, u32[]{:S(2)}) collective-permute-start(bf16[2,128,128]{2,1,0:T(8,128)(2,1)S(1)} %get-tuple-element.38.blocks_ref), channel_id=1, source_target_pairs={{0,1},{1,0},{2,3},{3,2},{4,5},{5,4},{6,7},{7,6},{8,9},{9,8},{10,11... | collective-permute-start | bytes 196616 | tf_op jit(solution)/shard_map/ppermute | solution.py:50
  41.2 22.3 %collective-permute-start.10 = (bf16[2,8,128,128]{3,2,1,0:T(8,128)(2,1)S(1)}, bf16[2,8,128,128]{3,2,1,0:T(8,128)(2,1)S(1)}, u32[]{:S(2)}, u32[]{:S(2)}) collective-permute-start(bf16[2,8,128,128]{3,2,1,0:T(8,128)(2,1)S(1)} %pad_maximum_fusion.1.refs_1_), channel_id=1, source_target_pairs={{0,8},{1,3},{2,10},{3,5},{4,12},{5,7},{6,14},{7,1},{8,16},{9,11},{... | collective-permute-start | bytes 1572872 | tf_op jit(solution)/shard_map/ppermute | solution.py:46
  43.1 21.7 %collective-permute-start.8 = (bf16[2,8,128,128]{3,2,1,0:T(8,128)(2,1)S(1)}, bf16[2,8,128,128]{3,2,1,0:T(8,128)(2,1)S(1)}, u32[]{:S(2)}, u32[]{:S(2)}) collective-permute-start(bf16[2,8,128,128]{3,2,1,0:T(8,128)(2,1)S(1)} %pad_maximum_fusion.refs_0_), channel_id=1, source_target_pairs={{0,24},{1,7},{2,26},{3,1},{4,28},{5,3},{6,30},{7,5},{8,0},{9,15},{... | collective-permute-start | bytes 1572872 | tf_op jit(solution)/shard_map/ppermute | solution.py:46
  46.3 19.9 %collective-permute-start.3 = (bf16[2,8,128,128]{3,2,1,0:T(8,128)(2,1)S(1)}, bf16[2,8,128,128]{3,2,1,0:T(8,128)(2,1)S(1)}, u32[]{:S(2)}, u32[]{:S(2)}) collective-permute-start(bf16[2,8,128,128]{3,2,1,0:T(8,128)(2,1)S(1)} %collective-permute-done.2.refs_0_), channel_id=1, source_target_pairs={{0,8},{1,3},{2,10},{3,5},{4,12},{5,7},{6,14},{7,1},{8,16},{9,11},{... | collective-permute-start | bytes 1572872 | tf_op jit(solution)/shard_map/ppermute | solution.py:46
  46.3 19.9 %collective-permute-start.7 = (bf16[2,8,128,128]{3,2,1,0:T(8,128)(2,1)S(1)}, bf16[2,8,128,128]{3,2,1,0:T(8,128)(2,1)S(1)}, u32[]{:S(2)}, u32[]{:S(2)}) collective-permute-start(bf16[2,8,128,128]{3,2,1,0:T(8,128)(2,1)S(1)} %collective-permute-done.6.refs_1_), channel_id=1, source_target_pairs={{0,24},{1,7},{2,26},{3,1},{4,28},{5,3},{6,30},{7,5},{8,0},{9,15},{... | collective-permute-start | bytes 1572872 | tf_op jit(solution)/shard_map/ppermute | solution.py:46
  49.0 10.0 %collective-permute-start.13 = (bf16[2,2,128,128]{3,2,1,0:T(8,128)(2,1)S(1)}, bf16[2,2,128,128]{3,2,1,0:T(8,128)(2,1)S(1)}, u32[]{:S(2)}, u32[]{:S(2)}) collective-permute-start(bf16[2,2,128,128]{3,2,1,0:T(8,128)(2,1)S(1)} %collective-permute-done.12.fetched_ref), channel_id=1, source_target_pairs={{0,1},{1,0},{2,3},{3,2},{4,5},{5,4},{6,7},{7,6},{8,9},{9,8},{10,11... | collective-permute-start | bytes 393224 | tf_op jit(solution)/shard_map/ppermute | solution.py:50
  81.2 8.3 %collective-permute-start.18 = (bf16[8,128,128]{2,1,0:T(8,128)(2,1)S(1)}, bf16[8,128,128]{2,1,0:T(8,128)(2,1)S(1)}, u32[]{:S(2)}, u32[]{:S(2)}) collective-permute-start(bf16[8,128,128]{2,1,0:T(8,128)(2,1)S(1)} %all_to_all.11), channel_id=1, source_target_pairs={{0,6},{1,25},{2,0},{3,27},{4,2},{5,29},{6,4},{7,31},{8,14},{9,1},{... | collective-permute-start | bytes 786440 | tf_op jit(solution)/shard_map/ppermute | solution.py:46
  82.4 7.2 %collective-permute-start.19 = (bf16[8,128,128]{2,1,0:T(8,128)(2,1)S(1)}, bf16[8,128,128]{2,1,0:T(8,128)(2,1)S(1)}, u32[]{:S(2)}, u32[]{:S(2)}) collective-permute-start(bf16[8,128,128]{2,1,0:T(8,128)(2,1)S(1)} %all_to_all.11), channel_id=1, source_target_pairs={{0,4},{1,17},{2,6},{3,19},{4,0},{5,21},{6,2},{7,23},{8,12},{9,25},... | collective-permute-start | bytes 786440 | tf_op jit(solution)/shard_map/ppermute | solution.py:46
  82.4 9.0 %collective-permute-start.15 = (bf16[8,128,128]{2,1,0:T(8,128)(2,1)S(1)}, bf16[8,128,128]{2,1,0:T(8,128)(2,1)S(1)}, u32[]{:S(2)}, u32[]{:S(2)}) collective-permute-start(bf16[8,128,128]{2,1,0:T(8,128)(2,1)S(1)} %all_to_all.11), channel_id=1, source_target_pairs={{0,2},{1,9},{2,4},{3,11},{4,6},{5,13},{6,0},{7,15},{8,10},{9,17},{... | collective-permute-start | bytes 786440 | tf_op jit(solution)/shard_map/ppermute | solution.py:46
  89.6 9.8 %collective-permute-start.20 = (bf16[2,8,128,128]{3,2,1,0:T(8,128)(2,1)S(1)}, bf16[2,8,128,128]{3,2,1,0:T(8,128)(2,1)S(1)}, u32[]{:S(2)}, u32[]{:S(2)}) collective-permute-start(bf16[2,8,128,128]{3,2,1,0:T(8,128)(2,1)S(1)} %pad_maximum_fusion.3.refs_1_), channel_id=1, source_target_pairs={{0,24},{1,7},{2,26},{3,1},{4,28},{5,3},{6,30},{7,5},{8,0},{9,15},{... | collective-permute-start | bytes 1572872 | tf_op jit(solution)/shard_map/ppermute | solution.py:46
  91.4 9.3 %collective-permute-start.16 = (bf16[2,8,128,128]{3,2,1,0:T(8,128)(2,1)S(1)}, bf16[2,8,128,128]{3,2,1,0:T(8,128)(2,1)S(1)}, u32[]{:S(2)}, u32[]{:S(2)}) collective-permute-start(bf16[2,8,128,128]{3,2,1,0:T(8,128)(2,1)S(1)} %pad_maximum_fusion.2.refs_0_), channel_id=1, source_target_pairs={{0,8},{1,3},{2,10},{3,5},{4,12},{5,7},{6,14},{7,1},{8,16},{9,11},{... | collective-permute-start | bytes 1572872 | tf_op jit(solution)/shard_map/ppermute | solution.py:46
  91.5 34.3 %collective-permute-start.23 = (bf16[2,8,128,128]{3,2,1,0:T(8,128)(2,1)S(1)}, bf16[2,8,128,128]{3,2,1,0:T(8,128)(2,1)S(1)}, u32[]{:S(2)}, u32[]{:S(2)}) collective-permute-start(bf16[2,8,128,128]{3,2,1,0:T(8,128)(2,1)S(1)} %pad_maximum_fusion.3.refs_1_), channel_id=1, source_target_pairs={{0,8},{1,3},{2,10},{3,5},{4,12},{5,7},{6,14},{7,1},{8,16},{9,11},{... | collective-permute-start | bytes 1572872 | tf_op jit(solution)/shard_map/ppermute | solution.py:46
  91.6 9.3 %collective-permute-start.24 = (bf16[2,128,128]{2,1,0:T(8,128)(2,1)S(1)}, bf16[2,128,128]{2,1,0:T(8,128)(2,1)S(1)}, u32[]{:S(2)}, u32[]{:S(2)}) collective-permute-start(bf16[2,128,128]{2,1,0:T(8,128)(2,1)S(1)} %get-tuple-element.51.blocks_ref), channel_id=1, source_target_pairs={{0,1},{1,0},{2,3},{3,2},{4,5},{5,4},{6,7},{7,6},{8,9},{9,8},{10,11... | collective-permute-start | bytes 196616 | tf_op jit(solution)/shard_map/ppermute | solution.py:50
  95.7 31.4 %collective-permute-start.22 = (bf16[2,8,128,128]{3,2,1,0:T(8,128)(2,1)S(1)}, bf16[2,8,128,128]{3,2,1,0:T(8,128)(2,1)S(1)}, u32[]{:S(2)}, u32[]{:S(2)}) collective-permute-start(bf16[2,8,128,128]{3,2,1,0:T(8,128)(2,1)S(1)} %pad_maximum_fusion.2.refs_0_), channel_id=1, source_target_pairs={{0,24},{1,7},{2,26},{3,1},{4,28},{5,3},{6,30},{7,5},{8,0},{9,15},{... | collective-permute-start | bytes 1572872 | tf_op jit(solution)/shard_map/ppermute | solution.py:46
  99.4 29.1 %collective-permute-start.21 = (bf16[2,8,128,128]{3,2,1,0:T(8,128)(2,1)S(1)}, bf16[2,8,128,128]{3,2,1,0:T(8,128)(2,1)S(1)}, u32[]{:S(2)}, u32[]{:S(2)}) collective-permute-start(bf16[2,8,128,128]{3,2,1,0:T(8,128)(2,1)S(1)} %collective-permute-done.20.refs_1_), channel_id=1, source_target_pairs={{0,24},{1,7},{2,26},{3,1},{4,28},{5,3},{6,30},{7,5},{8,0},{9,15},{... | collective-permute-start | bytes 1572872 | tf_op jit(solution)/shard_map/ppermute | solution.py:46
  100.7 27.8 %collective-permute-start.17 = (bf16[2,8,128,128]{3,2,1,0:T(8,128)(2,1)S(1)}, bf16[2,8,128,128]{3,2,1,0:T(8,128)(2,1)S(1)}, u32[]{:S(2)}, u32[]{:S(2)}) collective-permute-start(bf16[2,8,128,128]{3,2,1,0:T(8,128)(2,1)S(1)} %collective-permute-done.16.refs_0_), channel_id=1, source_target_pairs={{0,8},{1,3},{2,10},{3,5},{4,12},{5,7},{6,14},{7,1},{8,16},{9,11},{... | collective-permute-start | bytes 1572872 | tf_op jit(solution)/shard_map/ppermute | solution.py:46
  100.9 11.8 %collective-permute-start.25 = (bf16[2,2,128,128]{3,2,1,0:T(8,128)(2,1)S(1)}, bf16[2,2,128,128]{3,2,1,0:T(8,128)(2,1)S(1)}, u32[]{:S(2)}, u32[]{:S(2)}) collective-permute-start(bf16[2,2,128,128]{3,2,1,0:T(8,128)(2,1)S(1)} %pad_maximum_fusion.5), channel_id=1, source_target_pairs={{0,2},{1,255},{2,4},{3,1},{4,6},{5,3},{6,8},{7,5},{8,10},{9,7},{10... | collective-permute-start | bytes 393224 | tf_op jit(solution)/shard_map/ppermute | solution.py:54
  112.7 9.4 %collective-permute-start.26 = (bf16[2,2,128,128]{3,2,1,0:T(8,128)(2,1)S(1)}, bf16[2,2,128,128]{3,2,1,0:T(8,128)(2,1)S(1)}, u32[]{:S(2)}, u32[]{:S(2)}) collective-permute-start(bf16[2,2,128,128]{3,2,1,0:T(8,128)(2,1)S(1)} %collective-permute-done.25.fetched_ref), channel_id=1, source_target_pairs={{0,1},{1,0},{2,3},{3,2},{4,5},{5,4},{6,7},{7,6},{8,9},{9,8},{10,11... | collective-permute-start | bytes 393224 | tf_op jit(solution)/shard_map/ppermute | solution.py:50
  (14 other events, 34.7 us)

commit v8 on v7

--- a/solution.py
+++ b/solution.py
@@ -156,14 +156,14 @@
     )(me, own.reshape(shape), other.reshape(shape))
 
 
-def dense_kernel(halves, me_ref, shift_ref, own_row_ref, other_row_ref, *refs):
+def dense_kernel(halves, turns, me_ref, shift_ref, own_row_ref, other_row_ref, *refs):
     chunk_refs, (tiles_ref, start_ref, out_ref) = refs[:halves], refs[halves:]
     me = me_ref[0]
     x, y, core = me // (NY * NC) % NX, me // NC % NY, me % NC
     fixed = (jnp.where(core == 0, x, y) + shift_ref[0]) % SIDE
     out_ref[...] = start_ref[...]
-    for k, turn in enumerate(TURNS):
-        chunk_ref, at = chunk_refs[k * halves // SIDE], k % (SIDE // halves)
+    for k, turn in enumerate(turns):
+        chunk_ref, at = chunk_refs[k * halves // len(turns)], k % (len(turns) // halves)
         along = (jnp.where(core == 0, y, x) + turn) % SIDE
         at_x = jnp.where(core == 0, fixed, along)
         at_y = jnp.where(core == 0, along, fixed)
@@ -176,15 +176,17 @@
             out_ref[side] += jnp.dot(left, right, preferred_element_type=jnp.float32)
 
 
-def dense_part(me, shift, rows, chunks, tiles, start):
-    return pl.pallas_call(
-        functools.partial(dense_kernel, len(chunks)),
+def dense_part(me, shift, rows, chunks, tiles, start, turns=TURNS):
+    return pl.pallas_call(
+        functools.partial(dense_kernel, len(chunks), turns),
         out_shape=jax.ShapeDtypeStruct((NC, TILE, NB * F), jnp.float32),
         in_specs=[SMEM] * 4 + [VMEM] * (len(chunks) + 2),
         out_specs=VMEM,
         compiler_params=pltpu.CompilerParams(vmem_limit_bytes=16 << 20),
         cost_estimate=pl.CostEstimate(
-            flops=8 * SIDE * NZ * TILE**3, bytes_accessed=6 * SIDE * NZ * TILE**2, transcendentals=0
+            flops=4 * NC * len(turns) * NZ * TILE**3,
+            bytes_accessed=6 * len(turns) * NZ * TILE**2,
+            transcendentals=0,
         ),
         name="dense_part",
     )(me, jnp.array([shift], jnp.int32), *rows, *chunks, tiles, start)
@@ -246,7 +248,8 @@
         side_ahead = step(column, -1, True)
         opposite = step(column, 2, True)
         fetched = from_chips(pair)
-        first, last = jnp.stack([column, side_behind]), jnp.stack([side_ahead, opposite])
+        first = jnp.stack([column, side_behind])
+        last = jnp.stack([side_ahead, opposite])
         if tiles is None:
             tiles = collect(me, dense_tiles, lax.optimization_barrier((first, other_tiles))[1])
         behind_first = step(first, 1, False)
@@ -259,8 +262,9 @@
         sparse = sparse_sums(me, sparse_row, sparse_src, sparse_count, fetch_list, near_blocks, sparse_tiles)
         total = dense_part(me, SIDE - 1, rows, (behind_first, behind_last), tiles, total)
         total = dense_part(me, 1, rows, (ahead_first, ahead_last), tiles, total)
-        far, total, sparse = lax.optimization_barrier((far, total, sparse))
-        total = dense_part(me, 2, rows, far, tiles, total)
+        far_first, total, sparse = lax.optimization_barrier((far[0], total, sparse))
+        total = dense_part(me, 2, rows, (far_first,), tiles, total, TURNS[: SIDE // 2])
+        total = dense_part(me, 2, rows, (far[1],), tiles, total, TURNS[SIDE // 2 :])
         returned = swap_cores(total[1])
         return *finish(me, hub_block, total, returned, sparse, weight, dtype, wide), tiles
 

time: 133 us -> 134 us (level)
  the two profiles are of different devices: /device:TPU:35 before, /device:TPU:1 now
where the time goes in v8:
time: 134 us
  starting transfers between devices  42.4 us (32%)
  blocking collectives  35.1 us (26%)
  waiting for transfers between devices  30 us (22%)
  Pallas kernels  23.2 us (17%)
  local copies, waits for them, and re-layouts  2.3 us (2%)
    all_to_all x2, blocking collectives, propagate(): lax.all_to_all(copies, 'blk', 0, 0, axis_index_groups=groups_along_z(), t...  35.1 us
    ppermute x18, starting transfers between devices, step(): return lax.ppermute(array, 'blk', pairs)  23.1 us
    ppermute x8, starting transfers between devices, swap_cores(): return lax.ppermute(array, 'blk', [(i, i ^ 1) for i in range(SHARDS)])  19.1 us
    ppermute x18, waiting for transfers between devices, step(): return lax.ppermute(array, 'blk', pairs)  13.5 us
    pallas_call x10, Pallas kernels, dense_part(): pl.pallas_call(functools.partial(dense_kernel, len(chunks), turns), out_s...  12.1 us
    ppermute x2, waiting for transfers between devices, from_chips(): lax.ppermute(array, 'blk', [(i, (i + (-NC if i % NC else NC)) % SHARDS) f...  11.9 us
    pallas_call x2, Pallas kernels, sparse_sums(): pl.pallas_call(sparse_kernel, out_shape=jax.ShapeDtypeStruct((TILE, NB *...  4.72 us
    ppermute x8, waiting for transfers between devices, swap_cores(): return lax.ppermute(array, 'blk', [(i, i ^ 1) for i in range(SHARDS)])  4.61 us
  transfers between devices with their start and end apart: 28, of which 12 were waited for; matrix products, arithmetic and copies ran while one was open for 0% of the time, Pallas kernels for 14%

profile of v8, /device:TPU:1, one launch (start us, length us, event | category | flops | bytes accessed | tf_op | source)
XLA Modules:
  0.0 134.3 jit_solution(665877259338283339)
XLA Ops:
  0.0 3.2 %collective-permute-start.6 = (bf16[256,128,128]{2,1,0:T(8,128)(2,1)}, bf16[256,128,128]{2,1,0:T(8,128)(2,1)}, u32[]{:S(2)}, u32[]{:S(2)}) collective-permute-start(bf16[256,128,128]{2,1,0:T(8,128)(2,1)} %param.24), channel_id=1, source_target_pairs={{0,1},{1,0},{2,3},{3,2},{4,5},{5,4},{6,7},{7,6},{8,9},{9,8},{10,11... | collective-permute-start | bytes 25165832 | tf_op jit(solution)/shard_map/ppermute | solution.py:50
  5.4 18.6 %all_to_all.10 = bf16[8,128,128]{2,1,0:T(8,128)(2,1)S(1)} all-to-all(bf16[8,128,128]{2,1,0:T(8,128)(2,1)S(1)} %get-tuple-element.31), channel_id=1, replica_groups={{0,32,64,96,128,160,192,224},{1,33,65,97,129,161,193,225},{2,34,66,98,1..., dimensions={0} | all-to-all | bytes 524288 | tf_op jit(solution)/shard_map/all_to_all | solution.py:243
  25.2 1.5 %collective-permute-start.1 = (bf16[8,128,128]{2,1,0:T(8,128)(2,1)S(1)}, bf16[8,128,128]{2,1,0:T(8,128)(2,1)S(1)}, u32[]{:S(2)}, u32[]{:S(2)}) collective-permute-start(bf16[8,128,128]{2,1,0:T(8,128)(2,1)S(1)} %all_to_all.10), channel_id=1, source_target_pairs={{0,6},{1,25},{2,0},{3,27},{4,2},{5,29},{6,4},{7,31},{8,14},{9,1},{... | collective-permute-start | bytes 786440 | tf_op jit(solution)/shard_map/ppermute | solution.py:46
  26.7 1.5 %collective-permute-start.2 = (bf16[8,128,128]{2,1,0:T(8,128)(2,1)S(1)}, bf16[8,128,128]{2,1,0:T(8,128)(2,1)S(1)}, u32[]{:S(2)}, u32[]{:S(2)}) collective-permute-start(bf16[8,128,128]{2,1,0:T(8,128)(2,1)S(1)} %all_to_all.10), channel_id=1, source_target_pairs={{0,4},{1,17},{2,6},{3,19},{4,0},{5,21},{6,2},{7,23},{8,12},{9,25},... | collective-permute-start | bytes 786440 | tf_op jit(solution)/shard_map/ppermute | solution.py:46
  28.2 2.5 %collective-permute-done.5 = bf16[8,128,128]{2,1,0:T(8,128)(2,1)S(1)} collective-permute-done((bf16[8,128,128]{2,1,0:T(8,128)(2,1)S(1)}, bf16[8,128,128]{2,1,0:T(8,128)(2,1)S(1)}, u32[]{:S(2)}, u32[]{:S(2)}) %collective-permute-start.5) | collective-permute-done | bytes 262176 | tf_op jit(solution)/shard_map/ppermute | solution.py:46
  31.9 2.7 %collective-permute-done.2 = bf16[8,128,128]{2,1,0:T(8,128)(2,1)S(1)} collective-permute-done((bf16[8,128,128]{2,1,0:T(8,128)(2,1)S(1)}, bf16[8,128,128]{2,1,0:T(8,128)(2,1)S(1)}, u32[]{:S(2)}, u32[]{:S(2)}) %collective-permute-start.2) | collective-permute-done | bytes 262176 | tf_op jit(solution)/shard_map/ppermute | solution.py:46
  34.6 2.8 %collective-permute-start.3 = (bf16[2,8,128,128]{3,2,1,0:T(8,128)(2,1)S(1)}, bf16[2,8,128,128]{3,2,1,0:T(8,128)(2,1)S(1)}, u32[]{:S(2)}, u32[]{:S(2)}) collective-permute-start(bf16[2,8,128,128]{3,2,1,0:T(8,128)(2,1)S(1)} %pad_maximum_fusion.refs_1_), channel_id=1, source_target_pairs={{0,24},{1,7},{2,26},{3,1},{4,28},{5,3},{6,30},{7,5},{8,0},{9,15},{... | collective-permute-start | bytes 1572872 | tf_op jit(solution)/shard_map/ppermute | solution.py:46
  37.4 2.5 %collective-permute-start.11 = (bf16[2,128,128]{2,1,0:T(8,128)(2,1)S(1)}, bf16[2,128,128]{2,1,0:T(8,128)(2,1)S(1)}, u32[]{:S(2)}, u32[]{:S(2)}) collective-permute-start(bf16[2,128,128]{2,1,0:T(8,128)(2,1)S(1)} %get-tuple-element.36.blocks_ref), channel_id=1, source_target_pairs={{0,1},{1,0},{2,3},{3,2},{4,5},{5,4},{6,7},{7,6},{8,9},{9,8},{10,11... | collective-permute-start | bytes 196616 | tf_op jit(solution)/shard_map/ppermute | solution.py:50
  45.0 3.9 %collective-permute-start.9 = (bf16[2,8,128,128]{3,2,1,0:T(8,128)(2,1)S(1)}, bf16[2,8,128,128]{3,2,1,0:T(8,128)(2,1)S(1)}, u32[]{:S(2)}, u32[]{:S(2)}) collective-permute-start(bf16[2,8,128,128]{3,2,1,0:T(8,128)(2,1)S(1)} %pad_maximum_fusion.1.refs_0_), channel_id=1, source_target_pairs={{0,24},{1,7},{2,26},{3,1},{4,28},{5,3},{6,30},{7,5},{8,0},{9,15},{... | collective-permute-start | bytes 1572872 | tf_op jit(solution)/shard_map/ppermute | solution.py:46
  48.9 2.7 %collective-permute-start.4 = (bf16[2,8,128,128]{3,2,1,0:T(8,128)(2,1)S(1)}, bf16[2,8,128,128]{3,2,1,0:T(8,128)(2,1)S(1)}, u32[]{:S(2)}, u32[]{:S(2)}) collective-permute-start(bf16[2,8,128,128]{3,2,1,0:T(8,128)(2,1)S(1)} %collective-permute-done.3.refs_1_), channel_id=1, source_target_pairs={{0,24},{1,7},{2,26},{3,1},{4,28},{5,3},{6,30},{7,5},{8,0},{9,15},{... | collective-permute-start | bytes 1572872 | tf_op jit(solution)/shard_map/ppermute | solution.py:46
  51.6 3.4 %collective-permute-start.13 = (bf16[2,2,128,128]{3,2,1,0:T(8,128)(2,1)S(1)}, bf16[2,2,128,128]{3,2,1,0:T(8,128)(2,1)S(1)}, u32[]{:S(2)}, u32[]{:S(2)}) collective-permute-start(bf16[2,2,128,128]{3,2,1,0:T(8,128)(2,1)S(1)} %collective-permute-done.12.fetched_ref), channel_id=1, source_target_pairs={{0,1},{1,0},{2,3},{3,2},{4,5},{5,4},{6,7},{7,6},{8,9},{9,8},{10,11... | collective-permute-start | bytes 393224 | tf_op jit(solution)/shard_map/ppermute | solution.py:50
  55.7 3.5 %collect.1.refs_2_.refs_1_ = bf16[2,8,4,4,128,128]{5,4,3,2,1,0:T(8,128)(2,1)S(1)} custom-call(s32[1]{0:T(128)} %bitcast.me_ref, bf16[8,4,4,2,128,128]{5,4,3,2,1,0:T(8,128)(2,1)} %bitcast.24, bf16[8,4,4,2,128,128]{5,4,3,2,1,0:T(8,128)(2,1)} %bitcast.6.other_ref), custom_call_target="tpu_custom_call" | custom-call | bytes 8388608 | tf_op jit(solution)/shard_map/collect/pallas_call | solution.py:147
  61.3 2.4 %sparse_sums.2.sparse_ref = f32[128,256]{1,0:T(8,128)S(1)} custom-call(s32[1]{0:T(128)} %bitcast.me_ref, s32[112]{0:T(128)S(1)} %copy-done.7, s32[112]{0:T(128)S(1)} %copy-done.8, s32[1]{0:T(128)S(6)} %copy.22.count_ref, s32[1,4]{1,0:T(1,128)S(1)} %copy-done.9, bf16[2,128,128]{2,1,0:T(8,128)(2,1)S(1)} %get-tuple-element.36.blocks_ref, ...), custom_call_target="tpu_custom_call" | custom-call | flops 469762048 | bytes 3670016 | tf_op jit(solution)/shard_map/sparse_sums/pallas_call | solution.py:120
  70.8 16.5 %all_to_all.11 = bf16[8,128,128]{2,1,0:T(8,128)(2,1)S(1)} all-to-all(bf16[8,128,128]{2,1,0:T(8,128)(2,1)S(1)} %get-tuple-element.44), channel_id=1, replica_groups={{0,32,64,96,128,160,192,224},{1,33,65,97,129,161,193,225},{2,34,66,98,1..., dimensions={0} | all-to-all | bytes 524288 | tf_op jit(solution)/shard_map/all_to_all | solution.py:243
  87.6 2.4 %collective-permute-start.15 = (bf16[8,128,128]{2,1,0:T(8,128)(2,1)S(1)}, bf16[8,128,128]{2,1,0:T(8,128)(2,1)S(1)}, u32[]{:S(2)}, u32[]{:S(2)}) collective-permute-start(bf16[8,128,128]{2,1,0:T(8,128)(2,1)S(1)} %all_to_all.11), channel_id=1, source_target_pairs={{0,6},{1,25},{2,0},{3,27},{4,2},{5,29},{6,4},{7,31},{8,14},{9,1},{... | collective-permute-start | bytes 786440 | tf_op jit(solution)/shard_map/ppermute | solution.py:46
  90.0 4.0 %collective-permute-done.19 = bf16[8,128,128]{2,1,0:T(8,128)(2,1)S(1)} collective-permute-done((bf16[8,128,128]{2,1,0:T(8,128)(2,1)S(1)}, bf16[8,128,128]{2,1,0:T(8,128)(2,1)S(1)}, u32[]{:S(2)}, u32[]{:S(2)}) %collective-permute-start.19) | collective-permute-done | bytes 262176 | tf_op jit(solution)/shard_map/ppermute | solution.py:46
  94.1 1.9 %collective-permute-done.15 = bf16[8,128,128]{2,1,0:T(8,128)(2,1)S(1)} collective-permute-done((bf16[8,128,128]{2,1,0:T(8,128)(2,1)S(1)}, bf16[8,128,128]{2,1,0:T(8,128)(2,1)S(1)}, u32[]{:S(2)}, u32[]{:S(2)}) %collective-permute-start.15) | collective-permute-done | bytes 262176 | tf_op jit(solution)/shard_map/ppermute | solution.py:46
  97.1 1.5 %collective-permute-start.23 = (bf16[2,8,128,128]{3,2,1,0:T(8,128)(2,1)S(1)}, bf16[2,8,128,128]{3,2,1,0:T(8,128)(2,1)S(1)}, u32[]{:S(2)}, u32[]{:S(2)}) collective-permute-start(bf16[2,8,128,128]{3,2,1,0:T(8,128)(2,1)S(1)} %pad_maximum_fusion.2.refs_1_), channel_id=1, source_target_pairs={{0,8},{1,3},{2,10},{3,5},{4,12},{5,7},{6,14},{7,1},{8,16},{9,11},{... | collective-permute-start | bytes 1572872 | tf_op jit(solution)/shard_map/ppermute | solution.py:46
  98.6 5.4 %collective-permute-start.24 = (bf16[2,128,128]{2,1,0:T(8,128)(2,1)S(1)}, bf16[2,128,128]{2,1,0:T(8,128)(2,1)S(1)}, u32[]{:S(2)}, u32[]{:S(2)}) collective-permute-start(bf16[2,128,128]{2,1,0:T(8,128)(2,1)S(1)} %get-tuple-element.48.blocks_ref), channel_id=1, source_target_pairs={{0,1},{1,0},{2,3},{3,2},{4,5},{5,4},{6,7},{7,6},{8,9},{9,8},{10,11... | collective-permute-start | bytes 196616 | tf_op jit(solution)/shard_map/ppermute | solution.py:50
  105.4 2.6 %collective-permute-start.18 = (bf16[2,8,128,128]{3,2,1,0:T(8,128)(2,1)S(1)}, bf16[2,8,128,128]{3,2,1,0:T(8,128)(2,1)S(1)}, u32[]{:S(2)}, u32[]{:S(2)}) collective-permute-start(bf16[2,8,128,128]{3,2,1,0:T(8,128)(2,1)S(1)} %collective-permute-done.17.refs_1_), channel_id=1, source_target_pairs={{0,24},{1,7},{2,26},{3,1},{4,28},{5,3},{6,30},{7,5},{8,0},{9,15},{... | collective-permute-start | bytes 1572872 | tf_op jit(solution)/shard_map/ppermute | solution.py:46
  108.1 11.2 %collective-permute-done.25.fetched_ref = bf16[2,2,128,128]{3,2,1,0:T(8,128)(2,1)S(1)} collective-permute-done((bf16[2,2,128,128]{3,2,1,0:T(8,128)(2,1)S(1)}, bf16[2,2,128,128]{3,2,1,0:T(8,128)(2,1)S(1)}, u32[]{:S(2)}, u32[]{:S(2)}) %collective-permute-start.25) | collective-permute-done | bytes 131104 | tf_op jit(solution)/shard_map/ppermute | solution.py:54
  119.3 3.6 %collective-permute-start.26 = (bf16[2,2,128,128]{3,2,1,0:T(8,128)(2,1)S(1)}, bf16[2,2,128,128]{3,2,1,0:T(8,128)(2,1)S(1)}, u32[]{:S(2)}, u32[]{:S(2)}) collective-permute-start(bf16[2,2,128,128]{3,2,1,0:T(8,128)(2,1)S(1)} %collective-permute-done.25.fetched_ref), channel_id=1, source_target_pairs={{0,1},{1,0},{2,3},{3,2},{4,5},{5,4},{6,7},{7,6},{8,9},{9,8},{10,11... | collective-permute-start | bytes 393224 | tf_op jit(solution)/shard_map/ppermute | solution.py:50
  124.2 2.3 %sparse_sums.3.sparse_ref = f32[128,256]{1,0:T(8,128)S(1)} custom-call(s32[1]{0:T(128)} %bitcast.me_ref, s32[112]{0:T(128)S(1)} %copy-done.7, s32[112]{0:T(128)S(1)} %copy-done.8, s32[1]{0:T(128)S(6)} %copy.22.count_ref, s32[1,4]{1,0:T(1,128)S(1)} %copy-done.9, bf16[2,128,128]{2,1,0:T(8,128)(2,1)S(1)} %get-tuple-element.48.blocks_ref, ...), custom_call_target="tpu_custom_call" | custom-call | flops 469762048 | bytes 3670016 | tf_op jit(solution)/shard_map/sparse_sums/pallas_call | solution.py:120
  132.8 1.5 %finish.3 = f32[2,128,128]{2,1,0:T(8,128)} custom-call(s32[1]{0:T(128)} %bitcast.me_ref, s32[256]{0:T(256)S(1)} %copy-done.6, f32[2,128,256]{2,1,0:T(8,128)S(1)} %dense_part.19.dense_ref, f32[128,256]{1,0:T(8,128)S(1)} %collective-permute-done.27.other_ref, f32[128,256]{1,0:T(8,128)S(1)} %sparse_sums.3.sparse_ref, f32[128,128]{1,0:T(8,128)S(1)} %copy-done.3), custom_call_target="tpu_custom_call" | custom-call | tf_op jit(solution)/shard_map/finish/pallas_call | solution.py:214
  (79 shorter events, 29.3 us)
Async XLA Ops:
  0.0 51.6 %collective-permute-start.6 = (bf16[256,128,128]{2,1,0:T(8,128)(2,1)}, bf16[256,128,128]{2,1,0:T(8,128)(2,1)}, u32[]{:S(2)}, u32[]{:S(2)}) collective-permute-start(bf16[256,128,128]{2,1,0:T(8,128)(2,1)} %param.24), channel_id=1, source_target_pairs={{0,1},{1,0},{2,3},{3,2},{4,5},{5,4},{6,7},{7,6},{8,9},{9,8},{10,11... | collective-permute-start | bytes 25165832 | tf_op jit(solution)/shard_map/ppermute | solution.py:50
  24.0 6.7 %collective-permute-start.5 = (bf16[8,128,128]{2,1,0:T(8,128)(2,1)S(1)}, bf16[8,128,128]{2,1,0:T(8,128)(2,1)S(1)}, u32[]{:S(2)}, u32[]{:S(2)}) collective-permute-start(bf16[8,128,128]{2,1,0:T(8,128)(2,1)S(1)} %all_to_all.10), channel_id=1, source_target_pairs={{0,2},{1,9},{2,4},{3,11},{4,6},{5,13},{6,0},{7,15},{8,10},{9,17},{... | collective-permute-start | bytes 786440 | tf_op jit(solution)/shard_map/ppermute | solution.py:46
  25.2 6.7 %collective-permute-start.1 = (bf16[8,128,128]{2,1,0:T(8,128)(2,1)S(1)}, bf16[8,128,128]{2,1,0:T(8,128)(2,1)S(1)}, u32[]{:S(2)}, u32[]{:S(2)}) collective-permute-start(bf16[8,128,128]{2,1,0:T(8,128)(2,1)S(1)} %all_to_all.10), channel_id=1, source_target_pairs={{0,6},{1,25},{2,0},{3,27},{4,2},{5,29},{6,4},{7,31},{8,14},{9,1},{... | collective-permute-start | bytes 786440 | tf_op jit(solution)/shard_map/ppermute | solution.py:46
  26.7 7.8 %collective-permute-start.2 = (bf16[8,128,128]{2,1,0:T(8,128)(2,1)S(1)}, bf16[8,128,128]{2,1,0:T(8,128)(2,1)S(1)}, u32[]{:S(2)}, u32[]{:S(2)}) collective-permute-start(bf16[8,128,128]{2,1,0:T(8,128)(2,1)S(1)} %all_to_all.10), channel_id=1, source_target_pairs={{0,4},{1,17},{2,6},{3,19},{4,0},{5,21},{6,2},{7,23},{8,12},{9,25},... | collective-permute-start | bytes 786440 | tf_op jit(solution)/shard_map/ppermute | solution.py:46
  30.8 18.1 %collective-permute-start.7 = (bf16[2,8,128,128]{3,2,1,0:T(8,128)(2,1)S(1)}, bf16[2,8,128,128]{3,2,1,0:T(8,128)(2,1)S(1)}, u32[]{:S(2)}, u32[]{:S(2)}) collective-permute-start(bf16[2,8,128,128]{3,2,1,0:T(8,128)(2,1)S(1)} %pad_maximum_fusion.1.refs_0_), channel_id=1, source_target_pairs={{0,8},{1,3},{2,10},{3,5},{4,12},{5,7},{6,14},{7,1},{8,16},{9,11},{... | collective-permute-start | bytes 1572872 | tf_op jit(solution)/shard_map/ppermute | solution.py:46
  34.6 14.3 %collective-permute-start.3 = (bf16[2,8,128,128]{3,2,1,0:T(8,128)(2,1)S(1)}, bf16[2,8,128,128]{3,2,1,0:T(8,128)(2,1)S(1)}, u32[]{:S(2)}, u32[]{:S(2)}) collective-permute-start(bf16[2,8,128,128]{3,2,1,0:T(8,128)(2,1)S(1)} %pad_maximum_fusion.refs_1_), channel_id=1, source_target_pairs={{0,24},{1,7},{2,26},{3,1},{4,28},{5,3},{6,30},{7,5},{8,0},{9,15},{... | collective-permute-start | bytes 1572872 | tf_op jit(solution)/shard_map/ppermute | solution.py:46
  40.8 4.2 %collective-permute-start.12 = (bf16[2,2,128,128]{3,2,1,0:T(8,128)(2,1)S(1)}, bf16[2,2,128,128]{3,2,1,0:T(8,128)(2,1)S(1)}, u32[]{:S(2)}, u32[]{:S(2)}) collective-permute-start(bf16[2,2,128,128]{3,2,1,0:T(8,128)(2,1)S(1)} %pad_maximum_fusion.4), channel_id=1, source_target_pairs={{0,2},{1,255},{2,4},{3,1},{4,6},{5,3},{6,8},{7,5},{8,10},{9,7},{10... | collective-permute-start | bytes 393224 | tf_op jit(solution)/shard_map/ppermute | solution.py:54
  42.8 20.9 %collective-permute-start.10 = (bf16[2,8,128,128]{3,2,1,0:T(8,128)(2,1)S(1)}, bf16[2,8,128,128]{3,2,1,0:T(8,128)(2,1)S(1)}, u32[]{:S(2)}, u32[]{:S(2)}) collective-permute-start(bf16[2,8,128,128]{3,2,1,0:T(8,128)(2,1)S(1)} %pad_maximum_fusion.refs_1_), channel_id=1, source_target_pairs={{0,8},{1,3},{2,10},{3,5},{4,12},{5,7},{6,14},{7,1},{8,16},{9,11},{... | collective-permute-start | bytes 1572872 | tf_op jit(solution)/shard_map/ppermute | solution.py:46
  45.0 20.0 %collective-permute-start.9 = (bf16[2,8,128,128]{3,2,1,0:T(8,128)(2,1)S(1)}, bf16[2,8,128,128]{3,2,1,0:T(8,128)(2,1)S(1)}, u32[]{:S(2)}, u32[]{:S(2)}) collective-permute-start(bf16[2,8,128,128]{3,2,1,0:T(8,128)(2,1)S(1)} %pad_maximum_fusion.1.refs_0_), channel_id=1, source_target_pairs={{0,24},{1,7},{2,26},{3,1},{4,28},{5,3},{6,30},{7,5},{8,0},{9,15},{... | collective-permute-start | bytes 1572872 | tf_op jit(solution)/shard_map/ppermute | solution.py:46
  48.9 17.5 %collective-permute-start.8 = (bf16[2,8,128,128]{3,2,1,0:T(8,128)(2,1)S(1)}, bf16[2,8,128,128]{3,2,1,0:T(8,128)(2,1)S(1)}, u32[]{:S(2)}, u32[]{:S(2)}) collective-permute-start(bf16[2,8,128,128]{3,2,1,0:T(8,128)(2,1)S(1)} %collective-permute-done.7.refs_0_), channel_id=1, source_target_pairs={{0,8},{1,3},{2,10},{3,5},{4,12},{5,7},{6,14},{7,1},{8,16},{9,11},{... | collective-permute-start | bytes 1572872 | tf_op jit(solution)/shard_map/ppermute | solution.py:46
  48.9 18.5 %collective-permute-start.4 = (bf16[2,8,128,128]{3,2,1,0:T(8,128)(2,1)S(1)}, bf16[2,8,128,128]{3,2,1,0:T(8,128)(2,1)S(1)}, u32[]{:S(2)}, u32[]{:S(2)}) collective-permute-start(bf16[2,8,128,128]{3,2,1,0:T(8,128)(2,1)S(1)} %collective-permute-done.3.refs_1_), channel_id=1, source_target_pairs={{0,24},{1,7},{2,26},{3,1},{4,28},{5,3},{6,30},{7,5},{8,0},{9,15},{... | collective-permute-start | bytes 1572872 | tf_op jit(solution)/shard_map/ppermute | solution.py:46
  51.6 9.0 %collective-permute-start.13 = (bf16[2,2,128,128]{3,2,1,0:T(8,128)(2,1)S(1)}, bf16[2,2,128,128]{3,2,1,0:T(8,128)(2,1)S(1)}, u32[]{:S(2)}, u32[]{:S(2)}) collective-permute-start(bf16[2,2,128,128]{3,2,1,0:T(8,128)(2,1)S(1)} %collective-permute-done.12.fetched_ref), channel_id=1, source_target_pairs={{0,1},{1,0},{2,3},{3,2},{4,5},{5,4},{6,7},{7,6},{8,9},{9,8},{10,11... | collective-permute-start | bytes 393224 | tf_op jit(solution)/shard_map/ppermute | solution.py:50
  87.3 6.7 %collective-permute-start.19 = (bf16[8,128,128]{2,1,0:T(8,128)(2,1)S(1)}, bf16[8,128,128]{2,1,0:T(8,128)(2,1)S(1)}, u32[]{:S(2)}, u32[]{:S(2)}) collective-permute-start(bf16[8,128,128]{2,1,0:T(8,128)(2,1)S(1)} %all_to_all.11), channel_id=1, source_target_pairs={{0,2},{1,9},{2,4},{3,11},{4,6},{5,13},{6,0},{7,15},{8,10},{9,17},{... | collective-permute-start | bytes 786440 | tf_op jit(solution)/shard_map/ppermute | solution.py:46
  87.6 8.5 %collective-permute-start.15 = (bf16[8,128,128]{2,1,0:T(8,128)(2,1)S(1)}, bf16[8,128,128]{2,1,0:T(8,128)(2,1)S(1)}, u32[]{:S(2)}, u32[]{:S(2)}) collective-permute-start(bf16[8,128,128]{2,1,0:T(8,128)(2,1)S(1)} %all_to_all.11), channel_id=1, source_target_pairs={{0,6},{1,25},{2,0},{3,27},{4,2},{5,29},{6,4},{7,31},{8,14},{9,1},{... | collective-permute-start | bytes 786440 | tf_op jit(solution)/shard_map/ppermute | solution.py:46
  90.0 7.0 %collective-permute-start.16 = (bf16[8,128,128]{2,1,0:T(8,128)(2,1)S(1)}, bf16[8,128,128]{2,1,0:T(8,128)(2,1)S(1)}, u32[]{:S(2)}, u32[]{:S(2)}) collective-permute-start(bf16[8,128,128]{2,1,0:T(8,128)(2,1)S(1)} %all_to_all.11), channel_id=1, source_target_pairs={{0,4},{1,17},{2,6},{3,19},{4,0},{5,21},{6,2},{7,23},{8,12},{9,25},... | collective-permute-start | bytes 786440 | tf_op jit(solution)/shard_map/ppermute | solution.py:46
  94.1 11.3 %collective-permute-start.20 = (bf16[2,8,128,128]{3,2,1,0:T(8,128)(2,1)S(1)}, bf16[2,8,128,128]{3,2,1,0:T(8,128)(2,1)S(1)}, u32[]{:S(2)}, u32[]{:S(2)}) collective-permute-start(bf16[2,8,128,128]{3,2,1,0:T(8,128)(2,1)S(1)} %pad_maximum_fusion.3.refs_0_), channel_id=1, source_target_pairs={{0,8},{1,3},{2,10},{3,5},{4,12},{5,7},{6,14},{7,1},{8,16},{9,11},{... | collective-permute-start | bytes 1572872 | tf_op jit(solution)/shard_map/ppermute | solution.py:46
  97.0 8.4 %collective-permute-start.17 = (bf16[2,8,128,128]{3,2,1,0:T(8,128)(2,1)S(1)}, bf16[2,8,128,128]{3,2,1,0:T(8,128)(2,1)S(1)}, u32[]{:S(2)}, u32[]{:S(2)}) collective-permute-start(bf16[2,8,128,128]{3,2,1,0:T(8,128)(2,1)S(1)} %pad_maximum_fusion.2.refs_1_), channel_id=1, source_target_pairs={{0,24},{1,7},{2,26},{3,1},{4,28},{5,3},{6,30},{7,5},{8,0},{9,15},{... | collective-permute-start | bytes 1572872 | tf_op jit(solution)/shard_map/ppermute | solution.py:46
  97.1 29.4 %collective-permute-start.23 = (bf16[2,8,128,128]{3,2,1,0:T(8,128)(2,1)S(1)}, bf16[2,8,128,128]{3,2,1,0:T(8,128)(2,1)S(1)}, u32[]{:S(2)}, u32[]{:S(2)}) collective-permute-start(bf16[2,8,128,128]{3,2,1,0:T(8,128)(2,1)S(1)} %pad_maximum_fusion.2.refs_1_), channel_id=1, source_target_pairs={{0,8},{1,3},{2,10},{3,5},{4,12},{5,7},{6,14},{7,1},{8,16},{9,11},{... | collective-permute-start | bytes 1572872 | tf_op jit(solution)/shard_map/ppermute | solution.py:46
  98.6 9.4 %collective-permute-start.24 = (bf16[2,128,128]{2,1,0:T(8,128)(2,1)S(1)}, bf16[2,128,128]{2,1,0:T(8,128)(2,1)S(1)}, u32[]{:S(2)}, u32[]{:S(2)}) collective-permute-start(bf16[2,128,128]{2,1,0:T(8,128)(2,1)S(1)} %get-tuple-element.48.blocks_ref), channel_id=1, source_target_pairs={{0,1},{1,0},{2,3},{3,2},{4,5},{5,4},{6,7},{7,6},{8,9},{9,8},{10,11... | collective-permute-start | bytes 196616 | tf_op jit(solution)/shard_map/ppermute | solution.py:50
  103.9 23.9 %collective-permute-start.22 = (bf16[2,8,128,128]{3,2,1,0:T(8,128)(2,1)S(1)}, bf16[2,8,128,128]{3,2,1,0:T(8,128)(2,1)S(1)}, u32[]{:S(2)}, u32[]{:S(2)}) collective-permute-start(bf16[2,8,128,128]{3,2,1,0:T(8,128)(2,1)S(1)} %pad_maximum_fusion.3.refs_0_), channel_id=1, source_target_pairs={{0,24},{1,7},{2,26},{3,1},{4,28},{5,3},{6,30},{7,5},{8,0},{9,15},{... | collective-permute-start | bytes 1572872 | tf_op jit(solution)/shard_map/ppermute | solution.py:46
  105.3 23.9 %collective-permute-start.21 = (bf16[2,8,128,128]{3,2,1,0:T(8,128)(2,1)S(1)}, bf16[2,8,128,128]{3,2,1,0:T(8,128)(2,1)S(1)}, u32[]{:S(2)}, u32[]{:S(2)}) collective-permute-start(bf16[2,8,128,128]{3,2,1,0:T(8,128)(2,1)S(1)} %collective-permute-done.20.refs_0_), channel_id=1, source_target_pairs={{0,8},{1,3},{2,10},{3,5},{4,12},{5,7},{6,14},{7,1},{8,16},{9,11},{... | collective-permute-start | bytes 1572872 | tf_op jit(solution)/shard_map/ppermute | solution.py:46
  105.4 24.9 %collective-permute-start.18 = (bf16[2,8,128,128]{3,2,1,0:T(8,128)(2,1)S(1)}, bf16[2,8,128,128]{3,2,1,0:T(8,128)(2,1)S(1)}, u32[]{:S(2)}, u32[]{:S(2)}) collective-permute-start(bf16[2,8,128,128]{3,2,1,0:T(8,128)(2,1)S(1)} %collective-permute-done.17.refs_1_), channel_id=1, source_target_pairs={{0,24},{1,7},{2,26},{3,1},{4,28},{5,3},{6,30},{7,5},{8,0},{9,15},{... | collective-permute-start | bytes 1572872 | tf_op jit(solution)/shard_map/ppermute | solution.py:46
  108.0 11.2 %collective-permute-start.25 = (bf16[2,2,128,128]{3,2,1,0:T(8,128)(2,1)S(1)}, bf16[2,2,128,128]{3,2,1,0:T(8,128)(2,1)S(1)}, u32[]{:S(2)}, u32[]{:S(2)}) collective-permute-start(bf16[2,2,128,128]{3,2,1,0:T(8,128)(2,1)S(1)} %pad_maximum_fusion.5), channel_id=1, source_target_pairs={{0,2},{1,255},{2,4},{3,1},{4,6},{5,3},{6,8},{7,5},{8,10},{9,7},{10... | collective-permute-start | bytes 393224 | tf_op jit(solution)/shard_map/ppermute | solution.py:54
  119.3 4.9 %collective-permute-start.26 = (bf16[2,2,128,128]{3,2,1,0:T(8,128)(2,1)S(1)}, bf16[2,2,128,128]{3,2,1,0:T(8,128)(2,1)S(1)}, u32[]{:S(2)}, u32[]{:S(2)}) collective-permute-start(bf16[2,2,128,128]{3,2,1,0:T(8,128)(2,1)S(1)} %collective-permute-done.25.fetched_ref), channel_id=1, source_target_pairs={{0,1},{1,0},{2,3},{3,2},{4,5},{5,4},{6,7},{7,6},{8,9},{9,8},{10,11... | collective-permute-start | bytes 393224 | tf_op jit(solution)/shard_map/ppermute | solution.py:50
  (14 other events, 32.2 us)

commit v9 on v8

--- a/solution.py
+++ b/solution.py
@@ -59,32 +59,32 @@
     return jnp.concatenate([jnp.where(row == 0, block, zeros), jnp.where(row == 0, zeros, block)], axis=1)
 
 
-def enter_kernel(me_ref, hub_ref, features_ref, blocks_ref, copies_ref):
+def enter_kernel(hub_ref, features_ref, blocks_ref, copies_ref):
     blocks = [features_ref[b * TILE : (b + 1) * TILE].astype(jnp.bfloat16) for b in range(NB)]
-    hub = jnp.where(hub_ref[me_ref[0]] == 0, blocks[0], blocks[1])
+    hub = jnp.where(hub_ref[lax.axis_index("blk")] == 0, blocks[0], blocks[1])
     for b in range(NB):
         blocks_ref[b] = blocks[b]
     for z in range(NZ):
         copies_ref[z] = hub
 
 
-def enter(me, hub_block, features):
+def enter(hub_block, features):
     return pl.pallas_call(
         enter_kernel,
         out_shape=(
             jax.ShapeDtypeStruct((NB, TILE, F), jnp.bfloat16),
             jax.ShapeDtypeStruct((NZ, TILE, F), jnp.bfloat16),
         ),
-        in_specs=[SMEM, SMEM, VMEM],
+        in_specs=[SMEM, VMEM],
         out_specs=(VMEM, VMEM),
         compiler_params=pltpu.CompilerParams(vmem_limit_bytes=8 << 20),
         name="enter",
-    )(me, hub_block, features)
-
-
-def sparse_kernel(me_ref, row_ref, src_ref, count_ref, fetch_ref, blocks_ref, beside_ref, fetched_ref, shared_ref, tiles_ref, out_ref, placed_ref):
+    )(hub_block, features)
+
+
+def sparse_kernel(row_ref, src_ref, count_ref, fetch_ref, blocks_ref, beside_ref, fetched_ref, shared_ref, tiles_ref, out_ref, placed_ref):
     zeros = jnp.zeros((TILE, F), jnp.bfloat16)
-    even = me_ref[0] % NC == 0
+    even = lax.axis_index("blk") % NC == 0
     wanted = [fetch_ref[0, entry] for entry in range(2 * HOPS)]
     blocks = [
         blocks_ref[0],
@@ -116,21 +116,21 @@
     lax.fori_loop(0, (live + group - 1) // group, add, 0)
 
 
-def sparse_sums(me, row, src, count, wanted, near_blocks, tiles):
+def sparse_sums(row, src, count, wanted, near_blocks, tiles):
     return pl.pallas_call(
         sparse_kernel,
         out_shape=jax.ShapeDtypeStruct((TILE, NB * F), jnp.float32),
-        in_specs=[SMEM] * 5 + [VMEM] * 5,
+        in_specs=[SMEM] * 4 + [VMEM] * 5,
         out_specs=VMEM,
         scratch_shapes=[pltpu.VMEM((2 * SOURCES + 1, TILE, NB * F), jnp.bfloat16)],
         cost_estimate=pl.CostEstimate(flops=2 * KS * TILE**3, bytes_accessed=2 * KS * TILE**2, transcendentals=0),
         compiler_params=pltpu.CompilerParams(vmem_limit_bytes=16 << 20),
         name="sparse_sums",
-    )(me, row, src, count, wanted, *near_blocks, tiles)
-
-
-def collect_kernel(me_ref, own_ref, other_ref, out_ref, sems):
-    core = me_ref[0] % NC
+    )(row, src, count, wanted, *near_blocks, tiles)
+
+
+def collect_kernel(own_ref, other_ref, out_ref, sems):
+    core = lax.axis_index("blk") % NC
     copies = [
         pltpu.make_async_copy(tiles_ref.at[z, :, :, core], out_ref.at[side, z], sems.at[side, z])
         for side, tiles_ref in enumerate((own_ref, other_ref))
@@ -142,25 +142,25 @@
         copy.wait()
 
 
-def collect(me, own, other):
+def collect(own, other):
     shape = (NZ, NX, NY, NC, TILE, TILE)
     return pl.pallas_call(
         collect_kernel,
         out_shape=jax.ShapeDtypeStruct((NC, NZ, NX, NY, TILE, TILE), jnp.bfloat16),
-        in_specs=[SMEM, HBM, HBM],
+        in_specs=[HBM, HBM],
         out_specs=VMEM,
         scratch_shapes=[pltpu.SemaphoreType.DMA((NC, NZ))],
         compiler_params=pltpu.CompilerParams(vmem_limit_bytes=44 << 20),
         cost_estimate=pl.CostEstimate(flops=0, bytes_accessed=2 * SHARDS * TILE**2, transcendentals=0),
         name="collect",
-    )(me, own.reshape(shape), other.reshape(shape))
-
-
-def dense_kernel(halves, turns, me_ref, shift_ref, own_row_ref, other_row_ref, *refs):
+    )(own.reshape(shape), other.reshape(shape))
+
+
+def dense_kernel(halves, turns, shift, own_row_ref, other_row_ref, *refs):
     chunk_refs, (tiles_ref, start_ref, out_ref) = refs[:halves], refs[halves:]
-    me = me_ref[0]
+    me = lax.axis_index("blk")
     x, y, core = me // (NY * NC) % NX, me // NC % NY, me % NC
-    fixed = (jnp.where(core == 0, x, y) + shift_ref[0]) % SIDE
+    fixed = (jnp.where(core == 0, x, y) + shift) % SIDE
     out_ref[...] = start_ref[...]
     for k, turn in enumerate(turns):
         chunk_ref, at = chunk_refs[k * halves // len(turns)], k % (len(turns) // halves)
@@ -176,11 +176,11 @@
             out_ref[side] += jnp.dot(left, right, preferred_element_type=jnp.float32)
 
 
-def dense_part(me, shift, rows, chunks, tiles, start, turns=TURNS):
-    return pl.pallas_call(
-        functools.partial(dense_kernel, len(chunks), turns),
+def dense_part(shift, rows, chunks, tiles, start, turns=TURNS):
+    return pl.pallas_call(
+        functools.partial(dense_kernel, len(chunks), turns, shift),
         out_shape=jax.ShapeDtypeStruct((NC, TILE, NB * F), jnp.float32),
-        in_specs=[SMEM] * 4 + [VMEM] * (len(chunks) + 2),
+        in_specs=[SMEM] * 2 + [VMEM] * (len(chunks) + 2),
         out_specs=VMEM,
         compiler_params=pltpu.CompilerParams(vmem_limit_bytes=16 << 20),
         cost_estimate=pl.CostEstimate(
@@ -189,10 +189,10 @@
             transcendentals=0,
         ),
         name="dense_part",
-    )(me, jnp.array([shift], jnp.int32), *rows, *chunks, tiles, start)
-
-
-def finish_kernel(wide, me_ref, hub_ref, dense_ref, other_ref, sparse_ref, weight_ref, out_ref, *copies):
+    )(*rows, *chunks, tiles, start)
+
+
+def finish_kernel(wide, hub_ref, dense_ref, other_ref, sparse_ref, weight_ref, out_ref, *copies):
     blocks = []
     for block in range(NB):
         columns = slice(block * F, (block + 1) * F)
@@ -203,22 +203,22 @@
         blocks.append(jnp.maximum(projected, 0.0).astype(out_ref.dtype))
         out_ref[block] = blocks[block]
     if wide:
-        hub = jnp.where(hub_ref[me_ref[0]] == 0, blocks[0], blocks[1])
+        hub = jnp.where(hub_ref[lax.axis_index("blk")] == 0, blocks[0], blocks[1])
         for z in range(NZ):
             copies[0][z] = hub
 
 
-def finish(me, hub_block, dense, other, sparse, weight, dtype, wide):
+def finish(hub_block, dense, other, sparse, weight, dtype, wide):
     shape = jax.ShapeDtypeStruct((NB, TILE, F), dtype)
     copies = [jax.ShapeDtypeStruct((NZ, TILE, F), dtype)] if wide else []
     return pl.pallas_call(
         functools.partial(finish_kernel, wide),
         out_shape=(shape, *copies),
-        in_specs=[SMEM, SMEM] + [VMEM] * 4,
+        in_specs=[SMEM] + [VMEM] * 4,
         out_specs=(VMEM,) * (1 + len(copies)),
         compiler_params=pltpu.CompilerParams(vmem_limit_bytes=8 << 20),
         name="finish",
-    )(me, hub_block, dense, other, sparse, weight)
+    )(hub_block, dense, other, sparse, weight)
 
 
 def shards(
@@ -234,7 +234,6 @@
     sparse_count,
     fetch_list,
 ):
-    me = lax.axis_index("blk").astype(jnp.int32).reshape(1)
     rows = [dense_row, swap_cores(dense_row)]
     other_tiles = swap_cores(dense_tiles)
     zeros = jnp.zeros((NC, TILE, NB * F), jnp.float32)
@@ -251,24 +250,24 @@
         first = jnp.stack([column, side_behind])
         last = jnp.stack([side_ahead, opposite])
         if tiles is None:
-            tiles = collect(me, dense_tiles, lax.optimization_barrier((first, other_tiles))[1])
+            tiles = collect(dense_tiles, lax.optimization_barrier((first, other_tiles))[1])
         behind_first = step(first, 1, False)
         ahead_last = step(last, -1, False)
         behind_last, ahead_first = step(last, 1, False), step(first, -1, False)
         shared = swap_cores(fetched)
         far = (step(behind_first, 1, False), step(ahead_last, -1, False))
-        total = dense_part(me, 0, rows, (first, last), tiles, zeros)
+        total = dense_part(0, rows, (first, last), tiles, zeros)
         near_blocks, total = lax.optimization_barrier(((blocks, beside, fetched, shared), total))
-        sparse = sparse_sums(me, sparse_row, sparse_src, sparse_count, fetch_list, near_blocks, sparse_tiles)
-        total = dense_part(me, SIDE - 1, rows, (behind_first, behind_last), tiles, total)
-        total = dense_part(me, 1, rows, (ahead_first, ahead_last), tiles, total)
+        sparse = sparse_sums(sparse_row, sparse_src, sparse_count, fetch_list, near_blocks, sparse_tiles)
+        total = dense_part(SIDE - 1, rows, (behind_first, behind_last), tiles, total)
+        total = dense_part(1, rows, (ahead_first, ahead_last), tiles, total)
         far_first, total, sparse = lax.optimization_barrier((far[0], total, sparse))
-        total = dense_part(me, 2, rows, (far_first,), tiles, total, TURNS[: SIDE // 2])
-        total = dense_part(me, 2, rows, (far[1],), tiles, total, TURNS[SIDE // 2 :])
+        total = dense_part(2, rows, (far_first,), tiles, total, TURNS[: SIDE // 2])
+        total = dense_part(2, rows, (far[1],), tiles, total, TURNS[SIDE // 2 :])
         returned = swap_cores(total[1])
-        return *finish(me, hub_block, total, returned, sparse, weight, dtype, wide), tiles
-
-    blocks, copies = enter(me, hub_block, features)
+        return *finish(hub_block, total, returned, sparse, weight, dtype, wide), tiles
+
+    blocks, copies = enter(hub_block, features)
     hidden, copies, tiles = propagate(blocks, copies, weight_one, jnp.bfloat16, True)
     embedded, _ = propagate(hidden, copies, weight_two, jnp.float32, False, tiles)
     return embedded.reshape(NB * TILE, F)

time: 134 us -> 135 us (level)
  starting transfers between devices: 42.4 us -> 45.9 us
  waiting for transfers between devices: 30 us -> 28.1 us
  blocking collectives: 35.1 us -> 33.7 us
    ppermute x18, starting transfers between devices: 23.1 us -> 25.1 us  [step(): return lax.ppermute(array, 'blk', pairs)]
    ppermute x18, waiting for transfers between devices: 13.5 us -> 11.8 us  [step(): return lax.ppermute(array, 'blk', pairs)]
    ppermute x8, starting transfers between devices: 19.1 us -> 20.7 us  [swap_cores(): return lax.ppermute(array, 'blk', [(i, i ^ 1) for i in range(SHARDS)])]
    all_to_all x2, blocking collectives: 35.1 us -> 33.7 us  [propagate(): lax.all_to_all(copies, 'blk', 0, 0, axis_index_groups=groups_along_z(), t...]
  transfers between devices with their start and end apart: 28 -> 28, of which waited for: 12 -> 13; matrix products, arithmetic and copies ran while one was open for 0% -> 0% of each run, Pallas kernels for 14% -> 14%
where the time goes in v9:
time: 135 us
  starting transfers between devices  45.9 us (34%)
  blocking collectives  33.7 us (25%)
  waiting for transfers between devices  28.1 us (21%)
  Pallas kernels  23.4 us (17%)
  local copies, waits for them, and re-layouts  2.3 us (2%)
    all_to_all x2, blocking collectives, propagate(): lax.all_to_all(copies, 'blk', 0, 0, axis_index_groups=groups_along_z(), t...  33.7 us
    ppermute x18, starting transfers between devices, step(): return lax.ppermute(array, 'blk', pairs)  25.1 us
    ppermute x8, starting transfers between devices, swap_cores(): return lax.ppermute(array, 'blk', [(i, i ^ 1) for i in range(SHARDS)])  20.7 us
    pallas_call x10, Pallas kernels, dense_part(): pl.pallas_call(functools.partial(dense_kernel, len(chunks), turns, shift)...  12.1 us
    ppermute x2, waiting for transfers between devices, from_chips(): lax.ppermute(array, 'blk', [(i, (i + (-NC if i % NC else NC)) % SHARDS) f...  12.1 us
    ppermute x18, waiting for transfers between devices, step(): return lax.ppermute(array, 'blk', pairs)  11.8 us
    pallas_call x2, Pallas kernels, sparse_sums(): pl.pallas_call(sparse_kernel, out_shape=jax.ShapeDtypeStruct((TILE, NB *...  4.77 us
    ppermute x8, waiting for transfers between devices, swap_cores(): return lax.ppermute(array, 'blk', [(i, i ^ 1) for i in range(SHARDS)])  4.26 us
  transfers between devices with their start and end apart: 28, of which 13 were waited for; matrix products, arithmetic and copies ran while one was open for 0% of the time, Pallas kernels for 14%

profile of v9, /device:TPU:1, one launch (start us, length us, event | category | flops | bytes accessed | tf_op | source)
XLA Modules:
  0.0 134.7 jit_solution(12555006763970878072)
XLA Ops:
  0.0 3.2 %collective-permute-start.6 = (bf16[256,128,128]{2,1,0:T(8,128)(2,1)}, bf16[256,128,128]{2,1,0:T(8,128)(2,1)S(1)}, u32[]{:S(2)}, u32[]{:S(2)}) collective-permute-start(bf16[256,128,128]{2,1,0:T(8,128)(2,1)} %param.14), channel_id=1, source_target_pairs={{0,1},{1,0},{2,3},{3,2},{4,5},{5,4},{6,7},{7,6},{8,9},{9,8},{10,11... | collective-permute-start | bytes 25165832 | tf_op jit(solution)/shard_map/ppermute | solution.py:50
  5.4 18.6 %all_to_all.10 = bf16[8,128,128]{2,1,0:T(8,128)(2,1)S(1)} all-to-all(bf16[8,128,128]{2,1,0:T(8,128)(2,1)S(1)} %get-tuple-element.31), channel_id=1, replica_groups={{0,32,64,96,128,160,192,224},{1,33,65,97,129,161,193,225},{2,34,66,98,1..., dimensions={0} | all-to-all | bytes 524288 | tf_op jit(solution)/shard_map/all_to_all | solution.py:242
  25.2 1.5 %collective-permute-start.1 = (bf16[8,128,128]{2,1,0:T(8,128)(2,1)S(1)}, bf16[8,128,128]{2,1,0:T(8,128)(2,1)S(1)}, u32[]{:S(2)}, u32[]{:S(2)}) collective-permute-start(bf16[8,128,128]{2,1,0:T(8,128)(2,1)S(1)} %all_to_all.10), channel_id=1, source_target_pairs={{0,6},{1,25},{2,0},{3,27},{4,2},{5,29},{6,4},{7,31},{8,14},{9,1},{... | collective-permute-start | bytes 786440 | tf_op jit(solution)/shard_map/ppermute | solution.py:46
  26.7 1.5 %collective-permute-start.2 = (bf16[8,128,128]{2,1,0:T(8,128)(2,1)S(1)}, bf16[8,128,128]{2,1,0:T(8,128)(2,1)S(1)}, u32[]{:S(2)}, u32[]{:S(2)}) collective-permute-start(bf16[8,128,128]{2,1,0:T(8,128)(2,1)S(1)} %all_to_all.10), channel_id=1, source_target_pairs={{0,4},{1,17},{2,6},{3,19},{4,0},{5,21},{6,2},{7,23},{8,12},{9,25},... | collective-permute-start | bytes 786440 | tf_op jit(solution)/shard_map/ppermute | solution.py:46
  28.2 2.5 %collective-permute-done.5 = bf16[8,128,128]{2,1,0:T(8,128)(2,1)S(1)} collective-permute-done((bf16[8,128,128]{2,1,0:T(8,128)(2,1)S(1)}, bf16[8,128,128]{2,1,0:T(8,128)(2,1)S(1)}, u32[]{:S(2)}, u32[]{:S(2)}) %collective-permute-start.5) | collective-permute-done | bytes 262176 | tf_op jit(solution)/shard_map/ppermute | solution.py:46
  31.9 2.7 %collective-permute-done.2 = bf16[8,128,128]{2,1,0:T(8,128)(2,1)S(1)} collective-permute-done((bf16[8,128,128]{2,1,0:T(8,128)(2,1)S(1)}, bf16[8,128,128]{2,1,0:T(8,128)(2,1)S(1)}, u32[]{:S(2)}, u32[]{:S(2)}) %collective-permute-start.2) | collective-permute-done | bytes 262176 | tf_op jit(solution)/shard_map/ppermute | solution.py:46
  34.6 2.8 %collective-permute-start.3 = (bf16[2,8,128,128]{3,2,1,0:T(8,128)(2,1)S(1)}, bf16[2,8,128,128]{3,2,1,0:T(8,128)(2,1)S(1)}, u32[]{:S(2)}, u32[]{:S(2)}) collective-permute-start(bf16[2,8,128,128]{3,2,1,0:T(8,128)(2,1)S(1)} %pad_maximum_fusion.refs_1_), channel_id=1, source_target_pairs={{0,24},{1,7},{2,26},{3,1},{4,28},{5,3},{6,30},{7,5},{8,0},{9,15},{... | collective-permute-start | bytes 1572872 | tf_op jit(solution)/shard_map/ppermute | solution.py:46
  37.4 2.5 %collective-permute-start.11 = (bf16[2,128,128]{2,1,0:T(8,128)(2,1)S(1)}, bf16[2,128,128]{2,1,0:T(8,128)(2,1)S(1)}, u32[]{:S(2)}, u32[]{:S(2)}) collective-permute-start(bf16[2,128,128]{2,1,0:T(8,128)(2,1)S(1)} %get-tuple-element.36.blocks_ref), channel_id=1, source_target_pairs={{0,1},{1,0},{2,3},{3,2},{4,5},{5,4},{6,7},{7,6},{8,9},{9,8},{10,11... | collective-permute-start | bytes 196616 | tf_op jit(solution)/shard_map/ppermute | solution.py:50
  42.8 1.5 %collective-permute-start.10 = (bf16[2,8,128,128]{3,2,1,0:T(8,128)(2,1)S(1)}, bf16[2,8,128,128]{3,2,1,0:T(8,128)(2,1)S(1)}, u32[]{:S(2)}, u32[]{:S(2)}) collective-permute-start(bf16[2,8,128,128]{3,2,1,0:T(8,128)(2,1)S(1)} %pad_maximum_fusion.refs_1_), channel_id=1, source_target_pairs={{0,8},{1,3},{2,10},{3,5},{4,12},{5,7},{6,14},{7,1},{8,16},{9,11},{... | collective-permute-start | bytes 1572872 | tf_op jit(solution)/shard_map/ppermute | solution.py:46
  45.0 3.9 %collective-permute-start.9 = (bf16[2,8,128,128]{3,2,1,0:T(8,128)(2,1)S(1)}, bf16[2,8,128,128]{3,2,1,0:T(8,128)(2,1)S(1)}, u32[]{:S(2)}, u32[]{:S(2)}) collective-permute-start(bf16[2,8,128,128]{3,2,1,0:T(8,128)(2,1)S(1)} %pad_maximum_fusion.1.refs_0_), channel_id=1, source_target_pairs={{0,24},{1,7},{2,26},{3,1},{4,28},{5,3},{6,30},{7,5},{8,0},{9,15},{... | collective-permute-start | bytes 1572872 | tf_op jit(solution)/shard_map/ppermute | solution.py:46
  48.9 2.7 %collective-permute-start.4 = (bf16[2,8,128,128]{3,2,1,0:T(8,128)(2,1)S(1)}, bf16[2,8,128,128]{3,2,1,0:T(8,128)(2,1)S(1)}, u32[]{:S(2)}, u32[]{:S(2)}) collective-permute-start(bf16[2,8,128,128]{3,2,1,0:T(8,128)(2,1)S(1)} %collective-permute-done.3.refs_1_), channel_id=1, source_target_pairs={{0,24},{1,7},{2,26},{3,1},{4,28},{5,3},{6,30},{7,5},{8,0},{9,15},{... | collective-permute-start | bytes 1572872 | tf_op jit(solution)/shard_map/ppermute | solution.py:46
  51.6 3.4 %collective-permute-start.13 = (bf16[2,2,128,128]{3,2,1,0:T(8,128)(2,1)S(1)}, bf16[2,2,128,128]{3,2,1,0:T(8,128)(2,1)S(1)}, u32[]{:S(2)}, u32[]{:S(2)}) collective-permute-start(bf16[2,2,128,128]{3,2,1,0:T(8,128)(2,1)S(1)} %collective-permute-done.12.fetched_ref), channel_id=1, source_target_pairs={{0,1},{1,0},{2,3},{3,2},{4,5},{5,4},{6,7},{7,6},{8,9},{9,8},{10,11... | collective-permute-start | bytes 393224 | tf_op jit(solution)/shard_map/ppermute | solution.py:50
  55.7 3.5 %collect.1.refs_2_.refs_1_ = bf16[2,8,4,4,128,128]{5,4,3,2,1,0:T(8,128)(2,1)S(1)} custom-call(bf16[8,4,4,2,128,128]{5,4,3,2,1,0:T(8,128)(2,1)} %bitcast.23, bf16[8,4,4,2,128,128]{5,4,3,2,1,0:T(8,128)(2,1)} %bitcast.24), custom_call_target="tpu_custom_call" | custom-call | bytes 8388608 | tf_op jit(solution)/shard_map/collect/pallas_call | solution.py:147
  61.3 2.5 %sparse_sums.2.sparse_ref = f32[128,256]{1,0:T(8,128)S(1)} custom-call(s32[112]{0:T(128)S(1)} %copy-done.7, s32[112]{0:T(128)S(1)} %copy-done.8, s32[1]{0:T(128)S(6)} %copy.12.count_ref, s32[1,4]{1,0:T(1,128)S(1)} %copy-done.9, bf16[2,128,128]{2,1,0:T(8,128)(2,1)S(1)} %get-tuple-element.36.blocks_ref, ...), custom_call_target="tpu_custom_call" | custom-call | flops 469762048 | bytes 3670016 | tf_op jit(solution)/shard_map/sparse_sums/pallas_call | solution.py:120
  71.7 15.1 %all_to_all.11 = bf16[8,128,128]{2,1,0:T(8,128)(2,1)S(1)} all-to-all(bf16[8,128,128]{2,1,0:T(8,128)(2,1)S(1)} %get-tuple-element.44), channel_id=1, replica_groups={{0,32,64,96,128,160,192,224},{1,33,65,97,129,161,193,225},{2,34,66,98,1..., dimensions={0} | all-to-all | bytes 524288 | tf_op jit(solution)/shard_map/all_to_all | solution.py:242
  87.0 2.5 %collective-permute-start.16 = (bf16[8,128,128]{2,1,0:T(8,128)(2,1)S(1)}, bf16[8,128,128]{2,1,0:T(8,128)(2,1)S(1)}, u32[]{:S(2)}, u32[]{:S(2)}) collective-permute-start(bf16[8,128,128]{2,1,0:T(8,128)(2,1)S(1)} %all_to_all.11), channel_id=1, source_target_pairs={{0,4},{1,17},{2,6},{3,19},{4,0},{5,21},{6,2},{7,23},{8,12},{9,25},... | collective-permute-start | bytes 786440 | tf_op jit(solution)/shard_map/ppermute | solution.py:46
  89.5 3.9 %collective-permute-done.19 = bf16[8,128,128]{2,1,0:T(8,128)(2,1)S(1)} collective-permute-done((bf16[8,128,128]{2,1,0:T(8,128)(2,1)S(1)}, bf16[8,128,128]{2,1,0:T(8,128)(2,1)S(1)}, u32[]{:S(2)}, u32[]{:S(2)}) %collective-permute-start.19) | collective-permute-done | bytes 262176 | tf_op jit(solution)/shard_map/ppermute | solution.py:46
  94.9 1.5 %collective-permute-done.16 = bf16[8,128,128]{2,1,0:T(8,128)(2,1)S(1)} collective-permute-done((bf16[8,128,128]{2,1,0:T(8,128)(2,1)S(1)}, bf16[8,128,128]{2,1,0:T(8,128)(2,1)S(1)}, u32[]{:S(2)}, u32[]{:S(2)}) %collective-permute-start.16) | collective-permute-done | bytes 262176 | tf_op jit(solution)/shard_map/ppermute | solution.py:46
  98.5 5.3 %collective-permute-start.24 = (bf16[2,128,128]{2,1,0:T(8,128)(2,1)S(1)}, bf16[2,128,128]{2,1,0:T(8,128)(2,1)S(1)}, u32[]{:S(2)}, u32[]{:S(2)}) collective-permute-start(bf16[2,128,128]{2,1,0:T(8,128)(2,1)S(1)} %get-tuple-element.48.blocks_ref), channel_id=1, source_target_pairs={{0,1},{1,0},{2,3},{3,2},{4,5},{5,4},{6,7},{7,6},{8,9},{9,8},{10,11... | collective-permute-start | bytes 196616 | tf_op jit(solution)/shard_map/ppermute | solution.py:50
  105.4 2.4 %collective-permute-start.18 = (bf16[2,8,128,128]{3,2,1,0:T(8,128)(2,1)S(1)}, bf16[2,8,128,128]{3,2,1,0:T(8,128)(2,1)S(1)}, u32[]{:S(2)}, u32[]{:S(2)}) collective-permute-start(bf16[2,8,128,128]{3,2,1,0:T(8,128)(2,1)S(1)} %collective-permute-done.17.refs_1_), channel_id=1, source_target_pairs={{0,24},{1,7},{2,26},{3,1},{4,28},{5,3},{6,30},{7,5},{8,0},{9,15},{... | collective-permute-start | bytes 1572872 | tf_op jit(solution)/shard_map/ppermute | solution.py:46
  107.9 11.3 %collective-permute-done.25.fetched_ref = bf16[2,2,128,128]{3,2,1,0:T(8,128)(2,1)S(1)} collective-permute-done((bf16[2,2,128,128]{3,2,1,0:T(8,128)(2,1)S(1)}, bf16[2,2,128,128]{3,2,1,0:T(8,128)(2,1)S(1)}, u32[]{:S(2)}, u32[]{:S(2)}) %collective-permute-start.25) | collective-permute-done | bytes 131104 | tf_op jit(solution)/shard_map/ppermute | solution.py:54
  119.2 4.0 %collective-permute-start.26 = (bf16[2,2,128,128]{3,2,1,0:T(8,128)(2,1)S(1)}, bf16[2,2,128,128]{3,2,1,0:T(8,128)(2,1)S(1)}, u32[]{:S(2)}, u32[]{:S(2)}) collective-permute-start(bf16[2,2,128,128]{3,2,1,0:T(8,128)(2,1)S(1)} %collective-permute-done.25.fetched_ref), channel_id=1, source_target_pairs={{0,1},{1,0},{2,3},{3,2},{4,5},{5,4},{6,7},{7,6},{8,9},{9,8},{10,11... | collective-permute-start | bytes 393224 | tf_op jit(solution)/shard_map/ppermute | solution.py:50
  124.6 2.3 %sparse_sums.3.sparse_ref = f32[128,256]{1,0:T(8,128)S(1)} custom-call(s32[112]{0:T(128)S(1)} %copy-done.7, s32[112]{0:T(128)S(1)} %copy-done.8, s32[1]{0:T(128)S(6)} %copy.12.count_ref, s32[1,4]{1,0:T(1,128)S(1)} %copy-done.9, bf16[2,128,128]{2,1,0:T(8,128)(2,1)S(1)} %get-tuple-element.48.blocks_ref, ...), custom_call_target="tpu_custom_call" | custom-call | flops 469762048 | bytes 3670016 | tf_op jit(solution)/shard_map/sparse_sums/pallas_call | solution.py:120
  133.2 1.5 %finish.3 = f32[2,128,128]{2,1,0:T(8,128)} custom-call(s32[256]{0:T(256)S(1)} %copy-done.6, f32[2,128,256]{2,1,0:T(8,128)S(1)} %dense_part.19.dense_ref, f32[128,256]{1,0:T(8,128)S(1)} %collective-permute-done.27.other_ref, f32[128,256]{1,0:T(8,128)S(1)} %sparse_sums.3.sparse_ref, f32[128,128]{1,0:T(8,128)S(1)} %copy-done.4), custom_call_target="tpu_custom_call" | custom-call | tf_op jit(solution)/shard_map/finish/pallas_call | solution.py:214
  (81 shorter events, 31.0 us)
Async XLA Ops:
  0.0 51.6 %collective-permute-start.6 = (bf16[256,128,128]{2,1,0:T(8,128)(2,1)}, bf16[256,128,128]{2,1,0:T(8,128)(2,1)S(1)}, u32[]{:S(2)}, u32[]{:S(2)}) collective-permute-start(bf16[256,128,128]{2,1,0:T(8,128)(2,1)} %param.14), channel_id=1, source_target_pairs={{0,1},{1,0},{2,3},{3,2},{4,5},{5,4},{6,7},{7,6},{8,9},{9,8},{10,11... | collective-permute-start | bytes 25165832 | tf_op jit(solution)/shard_map/ppermute | solution.py:50
  24.0 6.7 %collective-permute-start.5 = (bf16[8,128,128]{2,1,0:T(8,128)(2,1)S(1)}, bf16[8,128,128]{2,1,0:T(8,128)(2,1)S(1)}, u32[]{:S(2)}, u32[]{:S(2)}) collective-permute-start(bf16[8,128,128]{2,1,0:T(8,128)(2,1)S(1)} %all_to_all.10), channel_id=1, source_target_pairs={{0,2},{1,9},{2,4},{3,11},{4,6},{5,13},{6,0},{7,15},{8,10},{9,17},{... | collective-permute-start | bytes 786440 | tf_op jit(solution)/shard_map/ppermute | solution.py:46
  25.2 6.7 %collective-permute-start.1 = (bf16[8,128,128]{2,1,0:T(8,128)(2,1)S(1)}, bf16[8,128,128]{2,1,0:T(8,128)(2,1)S(1)}, u32[]{:S(2)}, u32[]{:S(2)}) collective-permute-start(bf16[8,128,128]{2,1,0:T(8,128)(2,1)S(1)} %all_to_all.10), channel_id=1, source_target_pairs={{0,6},{1,25},{2,0},{3,27},{4,2},{5,29},{6,4},{7,31},{8,14},{9,1},{... | collective-permute-start | bytes 786440 | tf_op jit(solution)/shard_map/ppermute | solution.py:46
  26.7 7.8 %collective-permute-start.2 = (bf16[8,128,128]{2,1,0:T(8,128)(2,1)S(1)}, bf16[8,128,128]{2,1,0:T(8,128)(2,1)S(1)}, u32[]{:S(2)}, u32[]{:S(2)}) collective-permute-start(bf16[8,128,128]{2,1,0:T(8,128)(2,1)S(1)} %all_to_all.10), channel_id=1, source_target_pairs={{0,4},{1,17},{2,6},{3,19},{4,0},{5,21},{6,2},{7,23},{8,12},{9,25},... | collective-permute-start | bytes 786440 | tf_op jit(solution)/shard_map/ppermute | solution.py:46
  30.8 18.1 %collective-permute-start.7 = (bf16[2,8,128,128]{3,2,1,0:T(8,128)(2,1)S(1)}, bf16[2,8,128,128]{3,2,1,0:T(8,128)(2,1)S(1)}, u32[]{:S(2)}, u32[]{:S(2)}) collective-permute-start(bf16[2,8,128,128]{3,2,1,0:T(8,128)(2,1)S(1)} %pad_maximum_fusion.1.refs_0_), channel_id=1, source_target_pairs={{0,8},{1,3},{2,10},{3,5},{4,12},{5,7},{6,14},{7,1},{8,16},{9,11},{... | collective-permute-start | bytes 1572872 | tf_op jit(solution)/shard_map/ppermute | solution.py:46
  34.6 14.3 %collective-permute-start.3 = (bf16[2,8,128,128]{3,2,1,0:T(8,128)(2,1)S(1)}, bf16[2,8,128,128]{3,2,1,0:T(8,128)(2,1)S(1)}, u32[]{:S(2)}, u32[]{:S(2)}) collective-permute-start(bf16[2,8,128,128]{3,2,1,0:T(8,128)(2,1)S(1)} %pad_maximum_fusion.refs_1_), channel_id=1, source_target_pairs={{0,24},{1,7},{2,26},{3,1},{4,28},{5,3},{6,30},{7,5},{8,0},{9,15},{... | collective-permute-start | bytes 1572872 | tf_op jit(solution)/shard_map/ppermute | solution.py:46
  40.8 4.2 %collective-permute-start.12 = (bf16[2,2,128,128]{3,2,1,0:T(8,128)(2,1)S(1)}, bf16[2,2,128,128]{3,2,1,0:T(8,128)(2,1)S(1)}, u32[]{:S(2)}, u32[]{:S(2)}) collective-permute-start(bf16[2,2,128,128]{3,2,1,0:T(8,128)(2,1)S(1)} %pad_maximum_fusion.4), channel_id=1, source_target_pairs={{0,2},{1,255},{2,4},{3,1},{4,6},{5,3},{6,8},{7,5},{8,10},{9,7},{10... | collective-permute-start | bytes 393224 | tf_op jit(solution)/shard_map/ppermute | solution.py:54
  42.8 20.9 %collective-permute-start.10 = (bf16[2,8,128,128]{3,2,1,0:T(8,128)(2,1)S(1)}, bf16[2,8,128,128]{3,2,1,0:T(8,128)(2,1)S(1)}, u32[]{:S(2)}, u32[]{:S(2)}) collective-permute-start(bf16[2,8,128,128]{3,2,1,0:T(8,128)(2,1)S(1)} %pad_maximum_fusion.refs_1_), channel_id=1, source_target_pairs={{0,8},{1,3},{2,10},{3,5},{4,12},{5,7},{6,14},{7,1},{8,16},{9,11},{... | collective-permute-start | bytes 1572872 | tf_op jit(solution)/shard_map/ppermute | solution.py:46
  45.0 20.1 %collective-permute-start.9 = (bf16[2,8,128,128]{3,2,1,0:T(8,128)(2,1)S(1)}, bf16[2,8,128,128]{3,2,1,0:T(8,128)(2,1)S(1)}, u32[]{:S(2)}, u32[]{:S(2)}) collective-permute-start(bf16[2,8,128,128]{3,2,1,0:T(8,128)(2,1)S(1)} %pad_maximum_fusion.1.refs_0_), channel_id=1, source_target_pairs={{0,24},{1,7},{2,26},{3,1},{4,28},{5,3},{6,30},{7,5},{8,0},{9,15},{... | collective-permute-start | bytes 1572872 | tf_op jit(solution)/shard_map/ppermute | solution.py:46
  48.9 17.5 %collective-permute-start.8 = (bf16[2,8,128,128]{3,2,1,0:T(8,128)(2,1)S(1)}, bf16[2,8,128,128]{3,2,1,0:T(8,128)(2,1)S(1)}, u32[]{:S(2)}, u32[]{:S(2)}) collective-permute-start(bf16[2,8,128,128]{3,2,1,0:T(8,128)(2,1)S(1)} %collective-permute-done.7.refs_0_), channel_id=1, source_target_pairs={{0,8},{1,3},{2,10},{3,5},{4,12},{5,7},{6,14},{7,1},{8,16},{9,11},{... | collective-permute-start | bytes 1572872 | tf_op jit(solution)/shard_map/ppermute | solution.py:46
  48.9 18.6 %collective-permute-start.4 = (bf16[2,8,128,128]{3,2,1,0:T(8,128)(2,1)S(1)}, bf16[2,8,128,128]{3,2,1,0:T(8,128)(2,1)S(1)}, u32[]{:S(2)}, u32[]{:S(2)}) collective-permute-start(bf16[2,8,128,128]{3,2,1,0:T(8,128)(2,1)S(1)} %collective-permute-done.3.refs_1_), channel_id=1, source_target_pairs={{0,24},{1,7},{2,26},{3,1},{4,28},{5,3},{6,30},{7,5},{8,0},{9,15},{... | collective-permute-start | bytes 1572872 | tf_op jit(solution)/shard_map/ppermute | solution.py:46
  51.6 9.0 %collective-permute-start.13 = (bf16[2,2,128,128]{3,2,1,0:T(8,128)(2,1)S(1)}, bf16[2,2,128,128]{3,2,1,0:T(8,128)(2,1)S(1)}, u32[]{:S(2)}, u32[]{:S(2)}) collective-permute-start(bf16[2,2,128,128]{3,2,1,0:T(8,128)(2,1)S(1)} %collective-permute-done.12.fetched_ref), channel_id=1, source_target_pairs={{0,1},{1,0},{2,3},{3,2},{4,5},{5,4},{6,7},{7,6},{8,9},{9,8},{10,11... | collective-permute-start | bytes 393224 | tf_op jit(solution)/shard_map/ppermute | solution.py:50
  86.8 6.7 %collective-permute-start.19 = (bf16[8,128,128]{2,1,0:T(8,128)(2,1)S(1)}, bf16[8,128,128]{2,1,0:T(8,128)(2,1)S(1)}, u32[]{:S(2)}, u32[]{:S(2)}) collective-permute-start(bf16[8,128,128]{2,1,0:T(8,128)(2,1)S(1)} %all_to_all.11), channel_id=1, source_target_pairs={{0,2},{1,9},{2,4},{3,11},{4,6},{5,13},{6,0},{7,15},{8,10},{9,17},{... | collective-permute-start | bytes 786440 | tf_op jit(solution)/shard_map/ppermute | solution.py:46
  87.0 9.4 %collective-permute-start.16 = (bf16[8,128,128]{2,1,0:T(8,128)(2,1)S(1)}, bf16[8,128,128]{2,1,0:T(8,128)(2,1)S(1)}, u32[]{:S(2)}, u32[]{:S(2)}) collective-permute-start(bf16[8,128,128]{2,1,0:T(8,128)(2,1)S(1)} %all_to_all.11), channel_id=1, source_target_pairs={{0,4},{1,17},{2,6},{3,19},{4,0},{5,21},{6,2},{7,23},{8,12},{9,25},... | collective-permute-start | bytes 786440 | tf_op jit(solution)/shard_map/ppermute | solution.py:46
  89.5 7.4 %collective-permute-start.15 = (bf16[8,128,128]{2,1,0:T(8,128)(2,1)S(1)}, bf16[8,128,128]{2,1,0:T(8,128)(2,1)S(1)}, u32[]{:S(2)}, u32[]{:S(2)}) collective-permute-start(bf16[8,128,128]{2,1,0:T(8,128)(2,1)S(1)} %all_to_all.11), channel_id=1, source_target_pairs={{0,6},{1,25},{2,0},{3,27},{4,2},{5,29},{6,4},{7,31},{8,14},{9,1},{... | collective-permute-start | bytes 786440 | tf_op jit(solution)/shard_map/ppermute | solution.py:46
  93.6 10.9 %collective-permute-start.20 = (bf16[2,8,128,128]{3,2,1,0:T(8,128)(2,1)S(1)}, bf16[2,8,128,128]{3,2,1,0:T(8,128)(2,1)S(1)}, u32[]{:S(2)}, u32[]{:S(2)}) collective-permute-start(bf16[2,8,128,128]{3,2,1,0:T(8,128)(2,1)S(1)} %pad_maximum_fusion.3.refs_0_), channel_id=1, source_target_pairs={{0,8},{1,3},{2,10},{3,5},{4,12},{5,7},{6,14},{7,1},{8,16},{9,11},{... | collective-permute-start | bytes 1572872 | tf_op jit(solution)/shard_map/ppermute | solution.py:46
  97.0 8.4 %collective-permute-start.17 = (bf16[2,8,128,128]{3,2,1,0:T(8,128)(2,1)S(1)}, bf16[2,8,128,128]{3,2,1,0:T(8,128)(2,1)S(1)}, u32[]{:S(2)}, u32[]{:S(2)}) collective-permute-start(bf16[2,8,128,128]{3,2,1,0:T(8,128)(2,1)S(1)} %pad_maximum_fusion.2.refs_1_), channel_id=1, source_target_pairs={{0,24},{1,7},{2,26},{3,1},{4,28},{5,3},{6,30},{7,5},{8,0},{9,15},{... | collective-permute-start | bytes 1572872 | tf_op jit(solution)/shard_map/ppermute | solution.py:46
  98.2 28.7 %collective-permute-start.23 = (bf16[2,8,128,128]{3,2,1,0:T(8,128)(2,1)S(1)}, bf16[2,8,128,128]{3,2,1,0:T(8,128)(2,1)S(1)}, u32[]{:S(2)}, u32[]{:S(2)}) collective-permute-start(bf16[2,8,128,128]{3,2,1,0:T(8,128)(2,1)S(1)} %pad_maximum_fusion.2.refs_1_), channel_id=1, source_target_pairs={{0,8},{1,3},{2,10},{3,5},{4,12},{5,7},{6,14},{7,1},{8,16},{9,11},{... | collective-permute-start | bytes 1572872 | tf_op jit(solution)/shard_map/ppermute | solution.py:46
  98.5 9.2 %collective-permute-start.24 = (bf16[2,128,128]{2,1,0:T(8,128)(2,1)S(1)}, bf16[2,128,128]{2,1,0:T(8,128)(2,1)S(1)}, u32[]{:S(2)}, u32[]{:S(2)}) collective-permute-start(bf16[2,128,128]{2,1,0:T(8,128)(2,1)S(1)} %get-tuple-element.48.blocks_ref), channel_id=1, source_target_pairs={{0,1},{1,0},{2,3},{3,2},{4,5},{5,4},{6,7},{7,6},{8,9},{9,8},{10,11... | collective-permute-start | bytes 196616 | tf_op jit(solution)/shard_map/ppermute | solution.py:50
  103.8 24.4 %collective-permute-start.22 = (bf16[2,8,128,128]{3,2,1,0:T(8,128)(2,1)S(1)}, bf16[2,8,128,128]{3,2,1,0:T(8,128)(2,1)S(1)}, u32[]{:S(2)}, u32[]{:S(2)}) collective-permute-start(bf16[2,8,128,128]{3,2,1,0:T(8,128)(2,1)S(1)} %pad_maximum_fusion.3.refs_0_), channel_id=1, source_target_pairs={{0,24},{1,7},{2,26},{3,1},{4,28},{5,3},{6,30},{7,5},{8,0},{9,15},{... | collective-permute-start | bytes 1572872 | tf_op jit(solution)/shard_map/ppermute | solution.py:46
  104.5 25.1 %collective-permute-start.21 = (bf16[2,8,128,128]{3,2,1,0:T(8,128)(2,1)S(1)}, bf16[2,8,128,128]{3,2,1,0:T(8,128)(2,1)S(1)}, u32[]{:S(2)}, u32[]{:S(2)}) collective-permute-start(bf16[2,8,128,128]{3,2,1,0:T(8,128)(2,1)S(1)} %collective-permute-done.20.refs_0_), channel_id=1, source_target_pairs={{0,8},{1,3},{2,10},{3,5},{4,12},{5,7},{6,14},{7,1},{8,16},{9,11},{... | collective-permute-start | bytes 1572872 | tf_op jit(solution)/shard_map/ppermute | solution.py:46
  105.4 25.3 %collective-permute-start.18 = (bf16[2,8,128,128]{3,2,1,0:T(8,128)(2,1)S(1)}, bf16[2,8,128,128]{3,2,1,0:T(8,128)(2,1)S(1)}, u32[]{:S(2)}, u32[]{:S(2)}) collective-permute-start(bf16[2,8,128,128]{3,2,1,0:T(8,128)(2,1)S(1)} %collective-permute-done.17.refs_1_), channel_id=1, source_target_pairs={{0,24},{1,7},{2,26},{3,1},{4,28},{5,3},{6,30},{7,5},{8,0},{9,15},{... | collective-permute-start | bytes 1572872 | tf_op jit(solution)/shard_map/ppermute | solution.py:46
  107.8 11.4 %collective-permute-start.25 = (bf16[2,2,128,128]{3,2,1,0:T(8,128)(2,1)S(1)}, bf16[2,2,128,128]{3,2,1,0:T(8,128)(2,1)S(1)}, u32[]{:S(2)}, u32[]{:S(2)}) collective-permute-start(bf16[2,2,128,128]{3,2,1,0:T(8,128)(2,1)S(1)} %pad_maximum_fusion.5), channel_id=1, source_target_pairs={{0,2},{1,255},{2,4},{3,1},{4,6},{5,3},{6,8},{7,5},{8,10},{9,7},{10... | collective-permute-start | bytes 393224 | tf_op jit(solution)/shard_map/ppermute | solution.py:54
  119.2 5.4 %collective-permute-start.26 = (bf16[2,2,128,128]{3,2,1,0:T(8,128)(2,1)S(1)}, bf16[2,2,128,128]{3,2,1,0:T(8,128)(2,1)S(1)}, u32[]{:S(2)}, u32[]{:S(2)}) collective-permute-start(bf16[2,2,128,128]{3,2,1,0:T(8,128)(2,1)S(1)} %collective-permute-done.25.fetched_ref), channel_id=1, source_target_pairs={{0,1},{1,0},{2,3},{3,2},{4,5},{5,4},{6,7},{7,6},{8,9},{9,8},{10,11... | collective-permute-start | bytes 393224 | tf_op jit(solution)/shard_map/ppermute | solution.py:50
  (15 other events, 38.8 us)
